TPU v7x, 512 devices: a whole 4x8x8 slice. The times are simulated.
512 devices in a mesh: lon: 32 (over x_hi, z, core), lat: 16 (over y, x_lo).
Axes of the slice: x: 4 (x_hi: 2, x_lo: 2; x = x_hi * 2 + x_lo), y: 8, z: 8, core: 2. Of those that a mesh axis runs over, the one named last changes fastest.
Arguments:
- sample_collection: float32 [17, 6, 128, 4096], P(None, None, 'lat', 'lon'), may hold values from -5.5 to 5.5
- obs_index: int32 [16, 32, 128], P('lat', 'lon'), may hold values from 0 to 1023, as said below
- obs_count: int32 [16, 32], P('lat', 'lon'), may hold values from 42 to 128
- obs_value: float32 [16, 32, 128], P('lat', 'lon'), may hold values from -5 to 5
- obs_weight: float32 [16, 32, 128], P('lat', 'lon'), may hold values from 8 to 128
Outputs:
- analysis: float32 [17, 6, 128, 4096], P(None, None, 'lat', 'lon')
- analysis_spread: float32 [17, 17], replicated
Inputs may be any that keep to these rules, and one draw needn't show every extreme that they name: `obs_index`: cell number within the tile, row-major over its 8 x 128 cells; slots at or past the tile's count are ignored.
All inputs are finite; a program needn't handle non-finite values.
Results may differ from a plain program's by a relative error of at most 0.00021.
Values sent between devices are 32-bit elements; how exact they have to be, the bound alone decides.
No kernel may reach another device: no remote copies, remote signals or barrier semaphores. Data moves between devices by JAX's collectives and lax.ppermute only.
A program may use at most 64 MiB of HBM per device.

v0:
```python
import math

import jax
import jax.numpy as jnp
from jax import lax
from jax.sharding import PartitionSpec as P

UNCERTAINTY_DIRS = 16
MEMBERS = 17
FIELDS = 6
SUBSTEPS = 4


time_step = 0.15
coriolis_scale = 0.5
grav_low = 0.5
depth_top = 4.0
depth_low = 6.0
forget = 0.9
highest = lax.Precision.HIGHEST


def padded_2(shard, sides, width, wrap):
    for axis, dim in sides:
        devices, length = (lax.axis_size(axis), shard.shape[dim])
        up = [(i, (i + 1) % devices) for i in range(devices if wrap else devices - 1)]
        down = [(j, i) for i, j in up]
        last = lax.slice_in_dim(shard, length - width, length, axis=dim)
        leading = lax.slice_in_dim(shard, 0, width, axis=dim)
        before = lax.ppermute(last, axis, up)
        after = lax.ppermute(leading, axis, down)
        shard = jnp.concatenate([before, shard, after], axis=dim)
    return shard


def from_east(quantity):
    return quantity[..., 1:-1, 2:]


def from_west(quantity):
    return quantity[..., 1:-1, :-2]


def from_north(quantity):
    return quantity[..., 2:, 1:-1]


def from_south(quantity):
    return quantity[..., :-2, 1:-1]


def neighbour_mean(quantity):
    return 0.25 * (
        from_east(quantity) + from_west(quantity) + from_north(quantity) + from_south(quantity)
    )


def zonal_slope(quantity):
    return 0.5 * (from_east(quantity) - from_west(quantity))


def merid_slope(quantity):
    return 0.5 * (from_north(quantity) - from_south(quantity))


def layer_update(thick, zonal, merid, pressure, rest_depth, coriolis):
    column = rest_depth + thick
    thick_new = neighbour_mean(thick) - time_step * (
        zonal_slope(column * zonal) + merid_slope(column * merid)
    )
    zonal_here = zonal[..., 1:-1, 1:-1]
    merid_here = merid[..., 1:-1, 1:-1]
    zonal_new = neighbour_mean(zonal) - time_step * (
        zonal_here * zonal_slope(zonal)
        + merid_here * merid_slope(zonal)
        - coriolis * merid_here
        + zonal_slope(pressure)
    )
    merid_new = neighbour_mean(merid) - time_step * (
        zonal_here * zonal_slope(merid)
        + merid_here * merid_slope(merid)
        + coriolis * zonal_here
        + merid_slope(pressure)
    )
    return (thick_new, zonal_new, merid_new)


def advance(padded, coriolis):
    thick_top = padded[..., 0, :, :]
    thick_low = padded[..., 3, :, :]
    press_top = thick_top + thick_low
    press_low = press_top + grav_low * thick_low
    upper_layer = layer_update(
        thick_top, padded[..., 1, :, :], padded[..., 2, :, :], press_top, depth_top, coriolis
    )
    lower_layer = layer_update(
        thick_low, padded[..., 4, :, :], padded[..., 5, :, :], press_low, depth_low, coriolis
    )
    return jnp.stack(upper_layer + lower_layer, axis=-3)


def coriolis_rows(first_row, row_count, total_rows):
    row_values = first_row + jnp.arange(row_count, dtype=jnp.float32)
    return (coriolis_scale * (2.0 * (row_values + 0.5) / total_rows - 1.0)).reshape(row_count, 1)


def margin_steps(padded, rim, first_row, rows_here, total_rows):
    state = padded
    margin = rim - 1
    start = first_row - margin
    count = rows_here + 2 * margin
    state = advance(state, coriolis_rows(start.astype(jnp.float32), count, total_rows))
    return state


def cholesky_lower(matrix):
    order = matrix.shape[0]
    columns = []
    for pivot in range(order):
        partial_col = matrix[:, pivot]
        for earlier in range(pivot):
            partial_col = partial_col - columns[earlier] * columns[earlier][pivot]
        diagonal_root = jnp.sqrt(partial_col[pivot])
        row_mask = (jnp.arange(order) >= pivot).astype(jnp.float32)
        columns.append(partial_col / diagonal_root * row_mask)
    return jnp.stack(columns, axis=1)


def lower_solve(factor, right):
    order = factor.shape[0]
    solved = []
    for row in range(order):
        value = right[row]
        for earlier in range(row):
            value = value - factor[row, earlier] * solved[earlier]
        solved.append(value / factor[row, row])
    return jnp.stack(solved, axis=0)


def upper_solve_transposed(factor, right):
    order = factor.shape[0]
    solved = [None] * order
    for row in range(order - 1, -1, -1):
        value = right[row]
        for later in range(row + 1, order):
            value = value - factor[later, row] * solved[later]
        solved[row] = value / factor[row, row]
    return jnp.stack(solved, axis=0)


def mode_space(obs_gram, obs_proj):
    identity = jnp.eye(UNCERTAINTY_DIRS, dtype=jnp.float32)
    gamma_matrix = identity - 1.0 / MEMBERS
    precision = UNCERTAINTY_DIRS / forget * gamma_matrix + obs_gram
    factor = cholesky_lower(precision)
    weights = upper_solve_transposed(factor, lower_solve(factor, obs_proj))
    projector = (
        jnp.concatenate([identity, jnp.zeros((1, UNCERTAINTY_DIRS), jnp.float32)], axis=0)
        - 1.0 / MEMBERS
    )
    root_fix = identity + (math.sqrt(MEMBERS) - 1.0) / UNCERTAINTY_DIRS
    omega_matrix = jnp.dot(projector, root_fix, precision=highest)
    rotation = math.sqrt(UNCERTAINTY_DIRS) * upper_solve_transposed(factor, omega_matrix.T)
    return (weights, rotation)


def on_device(sample_collection, obs_index, obs_count, obs_value, obs_weight):
    lat_tiles = lax.axis_size("lat")
    lon_tiles = lax.axis_size("lon")
    rows_here = sample_collection.shape[2]
    columns_here = sample_collection.shape[3]
    total_rows = rows_here * lat_tiles
    total_columns = columns_here * lon_tiles
    first_row = lax.axis_index("lat") * rows_here
    members_now = sample_collection
    for substep in range(SUBSTEPS):
        lat_padded = padded_2(members_now, (("lat", 2),), 1, False)
        all_padded = padded_2(lat_padded, (("lon", 3),), 1, True)
        members_now = margin_steps(all_padded, 1, first_row, rows_here, total_rows)
    sample_average_vector = jnp.mean(members_now, axis=0)
    mode_flat = (members_now[:UNCERTAINTY_DIRS] - sample_average_vector).reshape(
        UNCERTAINTY_DIRS, -1
    )
    interface_elevation = (members_now[:, 0] + members_now[:, 3]).reshape(MEMBERS, -1)
    slot_cells = obs_index.reshape(-1)
    slot_total = slot_cells.shape[0]
    cell_numbers = jnp.arange(rows_here * columns_here, dtype=jnp.int32)
    selector = (slot_cells[:, None] == cell_numbers[None, :]).astype(jnp.float32)
    observed = lax.dot_general(
        interface_elevation, selector, (((1,), (1,)), ((), ())), precision=highest
    )
    live_slots = (jnp.arange(slot_total, dtype=jnp.int32) < obs_count.reshape(())).astype(
        jnp.float32
    )
    weight = obs_weight.reshape(-1) * live_slots / (slot_total * lat_tiles * lon_tiles)
    obs_mean = jnp.mean(observed, axis=0)
    anomaly = observed[:UNCERTAINTY_DIRS] - obs_mean
    innovation = obs_value.reshape(-1) - obs_mean
    weighted = anomaly * weight
    gram_local = jnp.dot(weighted, anomaly.T, precision=highest)
    proj_local = jnp.dot(weighted, innovation, precision=highest)
    cell_total = FIELDS * total_rows * total_columns
    obs_gram, obs_proj = lax.psum((gram_local, proj_local), ("lon", "lat"))
    weights, rotation = mode_space(obs_gram, obs_proj)
    deviation = jnp.dot(rotation.T, mode_flat, precision=highest)
    spread = (
        lax.psum(jnp.dot(deviation, deviation.T, precision=highest), ("lon", "lat")) / cell_total
    )
    coefficient = weights[:, None] + rotation
    update = jnp.dot(coefficient.T, mode_flat, precision=highest).reshape(members_now.shape)
    analysis = sample_average_vector + update
    return (analysis, spread)


def solution(mesh):
    return jax.shard_map(
        on_device,
        mesh=mesh,
        in_specs=(
            P(None, None, "lat", "lon"),
            P("lat", "lon", None),
            P("lat", "lon"),
            P("lat", "lon", None),
            P("lat", "lon", None),
        ),
        out_specs=(P(None, None, "lat", "lon"), P()),
        check_vma=False,
    )
```

profile of v0, /device:TPU:1, one launch (start us, length us, event | category | flops | bytes accessed | tf_op | source)
XLA Modules:
  0.0 741.2 jit_solution(4579184215715674192)
XLA Ops:
  0.6 1.3 fusion.263
  1.9 3.9 collective-permute-start
  5.9 1.3 collective-permute-start.1
  7.3 1.1 constant_dynamic-update-slice_fusion.1
  8.4 2.6 collective-permute-done.1
  11.8 6.0 collective-permute-start.2
  18.4 3.2 collective-permute-start.3
  22.1 1.6 collective-permute-done.3
  26.6 4.1 collective-permute-start.4
  30.7 1.3 collective-permute-start.5
  32.1 3.7 collective-permute-done.5
  36.5 3.3 collective-permute-start.6
  40.3 7.1 collective-permute-start.7
  51.2 3.5 collective-permute-start.8
  54.7 1.3 collective-permute-start.9
  56.1 3.7 collective-permute-done.9
  60.6 1.9 collective-permute-start.10
  63.0 9.4 %collective-permute-start.11 = (f32[17,6,10,1]{0,3,2,1:T(1,128)S(1)}, f32[17,6,10,1]{0,3,2,1:T(1,128)S(1)}, u32[]{:S(2)}, u32[]{:S(2)}) collective-permute-start(f32[17,6,10,1]{0,3,2,1:T(1,128)S(1)} %copy.66), channel_id=1, source_target_pairs={{16,0},{32,16},{48,32},{64,48},{80,64},{96,80},{112,96},{128,112},... | collective-permute-start | bytes 12248 | tf_op jit(solution)/shard_map/ppermute | solution.py:31
  76.1 3.7 collective-permute-start.12
  79.7 1.3 collective-permute-start.13
  81.1 3.7 collective-permute-done.13
  85.6 1.9 collective-permute-start.14
  88.0 9.6 %collective-permute-start.15 = (f32[17,6,10,1]{0,3,2,1:T(1,128)S(1)}, f32[17,6,10,1]{0,3,2,1:T(1,128)S(1)}, u32[]{:S(2)}, u32[]{:S(2)}) collective-permute-start(f32[17,6,10,1]{0,3,2,1:T(1,128)S(1)} %copy.70), channel_id=1, source_target_pairs={{16,0},{32,16},{48,32},{64,48},{80,64},{96,80},{112,96},{128,112},... | collective-permute-start | bytes 12248 | tf_op jit(solution)/shard_map/ppermute | solution.py:31
  101.5 107.8 %psum.22 = f32[16,16]{1,0:T(8,128)S(1)} all-reduce(f32[16,16]{1,0:T(8,128)S(1)} %fusion.149), channel_id=1, replica_groups=mesh['lon'=32,'lat'=16] {'lon','lat'}, use_global_device_ids=true, to_apply=%region_3.0 | all-reduce | flops 256 | bytes 2048 | tf_op jit(solution)/shard_map/psum | solution.py:203
  211.2 4.0 fusion.161
  216.5 0.7 fusion.266
  219.1 0.7 fusion.279
  219.8 1.3 multiply_subtract_fusion.12
  223.2 1.9 multiply_subtract_fusion.11
  227.1 2.4 multiply_subtract_fusion.10
  231.4 3.1 multiply_subtract_fusion.9
  236.5 5.9 fusion.152
  242.4 3.7 multiply_subtract_fusion.8
  248.1 4.3 multiply_subtract_fusion.7
  254.4 4.9 multiply_subtract_fusion.6
  261.2 5.6 multiply_subtract_fusion.5
  268.8 6.2 multiply_subtract_fusion.4
  277.1 7.1 multiply_subtract_fusion.3
  286.0 7.5 %multiply_subtract_fusion.2 = f32[16]{0:T(128)S(1)} fusion(f32[16]{0:T(128)S(1)} %get-tuple-element.14, f32[]{:T(128)} %bitcast.171, f32[]{:T(128)} %bitcast.184, f32[]{:T(128)} %bitcast.183, f32[]{:T(128)} %bitcast.182, f32[]{:T(128)} %bitcast.181, f32[]{:T(128)} %bitcast.180, f32[]{:T(128)} %bitcast.179, f32[]{:T(128)} %bitcast.178, f32[]{:T(128)} %bitcast.177, ...), kind=kLoop, calls=%fused_computation.457 | loop fusion | flops 944 | bytes 988 | tf_op jit(solution)/shard_map/sub | solution.py:122
  295.5 8.1 %multiply_subtract_fusion.1 = f32[16]{0:T(128)S(1)} fusion(f32[16]{0:T(128)S(1)} %get-tuple-element.13, f32[]{:T(128)} %bitcast.187, f32[]{:T(128)} %bitcast.201, f32[]{:T(128)} %bitcast.200, f32[]{:T(128)} %bitcast.199, f32[]{:T(128)} %bitcast.198, f32[]{:T(128)} %bitcast.197, f32[]{:T(128)} %bitcast.196, f32[]{:T(128)} %bitcast.195, f32[]{:T(128)} %bitcast.194, ...), kind=kLoop, calls=%fused_computation.456 | loop fusion | flops 1024 | bytes 1060 | tf_op jit(solution)/shard_map/sub | solution.py:122
  305.4 8.9 %multiply_subtract_fusion = f32[16]{0:T(128)S(1)} fusion(f32[16]{0:T(128)S(1)} %get-tuple-element.12, f32[]{:T(128)} %bitcast.204, f32[]{:T(128)} %bitcast.219, f32[]{:T(128)} %bitcast.218, f32[]{:T(128)} %bitcast.217, f32[]{:T(128)} %bitcast.216, f32[]{:T(128)} %bitcast.215, f32[]{:T(128)} %bitcast.214, f32[]{:T(128)} %bitcast.213, f32[]{:T(128)} %bitcast.212, ...), kind=kLoop, calls=%fused_computation.455 | loop fusion | flops 1104 | bytes 1132 | tf_op jit(solution)/shard_map/sub | solution.py:122
  317.5 65.5 %subtract_divide_fusion = (f32[1,17]{1,0:T(1,128)S(1)}, f32[1,17]{1,0:T(1,128)S(1)}, f32[1,17]{1,0:T(1,128)S(1)}, f32[1,17]{1,0:T(1,128)S(1)}, f32[1,17]{1,0:T(1...) fusion(f32[16,17]{1,0:T(8,128)S(1)} %fusion.146, ...), kind=kLoop, calls=%fused_computation.445 | loop fusion | flops 3332 | bytes 2392 | tf_op jit(solution)/shard_map/div | solution.py:147
  383.0 58.1 %fusion.195 = (f32[17]{0:T(128)S(1)}, f32[17]{0:T(128)S(1)}, f32[17]{0:T(128)S(1)}, f32[17]{0:T(128)S(1)}, f32[17]{0:T(128)S(1)}, /*index=5*/f32[17]{0:T(128)S(1...) fusion(f32[16,17]{1,0:T(8,128)S(1)} %fusion.146, f32[1,17]{1,0:T(1,128)S(1)} %get-tuple-element.39, ...), kind=kLoop, calls=%fused_computation.366 | loop fusion | flops 2992 | bytes 2004 | tf_op jit(solution)/shard_map/div | solution.py:147
  441.1 19.3 %fusion.229 = (f32[1,17]{1,0:T(1,128)S(1)}, f32[17]{0:T(128)S(1)}) fusion(f32[1,17]{1,0:T(1,128)S(1)} %get-tuple-element.42, f32[1,17]{1,0:T(1,128)S(1)} %get-tuple-element.41, f32[1,17]{1,0:T(1,128)S(1)} %get-tuple-element.40, f32[1,17]{1,0:T(1,128)S(1)} %get-tuple-element.39, f32[17]{0:T(128)S(1)} %get-tuple-element.54, f32[17]{0:T(128)S(1)} %get-tuple-element.53, ...), kind=kLoop, calls=%fused_computation.472 | loop fusion | flops 1020 | bytes 1348 | tf_op jit(solution)/shard_map/stack | solution.py:148
  461.2 0.7 fusion.281
  462.1 94.7 %all-reduce.1 = (f32[16]{0:T(128)S(1)}, f32[17,17]{1,0:T(8,128)S(1)}) all-reduce(f32[16]{0:T(128)S(1)} %convolution_bitcast_fusion, f32[17,17]{1,0:T(8,128)S(1)} %fusion.281), channel_id=1, replica_groups=mesh['lon'=32,'lat'=16] {'lon','lat'}, use_global_device_ids=true, to_apply=%region_2.0 | all-reduce | flops 305 | bytes 2440 | tf_op jit(solution)/shard_map/psum | solution.py:203
  739.0 0.8 convolution_add_fusion
  739.8 0.8 copy.76
  (154 shorter events, 42.6 us)
Async XLA Ops:
  1.9 5.3 collective-permute-start
  5.9 5.1 collective-permute-start.1
  11.8 9.8 %collective-permute-start.2 = (f32[17,6,10,1]{0,1,3,2:T(8,128)S(1)}, f32[17,6,10,1]{0,1,3,2:T(8,128)S(1)}, u32[]{:S(2)}, u32[]{:S(2)}) collective-permute-start(f32[17,6,10,1]{0,1,3,2:T(8,128)S(1)} %copy.57), channel_id=1, source_target_pairs={{0,16},{16,32},{32,48},{48,64},{64,80},{80,96},{96,112},{112,128},... | collective-permute-start | bytes 12248 | tf_op jit(solution)/shard_map/ppermute | solution.py:30
  18.4 5.3 collective-permute-start.3
  26.6 5.5 collective-permute-start.4
  30.7 5.1 collective-permute-start.5
  36.5 10.9 %collective-permute-start.6 = (f32[17,6,10,1]{0,3,2,1:T(1,128)S(1)}, f32[17,6,10,1]{0,3,2,1:T(1,128)S(1)}, u32[]{:S(2)}, u32[]{:S(2)}) collective-permute-start(f32[17,6,10,1]{0,3,2,1:T(1,128)S(1)} %copy.61), channel_id=1, source_target_pairs={{0,16},{16,32},{32,48},{48,64},{64,80},{80,96},{96,112},{112,128},... | collective-permute-start | bytes 12248 | tf_op jit(solution)/shard_map/ppermute | solution.py:30
  40.3 7.9 %collective-permute-start.7 = (f32[17,6,10,1]{0,3,2,1:T(1,128)S(1)}, f32[17,6,10,1]{0,3,2,1:T(1,128)S(1)}, u32[]{:S(2)}, u32[]{:S(2)}) collective-permute-start(f32[17,6,10,1]{0,3,2,1:T(1,128)S(1)} %copy.62), channel_id=1, source_target_pairs={{16,0},{32,16},{48,32},{64,48},{80,64},{96,80},{112,96},{128,112},... | collective-permute-start | bytes 12248 | tf_op jit(solution)/shard_map/ppermute | solution.py:31
  51.2 4.9 collective-permute-start.8
  54.7 5.1 collective-permute-start.9
  60.6 11.8 %collective-permute-start.10 = (f32[17,6,10,1]{0,3,2,1:T(1,128)S(1)}, f32[17,6,10,1]{0,3,2,1:T(1,128)S(1)}, u32[]{:S(2)}, u32[]{:S(2)}) collective-permute-start(f32[17,6,10,1]{0,3,2,1:T(1,128)S(1)} %copy.65), channel_id=1, source_target_pairs={{0,16},{16,32},{32,48},{48,64},{64,80},{80,96},{96,112},{112,128},... | collective-permute-start | bytes 12248 | tf_op jit(solution)/shard_map/ppermute | solution.py:30
  63.0 10.2 %collective-permute-start.11 = (f32[17,6,10,1]{0,3,2,1:T(1,128)S(1)}, f32[17,6,10,1]{0,3,2,1:T(1,128)S(1)}, u32[]{:S(2)}, u32[]{:S(2)}) collective-permute-start(f32[17,6,10,1]{0,3,2,1:T(1,128)S(1)} %copy.66), channel_id=1, source_target_pairs={{16,0},{32,16},{48,32},{64,48},{80,64},{96,80},{112,96},{128,112},... | collective-permute-start | bytes 12248 | tf_op jit(solution)/shard_map/ppermute | solution.py:31
  76.1 5.1 collective-permute-start.12
  79.7 5.1 collective-permute-start.13
  85.6 12.8 %collective-permute-start.14 = (f32[17,6,10,1]{0,3,2,1:T(1,128)S(1)}, f32[17,6,10,1]{0,3,2,1:T(1,128)S(1)}, u32[]{:S(2)}, u32[]{:S(2)}) collective-permute-start(f32[17,6,10,1]{0,3,2,1:T(1,128)S(1)} %copy.69), channel_id=1, source_target_pairs={{0,16},{16,32},{32,48},{48,64},{64,80},{80,96},{96,112},{112,128},... | collective-permute-start | bytes 12248 | tf_op jit(solution)/shard_map/ppermute | solution.py:30
  88.0 10.9 %collective-permute-start.15 = (f32[17,6,10,1]{0,3,2,1:T(1,128)S(1)}, f32[17,6,10,1]{0,3,2,1:T(1,128)S(1)}, u32[]{:S(2)}, u32[]{:S(2)}) collective-permute-start(f32[17,6,10,1]{0,3,2,1:T(1,128)S(1)} %copy.70), channel_id=1, source_target_pairs={{16,0},{32,16},{48,32},{64,48},{80,64},{96,80},{112,96},{128,112},... | collective-permute-start | bytes 12248 | tf_op jit(solution)/shard_map/ppermute | solution.py:31
  100.3 0.7 copy-start.1
  100.3 1.1 copy-start
  317.3 144.6 %copy-start.2 = (f32[1,1,128]{2,1,0:T(1,128)S(1)}, f32[1,1,128]{2,1,0:T(1,128)}, u32[]{:S(2)}) copy-start(f32[1,1,128]{2,1,0:T(1,128)} %param.8) | copy-start | bytes 1540
where the time goes:
time: 748 us; the launch traced here: 741 us
  other arithmetic  228 us (30%)
  blocking collectives  202 us (27%)
  between operations  194 us (26%)
  starting transfers between devices  62.8 us (8%)
  local copies, waits for them, and re-layouts  34.3 us (5%)
  waiting for transfers between devices  16.3 us (2%)
    psum x2, blocking collectives, on_device(): obs_gram, obs_proj = lax.psum((gram_local, proj_local), ('lon', 'lat'))  202 us
    div x2, other arithmetic, upper_solve_transposed(): solved[row] = value / factor[row, row]  124 us
    sub x16, other arithmetic, cholesky_lower(): partial_col = partial_col - columns[earlier] * columns[earlier][pivot]  75.4 us
    ppermute x8, starting transfers between devices, padded_2(): after = lax.ppermute(leading, axis, down)  34.4 us
    ppermute x8, starting transfers between devices, padded_2(): before = lax.ppermute(last, axis, up)  28.3 us
    another operation x1, other arithmetic, upper_solve_transposed(): return jnp.stack(solved, axis=0)  19.3 us
    ppermute x8, waiting for transfers between devices, padded_2(): after = lax.ppermute(leading, axis, down)  16 us
  transfers between devices with their start and end apart: 16, of which 11 were waited for; matrix products, arithmetic and copies ran while one was open for 1% of the time, Pallas kernels for 0%

commit v1 on v0

v1 whole, which is shorter than its diff:
```python
import math

import jax
import jax.numpy as jnp
from jax import lax
from jax.experimental import pallas as pl
from jax.experimental.pallas import tpu as pltpu
from jax.sharding import PartitionSpec as P


DIRS = 16
MEMBERS = 17
FIELDS = 6
PAIRS = MEMBERS * FIELDS
SUBSTEPS = 4
RIM = 4
ROWS = 8
COLS = 128
CELLS = FIELDS * ROWS * COLS
STRIPS = FIELDS + 1

time_step = 0.15
depth_top = 4.0
depth_low = 6.0
forget = 0.9
highest = lax.Precision.HIGHEST
f32 = jnp.float32


def iota(shape, axis):
    return lax.broadcasted_iota(jnp.int32, shape, axis)


def vmem(count):
    return [pl.BlockSpec(memory_space=pltpu.VMEM)] * count


def pack_kernel(x_ref, north_ref, south_ref, strip_ref):
    lane = iota((ROWS, COLS), 1)
    for pair in range(PAIRS):
        block = x_ref[pair]
        north_ref[RIM * pair : RIM * (pair + 1), :] = block[RIM:, :]
        south_ref[RIM * pair : RIM * (pair + 1), :] = block[:RIM, :]
    for strip in range(STRIPS):
        total = jnp.zeros((ROWS, COLS), f32)
        for place in range(DIRS if strip < FIELDS else FIELDS):
            pair = place * FIELDS + strip if strip < FIELDS else DIRS * FIELDS + place
            moved = pltpu.roll(x_ref[pair], 8 * place, 1) if place else x_ref[pair]
            mask = ((lane - (8 * place - 4)) & (COLS - 1)) < 8
            total = jnp.where(mask, moved, total)
        strip_ref[strip] = total


def layer(thick, zonal, merid, slope_x, slope_y, depth, turn):
    (h, hE, hW, hN, hS), (u, uE, uW, uN, uS), (v, vE, vW, vN, vS) = thick, zonal, merid
    half = 0.5 * time_step
    flux = ((depth + hE) * uE - (depth + hW) * uW) + ((depth + hN) * vN - (depth + hS) * vS)
    h_new = 0.25 * ((hE + hW) + (hN + hS)) - half * flux
    u_new = 0.25 * ((uE + uW) + (uN + uS)) - (
        half * (u * (uE - uW) + v * (uN - uS) + slope_x) - turn * v
    )
    v_new = 0.25 * ((vE + vW) + (vN + vS)) - (
        half * (u * (vE - vW) + v * (vN - vS) + slope_y) + turn * u
    )
    return h_new, u_new, v_new


def advance(center, east, west, turn):
    stencil = []
    for c, e, w in zip(center, east, west):
        stencil.append((c, e, w, pltpu.roll(c, 15, 0), pltpu.roll(c, 1, 0)))
    top, low = stencil[0], stencil[3]
    top_x, top_y = top[1] - top[2], top[3] - top[4]
    low_x, low_y = low[1] - low[2], low[3] - low[4]
    sum_x, sum_y = top_x + low_x, top_y + low_y
    upper = layer(top, stencil[1], stencil[2], sum_x, sum_y, depth_top, turn)
    lower = layer(low, stencil[4], stencil[5], sum_x + 0.5 * low_x, sum_y + 0.5 * low_y, depth_low, turn)
    return upper + lower


def forecast_kernel(
    lat_ref, count_ref, x_ref, nm_ref, sm_ref, own_ref, cn_ref, cs_ref, index_ref, value_ref, weight_ref,
    modes_ref, pay_ref, state, strips, inner, dev, seen,
):
    lat = lat_ref[0, 0]
    lats = lat_ref[0, 1]
    tiles = lat_ref[0, 2]
    sub = iota((16, COLS), 0)
    lane = iota((16, COLS), 1)
    row = jnp.where(sub < 12, sub, sub - 16) + lat * ROWS
    inside = (row >= 0) & (row < lats * ROWS)
    turn = time_step * (0.5 * (2.0 * (row.astype(f32) + 0.5) / (lats * ROWS).astype(f32) - 1.0))
    sub8 = iota((ROWS, COLS), 0)

    for pair in range(PAIRS):
        state[0, pair, 0:8, :] = x_ref[pair]
        state[0, pair, 8:12, :] = nm_ref[RIM * pair : RIM * (pair + 1), :]
        state[0, pair, 12:16, :] = sm_ref[RIM * pair : RIM * (pair + 1), :]
    for strip in range(STRIPS):
        rim = jnp.where(sub8 < RIM, cn_ref[strip], cs_ref[strip])
        block = jnp.concatenate([own_ref[strip], rim], axis=0)
        if strip < FIELDS:
            strips[0, 0, strip] = block
        else:
            for field in range(FIELDS):
                strips[0, 1, field] = pltpu.roll(block, COLS - 8 * field, 1) if field else block

    for step in range(SUBSTEPS):
        now, later = step % 2, (step + 1) % 2

        def member_step(member, carry, now=now, later=later):
            which = member // DIRS
            place = member - which * DIRS
            shift = place * 8
            back = lax.rem(COLS - shift, COLS)
            edge = ((lane - shift + 1) & (COLS - 1)) < 2
            center, east, west = [], [], []
            for field in range(FIELDS):
                block = state[now, member * FIELDS + field]
                beyond = pltpu.roll(strips[now, which, field], back, 1)
                center.append(block)
                east.append(pltpu.roll(jnp.where(lane == 0, beyond, block), COLS - 1, 1))
                west.append(pltpu.roll(jnp.where(lane == COLS - 1, beyond, block), 1, 1))
                inner[which, field] = jnp.where(edge, pltpu.roll(block, shift, 1), inner[which, field])
            new = advance(center, east, west, turn)
            for field in range(FIELDS):
                state[later, member * FIELDS + field] = jnp.where(inside, new[field], 0.0)
            return carry

        lax.fori_loop(0, MEMBERS, member_step, 0)
        if step < SUBSTEPS - 1:
            for which in range(2):
                center, east, west = [], [], []
                for field in range(FIELDS):
                    block, beyond = strips[now, which, field], inner[which, field]
                    center.append(block)
                    east.append(pltpu.roll(jnp.where((lane & 7) == 0, beyond, block), COLS - 1, 1))
                    west.append(pltpu.roll(jnp.where((lane & 7) == 7, beyond, block), 1, 1))
                new = advance(center, east, west, turn)
                for field in range(FIELDS):
                    strips[later, which, field] = jnp.where(inside, new[field], 0.0)

    last = SUBSTEPS % 2
    cell = index_ref[...]
    column = jnp.broadcast_to(cell & (COLS - 1), (ROWS, COLS))
    at_row = jnp.broadcast_to(lax.shift_right_logical(cell, 7), (ROWS, COLS)) == sub8
    for member in range(MEMBERS):
        surface = state[last, member * FIELDS, 0:8, :] + state[last, member * FIELDS + 3, 0:8, :]
        picked = jnp.take_along_axis(surface, column, axis=1)
        seen[member : member + 1, :] = jnp.sum(jnp.where(at_row, picked, 0.0), axis=0, keepdims=True)

    for field in range(FIELDS):
        total = state[last, field, 0:8, :]
        for member in range(1, MEMBERS):
            total = total + state[last, member * FIELDS + field, 0:8, :]
        mean = total * (1.0 / MEMBERS)
        for member in range(DIRS):
            at = (member * FIELDS + field) * ROWS
            dev[at : at + ROWS, :] = state[last, member * FIELDS + field, 0:8, :] - mean
        at = (DIRS * FIELDS + field) * ROWS
        dev[at : at + ROWS, :] = mean
    for tile in range(FIELDS * ROWS):
        modes_ref[:, COLS * tile : COLS * (tile + 1)] = dev[pl.ds(tile, MEMBERS, stride=FIELDS * ROWS), :]

    modes = modes_ref[0:DIRS, :]
    mode_gram = lax.dot_general(modes, modes, (((1,), (1,)), ((), ())), precision=highest, preferred_element_type=f32)

    observed = seen[...]
    slot = iota((1, COLS), 1)
    live = (slot < count_ref[0, 0]).astype(f32)
    weight = weight_ref[...] * live / (COLS * tiles).astype(f32)
    obs_mean = jnp.sum(observed, axis=0, keepdims=True) * (1.0 / MEMBERS)
    anomaly = observed[0:DIRS, :] - obs_mean
    innovation = value_ref[...] - obs_mean
    weighted = anomaly * weight
    obs_gram = lax.dot_general(
        weighted, anomaly, (((1,), (1,)), ((), ())), precision=highest, preferred_element_type=f32
    )
    obs_proj = jnp.sum(weighted * innovation, axis=1, keepdims=True)
    pay_ref[...] = jnp.zeros((ROWS, COLS), f32)
    for half in range(2):
        rows, at = slice(8 * half, 8 * half + 8), 64 * half
        pay_ref[:, at : at + DIRS] = mode_gram[rows, :]
        pay_ref[:, at + DIRS : at + 2 * DIRS] = obs_gram[rows, :]
        pay_ref[:, at + 2 * DIRS : at + 2 * DIRS + 1] = obs_proj[rows, :]


def analysis_kernel(omega_ref, parts_ref, modes_ref, out_ref, spread_ref, cells):
    total = jnp.sum(parts_ref[...], axis=0)
    joined = jnp.concatenate([total[:, 0:64], total[:, 64:128]], axis=0)
    mode_gram = joined[:, 0:DIRS]
    sub = iota((DIRS, COLS), 0)
    lane = iota((DIRS, COLS), 1)
    work = jnp.concatenate([joined[:, DIRS:], jnp.zeros((DIRS, COLS - 48), f32)], axis=1)
    work = jnp.where(lane < DIRS + 1, work, 0.0)
    gamma = jnp.where(sub == lane, 1.0, 0.0) - 1.0 / MEMBERS
    work = work + jnp.where(lane < DIRS, (DIRS / forget) * gamma, 0.0)
    work = work + jnp.where(lane == sub + 2 * DIRS, 1.0, 0.0)
    for pivot in range(DIRS):
        column = jnp.broadcast_to(work[:, pivot : pivot + 1], (DIRS, COLS))
        inverse = 1.0 / jnp.sqrt(column[pivot : pivot + 1, :])
        row = work[pivot : pivot + 1, :] * inverse
        work = jnp.where(sub == pivot, row, work - jnp.where(sub > pivot, column * inverse, 0.0) * row)
    inverse_factor = work[:, 2 * DIRS : 3 * DIRS]
    solved = work[:, DIRS : DIRS + 1]
    weights = jnp.sum(solved * inverse_factor, axis=0, keepdims=True)
    rotation_t = jnp.dot(omega_ref[...], inverse_factor, precision=highest, preferred_element_type=f32)
    coefficient_t = rotation_t + weights
    for field in range(FIELDS):
        span = slice(field * ROWS * COLS, (field + 1) * ROWS * COLS)
        update = jnp.dot(coefficient_t, modes_ref[0:DIRS, span], precision=highest, preferred_element_type=f32)
        update = update + modes_ref[DIRS : DIRS + 1, span]
        for row_here in range(ROWS):
            cells[pl.ds(field * ROWS + row_here, MEMBERS, stride=FIELDS * ROWS), :] = update[
                :, COLS * row_here : COLS * (row_here + 1)
            ]
    out_ref[...] = cells[...].reshape(PAIRS, ROWS, COLS)
    half_way = jnp.dot(rotation_t, mode_gram, precision=highest, preferred_element_type=f32)
    spread_ref[...] = lax.dot_general(
        half_way, rotation_t, (((1,), (1,)), ((), ())), precision=highest, preferred_element_type=f32
    )


def omega():
    projector = [[(1.0 if i == j else 0.0) - 1.0 / MEMBERS for j in range(DIRS)] for i in range(MEMBERS)]
    root = (math.sqrt(MEMBERS) - 1.0) / DIRS
    rows = [[math.sqrt(DIRS) * (r[j] + root * sum(r)) for j in range(DIRS)] for r in projector]
    return jnp.array(rows, f32)


def sum_over(axis, part):
    count = lax.axis_size(axis)
    return lax.all_to_all(jnp.broadcast_to(part[None], (count,) + part.shape), axis, 0, 0)


def on_device(sample_collection, obs_index, obs_count, obs_value, obs_weight):
    lat_tiles, lon_tiles = lax.axis_size("lat"), lax.axis_size("lon")
    small = pltpu.CompilerParams(vmem_limit_bytes=12 * 2**20)
    blocks = sample_collection.reshape(PAIRS, ROWS, COLS)
    north_msg, south_msg, strip_msg = pl.pallas_call(
        pack_kernel,
        out_shape=[jax.ShapeDtypeStruct((PAIRS * RIM, COLS), f32)] * 2
        + [jax.ShapeDtypeStruct((STRIPS, ROWS, COLS), f32)],
        in_specs=vmem(1),
        out_specs=vmem(3),
        compiler_params=small,
    )(blocks)
    to_north = [(i, i + 1) for i in range(lat_tiles - 1)]
    to_south = [(j, i) for i, j in to_north]
    to_east = [(i, (i + 1) % lon_tiles) for i in range(lon_tiles)]
    to_west = [(j, i) for i, j in to_east]
    south_rows = lax.ppermute(north_msg, "lat", to_north)
    north_rows = lax.ppermute(south_msg, "lat", to_south)
    west_strip = lax.ppermute(strip_msg, "lon", to_east)
    east_strip = lax.ppermute(strip_msg, "lon", to_west)
    eastern = (iota(strip_msg.shape, 2) & 7) < RIM
    own_strip = jnp.where(eastern, east_strip, west_strip)
    south_strip = lax.ppermute(own_strip, "lat", to_north)
    north_strip = lax.ppermute(own_strip, "lat", to_south)

    scalars = jnp.stack([lax.axis_index("lat"), jnp.int32(lat_tiles), jnp.int32(lat_tiles * lon_tiles)]).reshape(1, 3)
    smem = pl.BlockSpec(memory_space=pltpu.SMEM)
    modes, part = pl.pallas_call(
        forecast_kernel,
        out_shape=[jax.ShapeDtypeStruct((MEMBERS, CELLS), f32), jax.ShapeDtypeStruct((ROWS, COLS), f32)],
        in_specs=[smem, smem] + vmem(9),
        out_specs=vmem(2),
        compiler_params=small,
        scratch_shapes=[
            pltpu.VMEM((2, PAIRS, 16, COLS), f32),
            pltpu.VMEM((2, 2, FIELDS, 16, COLS), f32),
            pltpu.VMEM((2, FIELDS, 16, COLS), f32),
            pltpu.VMEM((PAIRS * ROWS, COLS), f32),
            pltpu.VMEM((MEMBERS, COLS), f32),
        ],
    )(
        scalars, obs_count, blocks, north_rows, south_rows, own_strip, north_strip, south_strip,
        obs_index.reshape(1, COLS), obs_value.reshape(1, COLS), obs_weight.reshape(1, COLS),
    )
    part = jnp.sum(sum_over("lat", part), axis=0)
    parts = sum_over("lon", part)
    analysis, spread = pl.pallas_call(
        analysis_kernel,
        out_shape=[jax.ShapeDtypeStruct((PAIRS, ROWS, COLS), f32), jax.ShapeDtypeStruct((MEMBERS, MEMBERS), f32)],
        in_specs=vmem(3),
        out_specs=vmem(2),
        compiler_params=small,
        scratch_shapes=[pltpu.VMEM((PAIRS * ROWS, COLS), f32)],
    )(omega(), parts, modes)
    return analysis.reshape(sample_collection.shape), spread / (CELLS * lat_tiles * lon_tiles)


def solution(mesh):
    return jax.shard_map(
        on_device,
        mesh=mesh,
        in_specs=(
            P(None, None, "lat", "lon"),
            P("lat", "lon", None),
            P("lat", "lon"),
            P("lat", "lon", None),
            P("lat", "lon", None),
        ),
        out_specs=(P(None, None, "lat", "lon"), P()),
        check_vma=False,
    )
```

time: 748 us -> 85.5 us (0.11)
  other arithmetic: 228 us -> 0.71 us
  between operations: 194 us -> 1.44 us
  blocking collectives: 202 us -> 41.5 us
  starting transfers between devices: 62.8 us -> 19.2 us
  local copies, waits for them, and re-layouts: 34.3 us -> 1.74 us
  Pallas kernels: 0 us -> 17.3 us
  waiting for transfers between devices: 16.3 us -> 3.18 us
    psum x2 -> x0, blocking collectives: 202 us -> none  [on_device(): obs_gram, obs_proj = lax.psum((gram_local, proj_local), ('lon', 'lat'))]
    div x7 -> x1, other arithmetic: 124 us -> 0.6 us  [on_device(): spread / (CELLS * lat_tiles * lon_tiles)]
    sub x17 -> x0, other arithmetic: 75.4 us -> none  [the longest x16 75.4 us: cholesky_lower(): partial_col = partial_col - columns[earlier] * columns[earlier][pivot]]
    ppermute x16 -> x6, starting transfers between devices: 62.8 us -> 19.2 us  [the longest x1 5.38 us: on_device(): west_strip = lax.ppermute(strip_msg, 'lon', to_east)]
    all_to_all x0 -> x2, blocking collectives: none -> 41.5 us  [sum_over(): lax.all_to_all(jnp.broadcast_to(part[None], (count,) + part.shape), axis,...]
    slice x49 -> x0, local copies, waits for them, and re-layouts: 27.3 us -> none  [the longest x16 9.55 us: cholesky_lower(): diagonal_root = jnp.sqrt(partial_col[pivot])]
    another operation x5 -> x0, other arithmetic: 20.4 us -> none  [the longest x1 19.3 us: upper_solve_transposed(): return jnp.stack(solved, axis=0)]
    pallas_call x0 -> x3, Pallas kernels: none -> 17.3 us  [the longest x1 13.9 us: on_device(): pl.pallas_call(forecast_kernel, out_shape=[jax.ShapeDtypeStruct((MEMBERS,...]
  transfers between devices with their start and end apart: 16 -> 6, of which waited for: 11 -> 1; matrix products, arithmetic and copies ran while one was open for 1% -> 0% of each run, Pallas kernels for 0% -> 0%
where the time goes in v1:
time: 85.5 us; the launch traced here: 85 us
  blocking collectives  41.5 us (49%)
  starting transfers between devices  19.2 us (22%)
  Pallas kernels  17.3 us (20%)
  waiting for transfers between devices  3.18 us (4%)
  local copies, waits for them, and re-layouts  1.74 us (2%)
  between operations  1.44 us (2%)
    all_to_all x2, blocking collectives, sum_over(): lax.all_to_all(jnp.broadcast_to(part[None], (count,) + part.shape), axis,...  41.5 us
    pallas_call x1, Pallas kernels, on_device(): pl.pallas_call(forecast_kernel, out_shape=[jax.ShapeDtypeStruct((MEMBERS,...  13.9 us
    ppermute x1, starting transfers between devices, on_device(): west_strip = lax.ppermute(strip_msg, 'lon', to_east)  5.38 us
    ppermute x1, starting transfers between devices, on_device(): east_strip = lax.ppermute(strip_msg, 'lon', to_west)  5.29 us
    ppermute x1, starting transfers between devices, on_device(): south_rows = lax.ppermute(north_msg, 'lat', to_north)  4 us
    pallas_call x1, Pallas kernels, on_device(): pl.pallas_call(analysis_kernel, out_shape=[jax.ShapeDtypeStruct((PAIRS, R...  3.27 us
    ppermute x1, waiting for transfers between devices, on_device(): north_strip = lax.ppermute(own_strip, 'lat', to_south)  3.17 us
    ppermute x1, starting transfers between devices, on_device(): south_strip = lax.ppermute(own_strip, 'lat', to_north)  1.91 us
  transfers between devices with their start and end apart: 6, of which 1 were waited for; matrix products, arithmetic and copies ran while one was open for 0% of the time, Pallas kernels for 0%

profile of v1, /device:TPU:1, one launch (start us, length us, event | category | flops | bytes accessed | tf_op | source)
XLA Modules:
  0.0 85.0 jit_solution(16124034809006030031)
XLA Ops:
  0.6 0.0 copy-start
  0.6 1.0 %copy-done = f32[17,6,8,128]{3,2,1,0:T(8,128)S(1)} copy-done((f32[17,6,8,128]{3,2,1,0:T(8,128)S(1)}, f32[17,6,8,128]{3,2,1,0:T(8,128)}, u32[]{:S(2)}) %copy-start) | copy-done | bytes 417816
  1.6 0.0 copy-start.1
  1.6 0.2 shard_map.77
  1.8 5.4 %collective-permute-start.3 = (f32[7,8,128]{2,1,0:T(8,128)S(1)}, f32[7,8,128]{2,1,0:T(8,128)S(1)}, u32[]{:S(2)}, u32[]{:S(2)}) collective-permute-start(f32[7,8,128]{2,1,0:T(8,128)S(1)} %get-tuple-element.11), channel_id=1, source_target_pairs={{0,16},{16,32},{32,48},{48,64},{64,80},{80,96},{96,112},{112,128},... | collective-permute-start | bytes 86024 | tf_op jit(solution)/shard_map/ppermute | solution.py:254
  7.2 5.3 %collective-permute-start.2 = (f32[7,8,128]{2,1,0:T(8,128)S(1)}, f32[7,8,128]{2,1,0:T(8,128)S(1)}, u32[]{:S(2)}, u32[]{:S(2)}) collective-permute-start(f32[7,8,128]{2,1,0:T(8,128)S(1)} %get-tuple-element.11), channel_id=1, source_target_pairs={{16,0},{32,16},{48,32},{64,48},{80,64},{96,80},{112,96},{128,112},... | collective-permute-start | bytes 86024 | tf_op jit(solution)/shard_map/ppermute | solution.py:255
  12.5 1.3 %collective-permute-start = (f32[408,128]{1,0:T(8,128)S(1)}, f32[408,128]{1,0:T(8,128)S(1)}, u32[]{:S(2)}, u32[]{:S(2)}) collective-permute-start(f32[408,128]{1,0:T(8,128)S(1)} %get-tuple-element.9), channel_id=1, source_target_pairs={{1,0},{2,1},{3,2},{4,3},{5,4},{6,5},{7,6},{8,7},{9,8},{10,9},{11,1... | collective-permute-start | bytes 626696 | tf_op jit(solution)/shard_map/ppermute | solution.py:253
  13.8 4.0 %collective-permute-start.1 = (f32[408,128]{1,0:T(8,128)S(1)}, f32[408,128]{1,0:T(8,128)S(1)}, u32[]{:S(2)}, u32[]{:S(2)}) collective-permute-start(f32[408,128]{1,0:T(8,128)S(1)} %get-tuple-element.10), channel_id=1, source_target_pairs={{0,1},{1,2},{2,3},{3,4},{4,5},{5,6},{6,7},{7,8},{8,9},{9,10},{10,1... | collective-permute-start | bytes 626696 | tf_op jit(solution)/shard_map/ppermute | solution.py:252
  17.8 0.0 collective-permute-done.3
  17.8 0.0 collective-permute-done.2
  17.9 1.9 %collective-permute-start.5 = (f32[7,8,128]{2,1,0:T(8,128)S(1)}, f32[7,8,128]{2,1,0:T(8,128)S(1)}, u32[]{:S(2)}, u32[]{:S(2)}) collective-permute-start(f32[7,8,128]{2,1,0:T(8,128)S(1)} %broadcast_select_fusion.own_ref), channel_id=1, source_target_pairs={{0,1},{1,2},{2,3},{3,4},{4,5},{5,6},{6,7},{7,8},{8,9},{9,10},{10,1... | collective-permute-start | bytes 86024 | tf_op jit(solution)/shard_map/ppermute | solution.py:258
  19.8 1.3 %collective-permute-start.4 = (f32[7,8,128]{2,1,0:T(8,128)S(1)}, f32[7,8,128]{2,1,0:T(8,128)S(1)}, u32[]{:S(2)}, u32[]{:S(2)}) collective-permute-start(f32[7,8,128]{2,1,0:T(8,128)S(1)} %broadcast_select_fusion.own_ref), channel_id=1, source_target_pairs={{1,0},{2,1},{3,2},{4,3},{5,4},{6,5},{7,6},{8,7},{9,8},{10,9},{11,1... | collective-permute-start | bytes 86024 | tf_op jit(solution)/shard_map/ppermute | solution.py:259
  21.1 0.1 add_bitcast_fusion.lat_ref
  21.8 0.0 collective-permute-done.5.cs_ref
  21.8 3.2 %collective-permute-done.4.cn_ref = f32[7,8,128]{2,1,0:T(8,128)S(1)} collective-permute-done((f32[7,8,128]{2,1,0:T(8,128)S(1)}, f32[7,8,128]{2,1,0:T(8,128)S(1)}, u32[]{:S(2)}, u32[]{:S(2)}) %collective-permute-start.4) | collective-permute-done | bytes 28704 | tf_op jit(solution)/shard_map/ppermute | solution.py:259
  25.0 0.0 collective-permute-done.nm_ref
  25.0 0.0 collective-permute-done.1.sm_ref
  25.0 0.0 copy-start.3
  25.0 0.0 copy-start.4
  25.0 0.0 copy-start.5
  25.0 0.0 copy-done.1
  25.0 0.6 copy-done.3
  25.7 0.0 copy-done.4
  25.7 0.0 copy-done.5
  25.7 13.9 %shard_map.78 = (f32[17,6144]{1,0:T(8,128)S(1)}, f32[8,128]{1,0:T(8,128)S(1)}) custom-call(s32[1,3]{1,0:T(1,128)S(1)} %add_bitcast_fusion.lat_ref, s32[1,1]{1,0:T(1,128)S(6)} %copy.8.count_ref, f32[102,8,128]{2,1,0:T(8,128)S(1)} %bitcast.9, f32[408,128]{1,0:T(8,128)S(1)} %collective-permute-done.nm_ref, f32[408,128]{1,0:T(8,128)S(1)} %collective-permute-done.1.sm_ref, ...), custom_call_target="tpu_custom_call" | custom-call | tf_op jit(solution)/shard_map/pallas_call | solution.py:263
  39.5 0.1 broadcast_in_dim.4
  39.6 14.5 %all_to_all.10 = f32[16,8,128]{2,1,0:T(8,128)S(1)} all-to-all(f32[16,8,128]{2,1,0:T(8,128)S(1)} %broadcast_in_dim.4), channel_id=1, replica_groups=mesh['lon'=32,'lat'=16] {'lat'}, dimensions={0} | all-to-all | bytes 131072 | tf_op jit(solution)/shard_map/all_to_all | solution.py:233
  54.2 0.0 copy-start.2
  54.2 27.0 %all_to_all.11.parts_ref = f32[32,8,128]{2,1,0:T(8,128)S(1)} all-to-all(f32[32,8,128]{2,1,0:T(8,128)S(1)} %broadcast_in_dim.5), channel_id=1, replica_groups=mesh['lon'=32,'lat'=16] {'lon'}, dimensions={0} | all-to-all | bytes 262144 | tf_op jit(solution)/shard_map/all_to_all | solution.py:233
  81.2 0.0 copy-done.2
  81.2 3.3 %shard_map.79 = (f32[102,8,128]{2,1,0:T(8,128)}, f32[17,17]{1,0:T(8,128)S(1)}) custom-call(f32[17,16]{1,0:T(8,128)S(1)} %copy-done.2, f32[32,8,128]{2,1,0:T(8,128)S(1)} %all_to_all.11.parts_ref, f32[17,6144]{1,0:T(8,128)S(1)} %get-tuple-element.13.modes_ref), custom_call_target="tpu_custom_call" | custom-call | tf_op jit(solution)/shard_map/pallas_call | solution.py:282
  84.4 0.6 broadcast_multiply_fusion
  (4 shorter events, 0.0 us)
Async XLA Ops:
  0.6 1.0 %copy-start = (f32[17,6,8,128]{3,2,1,0:T(8,128)S(1)}, f32[17,6,8,128]{3,2,1,0:T(8,128)}, u32[]{:S(2)}) copy-start(f32[17,6,8,128]{3,2,1,0:T(8,128)} %param.6) | copy-start | bytes 1253380
  1.6 23.4 %copy-start.1 = (f32[17,6,8,128]{3,2,1,0:T(8,128)S(1)}, f32[17,6,8,128]{3,2,1,0:T(8,128)}, u32[]{:S(2)}) copy-start(f32[17,6,8,128]{3,2,1,0:T(8,128)} %param.6) | copy-start | bytes 1253380
  1.8 16.0 %collective-permute-start.3 = (f32[7,8,128]{2,1,0:T(8,128)S(1)}, f32[7,8,128]{2,1,0:T(8,128)S(1)}, u32[]{:S(2)}, u32[]{:S(2)}) collective-permute-start(f32[7,8,128]{2,1,0:T(8,128)S(1)} %get-tuple-element.11), channel_id=1, source_target_pairs={{0,16},{16,32},{32,48},{48,64},{64,80},{80,96},{96,112},{112,128},... | collective-permute-start | bytes 86024 | tf_op jit(solution)/shard_map/ppermute | solution.py:254
  7.2 10.6 %collective-permute-start.2 = (f32[7,8,128]{2,1,0:T(8,128)S(1)}, f32[7,8,128]{2,1,0:T(8,128)S(1)}, u32[]{:S(2)}, u32[]{:S(2)}) collective-permute-start(f32[7,8,128]{2,1,0:T(8,128)S(1)} %get-tuple-element.11), channel_id=1, source_target_pairs={{16,0},{32,16},{48,32},{64,48},{80,64},{96,80},{112,96},{128,112},... | collective-permute-start | bytes 86024 | tf_op jit(solution)/shard_map/ppermute | solution.py:255
  12.5 12.5 %collective-permute-start = (f32[408,128]{1,0:T(8,128)S(1)}, f32[408,128]{1,0:T(8,128)S(1)}, u32[]{:S(2)}, u32[]{:S(2)}) collective-permute-start(f32[408,128]{1,0:T(8,128)S(1)} %get-tuple-element.9), channel_id=1, source_target_pairs={{1,0},{2,1},{3,2},{4,3},{5,4},{6,5},{7,6},{8,7},{9,8},{10,9},{11,1... | collective-permute-start | bytes 626696 | tf_op jit(solution)/shard_map/ppermute | solution.py:253
  13.8 11.2 %collective-permute-start.1 = (f32[408,128]{1,0:T(8,128)S(1)}, f32[408,128]{1,0:T(8,128)S(1)}, u32[]{:S(2)}, u32[]{:S(2)}) collective-permute-start(f32[408,128]{1,0:T(8,128)S(1)} %get-tuple-element.10), channel_id=1, source_target_pairs={{0,1},{1,2},{2,3},{3,4},{4,5},{5,6},{6,7},{7,8},{8,9},{9,10},{10,1... | collective-permute-start | bytes 626696 | tf_op jit(solution)/shard_map/ppermute | solution.py:252
  17.9 4.0 %collective-permute-start.5 = (f32[7,8,128]{2,1,0:T(8,128)S(1)}, f32[7,8,128]{2,1,0:T(8,128)S(1)}, u32[]{:S(2)}, u32[]{:S(2)}) collective-permute-start(f32[7,8,128]{2,1,0:T(8,128)S(1)} %broadcast_select_fusion.own_ref), channel_id=1, source_target_pairs={{0,1},{1,2},{2,3},{3,4},{4,5},{5,6},{6,7},{7,8},{8,9},{9,10},{10,1... | collective-permute-start | bytes 86024 | tf_op jit(solution)/shard_map/ppermute | solution.py:258
  19.8 5.2 %collective-permute-start.4 = (f32[7,8,128]{2,1,0:T(8,128)S(1)}, f32[7,8,128]{2,1,0:T(8,128)S(1)}, u32[]{:S(2)}, u32[]{:S(2)}) collective-permute-start(f32[7,8,128]{2,1,0:T(8,128)S(1)} %broadcast_select_fusion.own_ref), channel_id=1, source_target_pairs={{1,0},{2,1},{3,2},{4,3},{5,4},{6,5},{7,6},{8,7},{9,8},{10,9},{11,1... | collective-permute-start | bytes 86024 | tf_op jit(solution)/shard_map/ppermute | solution.py:259
  25.0 0.7 copy-start.3
  25.0 0.7 copy-start.4
  25.0 0.7 copy-start.5
  54.2 27.0 %copy-start.2 = (f32[17,16]{1,0:T(8,128)S(1)}, f32[17,16]{1,0:T(8,128)}, u32[]{:S(2)}) copy-start(f32[17,16]{1,0:T(8,128)} %constant.19.clone.omega_ref) | copy-start | bytes 3268

commit v2 on v1

v2 whole, which is shorter than its diff:
```python
import math

import jax
import jax.numpy as jnp
from jax import lax
from jax.experimental import pallas as pl
from jax.experimental.pallas import tpu as pltpu
from jax.sharding import PartitionSpec as P


DIRS = 16
MEMBERS = 17
FIELDS = 6
PAIRS = MEMBERS * FIELDS
SUBSTEPS = 4
RIM = 4
ROWS = 8
COLS = 128
CELLS = FIELDS * ROWS * COLS
TILES = FIELDS * ROWS
HOME = 12
DEEP = 32
GROUP = 2
STRIPS = FIELDS + 1

time_step = 0.15
depth_top = 4.0
depth_low = 6.0
forget = 0.9
highest = lax.Precision.HIGHEST
f32 = jnp.float32


def iota(shape, axis):
    return lax.broadcasted_iota(jnp.int32, shape, axis)


def vmem(count):
    return [pl.BlockSpec(memory_space=pltpu.VMEM)] * count


def pack_kernel(
    x_hbm, index_hbm, count_hbm, value_hbm, weight_hbm, first_ref, second_ref, strip_ref, obs_ref,
    x_ref, index_ref, count_ref, value_ref, weight_ref, sems,
):
    moves = [
        pltpu.make_async_copy(source, target, sems.at[place])
        for place, (source, target) in enumerate(
            [
                (x_hbm, x_ref),
                (index_hbm, index_ref),
                (count_hbm, count_ref),
                (value_hbm, value_ref),
                (weight_hbm, weight_ref),
            ]
        )
    ]
    for move in moves:
        move.start()
    for move in moves:
        move.wait()
    even = (lax.axis_index("lat") & 1) == 0
    tiles = lax.axis_size("lat") * lax.axis_size("lon")

    def rows_out(north_first):
        first, second = (slice(RIM, ROWS), slice(0, RIM)) if north_first else (slice(0, RIM), slice(RIM, ROWS))
        for pair in range(PAIRS):
            first_ref[RIM * pair : RIM * (pair + 1), :] = x_ref[pair, first, :]
            second_ref[RIM * pair : RIM * (pair + 1), :] = x_ref[pair, second, :]

    pl.when(even)(lambda: rows_out(True))
    pl.when(jnp.logical_not(even))(lambda: rows_out(False))
    lane = iota((ROWS, COLS), 1)
    for strip in range(STRIPS):
        total = jnp.zeros((ROWS, COLS), f32)
        for place in range(DIRS if strip < FIELDS else FIELDS):
            pair = place * FIELDS + strip if strip < FIELDS else DIRS * FIELDS + place
            moved = pltpu.roll(x_ref[pair], 8 * place, 1) if place else x_ref[pair]
            mask = ((lane - (8 * place - 4)) & (COLS - 1)) < 8
            total = jnp.where(mask, moved, total)
        strip_ref[strip] = total
    live = (iota((1, COLS), 1) < count_ref[...]).astype(f32)
    obs_ref[...] = jnp.zeros((ROWS, COLS), f32)
    obs_ref[0:1, :] = index_ref[...].astype(f32)
    obs_ref[1:2, :] = value_ref[...]
    obs_ref[2:3, :] = weight_ref[...] * live / float(COLS * tiles)


def layer(thick, zonal, merid, slope_x, slope_y, depth, turn):
    (h, hE, hW, hN, hS), (u, uE, uW, uN, uS), (v, vE, vW, vN, vS) = thick, zonal, merid
    half = 0.5 * time_step
    flux = ((depth + hE) * uE - (depth + hW) * uW) + ((depth + hN) * vN - (depth + hS) * vS)
    h_new = 0.25 * ((hE + hW) + (hN + hS)) - half * flux
    u_new = 0.25 * ((uE + uW) + (uN + uS)) - (
        half * (u * (uE - uW) + v * (uN - uS) + slope_x) - turn * v
    )
    v_new = 0.25 * ((vE + vW) + (vN + vS)) - (
        half * (u * (vE - vW) + v * (vN - vS) + slope_y) + turn * u
    )
    return h_new, u_new, v_new


def advance(stencil, turn):
    top, low = stencil[0], stencil[3]
    top_x, top_y = top[1] - top[2], top[3] - top[4]
    low_x, low_y = low[1] - low[2], low[3] - low[4]
    sum_x, sum_y = top_x + low_x, top_y + low_y
    upper = layer(top, stencil[1], stencil[2], sum_x, sum_y, depth_top, turn)
    lower = layer(low, stencil[4], stencil[5], sum_x + 0.5 * low_x, sum_y + 0.5 * low_y, depth_low, turn)
    return upper + lower


def split(value):
    high = value.astype(jnp.bfloat16)
    rest = value - high.astype(f32)
    middle = rest.astype(jnp.bfloat16)
    return high, middle, (rest - middle.astype(f32)).astype(jnp.bfloat16)


def forecast_kernel(
    x_ref, first_ref, second_ref, own_ref, rim1_ref, rim2_ref, obs_ref,
    modes_ref, mean_ref, pay_ref, state, state2, strips, strips2, inner, final, dev, seen, gram,
):
    lat = lax.axis_index("lat")
    lats = lax.axis_size("lat")
    even = (lat & 1) == 0

    def rows_in(north_first):
        north, south = (first_ref, second_ref) if north_first else (second_ref, first_ref)
        for pair in range(PAIRS):
            state[pair, HOME - RIM : HOME, :] = south[RIM * pair : RIM * (pair + 1), :]
            state[pair, HOME : HOME + ROWS, :] = x_ref[pair]
            state[pair, HOME + ROWS : HOME + ROWS + RIM, :] = north[RIM * pair : RIM * (pair + 1), :]
        north, south = (rim1_ref, rim2_ref) if north_first else (rim2_ref, rim1_ref)
        for strip in range(STRIPS):
            blocks = [south[strip], own_ref[strip], north[strip]]
            for field in range(FIELDS) if strip == FIELDS else [strip]:
                which = 1 if strip == FIELDS else 0
                if which and field:
                    low, mid, high = [pltpu.roll(block, COLS - 8 * field, 1) for block in blocks]
                else:
                    low, mid, high = blocks
                strips[which, field, HOME - RIM : HOME, :] = low[RIM:, :]
                strips[which, field, HOME : HOME + ROWS, :] = mid
                strips[which, field, HOME + ROWS : HOME + ROWS + RIM, :] = high[:RIM, :]

    pl.when(even)(lambda: rows_in(True))
    pl.when(jnp.logical_not(even))(lambda: rows_in(False))

    def row_terms(first):
        row = iota((ROWS, COLS), 0) + (first + lat * ROWS)
        inside = (row >= 0) & (row < lats * ROWS)
        turn = time_step * (0.5 * (2.0 * (row.astype(f32) + 0.5) / float(lats * ROWS) - 1.0))
        return inside, turn

    lane = iota((ROWS, COLS), 1)
    for step in range(SUBSTEPS):
        done = step == SUBSTEPS - 1
        old, fresh = (state, state2) if step % 2 == 0 else (state2, state)
        old_strips, fresh_strips = (strips, strips2) if step % 2 == 0 else (strips2, strips)
        starts = [HOME] if done else [HOME - RIM, HOME + RIM]

        def triple(ref, start, *at):
            return [ref[(*at, slice(start + d, start + d + ROWS), slice(None))] for d in (0, 1, -1)]

        def members_step(members, which, shifts):
            for half, start in enumerate(starts):
                inside, turn = row_terms(start - HOME)
                stencils = []
                for member, shift in zip(members, shifts):
                    stencil = []
                    for field in range(FIELDS):
                        c, n, s = triple(old, start, member * FIELDS + field)
                        beyond = old_strips[which, field, start : start + ROWS, :]
                        if shift is not None:
                            beyond = pltpu.roll(beyond, COLS - shift, 1)
                        e = pltpu.roll(jnp.where(lane == 0, beyond, c), COLS - 1, 1)
                        w = pltpu.roll(jnp.where(lane == COLS - 1, beyond, c), 1, 1)
                        stencil.append((c, e, w, n, s))
                    stencils.append(stencil)
                if not done:
                    for field in range(FIELDS):
                        if shifts[0] is None:
                            inner[which, field, ROWS * half : ROWS * (half + 1), :] = stencils[0][field][0]
                            continue
                        total = inner[which, field, ROWS * half : ROWS * (half + 1), :]
                        for shift, stencil in zip(shifts, stencils):
                            edge = ((lane - shift + 1) & (COLS - 1)) < 2
                            total = jnp.where(edge, pltpu.roll(stencil[field][0], shift, 1), total)
                        inner[which, field, ROWS * half : ROWS * (half + 1), :] = total
                for member, stencil in zip(members, stencils):
                    new = advance(stencil, turn)
                    for field in range(FIELDS):
                        if done:
                            final[member * FIELDS + field] = new[field]
                        else:
                            fresh[member * FIELDS + field, start : start + ROWS, :] = jnp.where(inside, new[field], 0.0)

        def group_step(index, carry):
            members = [GROUP * index + k for k in range(GROUP)]
            members_step(members, 0, [8 * member for member in members])
            return carry

        lax.fori_loop(0, DIRS // GROUP, group_step, 0)
        members_step([DIRS], 1, [None])
        if not done:
            for which in range(2):
                for half, start in enumerate(starts):
                    inside, turn = row_terms(start - HOME)
                    stencil = []
                    for field in range(FIELDS):
                        c, n, s = triple(old_strips, start, which, field)
                        beyond = inner[which, field, ROWS * half : ROWS * (half + 1), :]
                        e = pltpu.roll(jnp.where((lane & 7) == 0, beyond, c), COLS - 1, 1)
                        w = pltpu.roll(jnp.where((lane & 7) == 7, beyond, c), 1, 1)
                        stencil.append((c, e, w, n, s))
                    new = advance(stencil, turn)
                    for field in range(FIELDS):
                        fresh_strips[which, field, start : start + ROWS, :] = jnp.where(inside, new[field], 0.0)

    sub8 = iota((ROWS, COLS), 0)
    cell = obs_ref[0:1, :].astype(jnp.int32)
    column = jnp.broadcast_to(cell & (COLS - 1), (ROWS, COLS))
    at_row = jnp.broadcast_to(lax.shift_right_logical(cell, 7), (ROWS, COLS)) == sub8
    for member in range(MEMBERS):
        surface = final[member * FIELDS] + final[member * FIELDS + 3]
        picked = jnp.take_along_axis(surface, column, axis=1)
        seen[member : member + 1, :] = jnp.sum(jnp.where(at_row, picked, 0.0), axis=0, keepdims=True)

    for field in range(FIELDS):
        total = final[field]
        for member in range(1, MEMBERS):
            total = total + final[member * FIELDS + field]
        mean = total * (1.0 / MEMBERS)
        mean_ref[ROWS * field : ROWS * (field + 1), :] = mean
        for member in range(DIRS):
            at = member * TILES + field * ROWS
            dev[at : at + ROWS, :] = final[member * FIELDS + field] - mean
    for tile in range(TILES):
        span = slice(COLS * tile, COLS * (tile + 1))
        parts = split(dev[pl.ds(tile, DIRS, stride=TILES), :])
        for place, part in enumerate((0, 1, 2, 0, 1, 0)):
            modes_ref[DIRS * place : DIRS * (place + 1), span] = parts[part]

    stack = modes_ref[0 : 3 * DIRS, :]
    blocks = lax.dot_general(stack, stack, (((1,), (1,)), ((), ())), preferred_element_type=f32)
    rows3 = blocks[0:DIRS, :] + (blocks[DIRS : 2 * DIRS, :] + blocks[2 * DIRS :, :])
    mode_gram = rows3[:, 0:DIRS] + (rows3[:, DIRS : 2 * DIRS] + rows3[:, 2 * DIRS :])

    observed = seen[...]
    obs_mean = jnp.sum(observed, axis=0, keepdims=True) * (1.0 / MEMBERS)
    anomaly = observed[0:DIRS, :] - obs_mean
    innovation = obs_ref[1:2, :] - obs_mean
    weighted = anomaly * obs_ref[2:3, :]
    obs_gram = lax.dot_general(
        weighted, anomaly, (((1,), (1,)), ((), ())), precision=highest, preferred_element_type=f32
    )
    obs_proj = jnp.sum(weighted * innovation, axis=1, keepdims=True)
    row, col = iota((DIRS, DIRS), 0), iota((DIRS, DIRS), 1)
    gram[...] = jnp.zeros((DIRS, COLS), f32)
    gram[:, 0:DIRS] = jnp.where(row < col, obs_gram, mode_gram)
    gram[:, DIRS : DIRS + 1] = jnp.sum(jnp.where(row == col, obs_gram, 0.0), axis=1, keepdims=True)
    gram[:, DIRS + 1 : DIRS + 2] = obs_proj
    packed = gram[0:4, :]
    for quarter in range(1, 4):
        packed = packed + pltpu.roll(gram[4 * quarter : 4 * quarter + 4, :], 32 * quarter, 1)
    pay_ref[...] = packed


def analysis_kernel(parts_ref, modes_ref, mean_ref, out_ref, spread_ref, gram):
    packed = jnp.sum(parts_ref[...], axis=0)
    for quarter in range(4):
        gram[4 * quarter : 4 * quarter + 4, :] = (
            pltpu.roll(packed, COLS - 32 * quarter, 1) if quarter else packed
        )
    joined = gram[...]
    row, col = iota((DIRS, DIRS), 0), iota((DIRS, DIRS), 1)
    square = joined[:, 0:DIRS]
    upper = jnp.where(row < col, square, 0.0)
    lower = jnp.where(row > col, square, 0.0)
    mode_gram = jnp.where(row == col, square, 0.0) + (lower + lower.T)
    obs_gram = jnp.where(row == col, joined[:, DIRS : DIRS + 1], 0.0) + (upper + upper.T)
    precision = obs_gram + (DIRS / forget) * (jnp.where(row == col, 1.0, 0.0) - 1.0 / MEMBERS)
    sub, lane = iota((DIRS, COLS), 0), iota((DIRS, COLS), 1)
    copies = 6 * DIRS
    gram[:, copies : copies + DIRS] = precision
    gram[:, copies + DIRS : copies + DIRS + 1] = joined[:, DIRS + 1 : DIRS + 2]
    unit = jnp.where((lane & (DIRS - 1)) == sub, 1.0, 0.0)
    work = jnp.where(lane < copies, unit, gram[...])
    work = jnp.where(lane <= copies + DIRS, work, 0.0)
    for pivot in range(DIRS):
        column = jnp.broadcast_to(work[:, copies + pivot : copies + pivot + 1], (DIRS, COLS))
        value = column[pivot : pivot + 1, :]
        inverse = lax.rsqrt(value)
        inverse = inverse * (1.5 - 0.5 * value * inverse * inverse)
        pivot_row = work[pivot : pivot + 1, :] * inverse
        work = jnp.where(sub == pivot, pivot_row, work - jnp.where(sub > pivot, column * inverse, 0.0) * pivot_row)
    inverse_factor = work[:, :copies]
    solved = work[:, copies + DIRS : copies + DIRS + 1]
    weights = jnp.sum(solved * inverse_factor, axis=0, keepdims=True)
    spare = (math.sqrt(MEMBERS) - 1.0) / DIRS
    scale = math.sqrt(DIRS)
    sums = jnp.sum(inverse_factor, axis=0, keepdims=True)
    rotation_t = jnp.concatenate(
        [
            scale * inverse_factor + (scale * (spare - 1.0) / MEMBERS) * sums,
            (-scale * (1.0 + DIRS * spare) / MEMBERS) * sums,
        ],
        axis=0,
    )
    coefficient_t = rotation_t + weights
    high, middle, low = split(coefficient_t)
    place = iota((MEMBERS, copies), 1)
    stack = jnp.where(place < 3 * DIRS, high.astype(f32), jnp.where(place < 5 * DIRS, middle.astype(f32), low.astype(f32)))
    stack = stack.astype(jnp.bfloat16)
    for field in range(FIELDS):
        span = slice(field * ROWS * COLS, (field + 1) * ROWS * COLS)
        update = jnp.dot(stack, modes_ref[:, span], preferred_element_type=f32)
        for row_here in range(ROWS):
            tile = field * ROWS + row_here
            out_ref[pl.ds(tile, MEMBERS, stride=TILES), :] = (
                update[:, COLS * row_here : COLS * (row_here + 1)] + mean_ref[tile : tile + 1, :]
            )
    rotation_t = rotation_t[:, 0:DIRS]
    half_way = jnp.dot(rotation_t, mode_gram, precision=highest, preferred_element_type=f32)
    spread = lax.dot_general(
        half_way, rotation_t, (((1,), (1,)), ((), ())), precision=highest, preferred_element_type=f32
    )
    spread_ref[...] = spread / float(CELLS * lax.axis_size("lat") * lax.axis_size("lon"))


def neighbours(axis, parity, wrap):
    count = lax.axis_size(axis)
    pairs = [(i, i + 1) for i in range(parity, count - 1, 2)]
    if wrap and parity:
        pairs.append((count - 1, 0))
    return pairs + [(j, i) for i, j in pairs]


def all_parts(part, groups):
    count = len(groups[0])
    return lax.all_to_all(
        jnp.broadcast_to(part[None], (count,) + part.shape), ("lon", "lat"), 0, 0, axis_index_groups=groups
    )


def on_device(sample_collection, obs_index, obs_count, obs_value, obs_weight):
    lat_tiles, lon_tiles = lax.axis_size("lat"), lax.axis_size("lon")
    small = pltpu.CompilerParams(vmem_limit_bytes=16 * 2**20)
    blocks = sample_collection.reshape(PAIRS, ROWS, COLS)
    rows_shape = jax.ShapeDtypeStruct((PAIRS * RIM, COLS), f32)
    strips_shape = jax.ShapeDtypeStruct((STRIPS, ROWS, COLS), f32)
    first_msg, second_msg, strip_msg, obs = pl.pallas_call(
        pack_kernel,
        out_shape=[rows_shape, rows_shape, strips_shape, jax.ShapeDtypeStruct((ROWS, COLS), f32)],
        in_specs=[pl.BlockSpec(memory_space=pltpu.HBM)] * 5,
        out_specs=vmem(4),
        scratch_shapes=[
            pltpu.VMEM((PAIRS, ROWS, COLS), f32),
            pltpu.VMEM((1, COLS), jnp.int32),
            pltpu.VMEM((1, 1), jnp.int32),
            pltpu.VMEM((1, COLS), f32),
            pltpu.VMEM((1, COLS), f32),
            pltpu.SemaphoreType.DMA((5,)),
        ],
        compiler_params=small,
    )(blocks, obs_index.reshape(1, COLS), obs_count, obs_value.reshape(1, COLS), obs_weight.reshape(1, COLS))
    strip1 = lax.ppermute(strip_msg, "lon", neighbours("lon", 0, True))
    strip2 = lax.ppermute(strip_msg, "lon", neighbours("lon", 1, True))
    first = lax.ppermute(first_msg, "lat", neighbours("lat", 0, False))
    second = lax.ppermute(second_msg, "lat", neighbours("lat", 1, False))
    eastern = (iota(strip_msg.shape, 2) & 7) < RIM
    own_strip = jnp.where(eastern == ((lax.axis_index("lon") & 1) == 0), strip1, strip2)
    rim1 = lax.ppermute(own_strip, "lat", neighbours("lat", 0, False))
    rim2 = lax.ppermute(own_strip, "lat", neighbours("lat", 1, False))

    modes, mean, part = pl.pallas_call(
        forecast_kernel,
        out_shape=[
            jax.ShapeDtypeStruct((6 * DIRS, CELLS), jnp.bfloat16),
            jax.ShapeDtypeStruct((TILES, COLS), f32),
            jax.ShapeDtypeStruct((4, COLS), f32),
        ],
        in_specs=vmem(7),
        out_specs=vmem(3),
        scratch_shapes=[
            pltpu.VMEM((PAIRS, DEEP, COLS), f32),
            pltpu.VMEM((PAIRS, DEEP, COLS), f32),
            pltpu.VMEM((2, FIELDS, DEEP, COLS), f32),
            pltpu.VMEM((2, FIELDS, DEEP, COLS), f32),
            pltpu.VMEM((2, FIELDS, ROWS + 2 * RIM, COLS), f32),
            pltpu.VMEM((PAIRS, ROWS, COLS), f32),
            pltpu.VMEM((DIRS * TILES, COLS), f32),
            pltpu.VMEM((MEMBERS, COLS), f32),
            pltpu.VMEM((DIRS, COLS), f32),
        ],
        compiler_params=small,
    )(blocks, first, second, own_strip, rim1, rim2, obs)

    fine = min(16, lon_tiles)
    index = [[lon * lat_tiles + lat for lat in range(lat_tiles)] for lon in range(lon_tiles)]
    near = [
        [index[base + k][lat] for k in range(fine)] for base in range(0, lon_tiles, fine) for lat in range(lat_tiles)
    ]
    far = [[index[lon][lat] for lon in range(k, lon_tiles, fine) for lat in range(lat_tiles)] for k in range(fine)]
    part = jnp.sum(all_parts(part, near), axis=0)
    parts = all_parts(part, far)
    analysis, spread = pl.pallas_call(
        analysis_kernel,
        out_shape=[jax.ShapeDtypeStruct((PAIRS * ROWS, COLS), f32), jax.ShapeDtypeStruct((MEMBERS, MEMBERS), f32)],
        in_specs=vmem(3),
        out_specs=vmem(2),
        scratch_shapes=[pltpu.VMEM((DIRS, COLS), f32)],
        compiler_params=small,
    )(parts, modes, mean)
    return analysis.reshape(sample_collection.shape), spread


def solution(mesh):
    return jax.shard_map(
        on_device,
        mesh=mesh,
        in_specs=(
            P(None, None, "lat", "lon"),
            P("lat", "lon", None),
            P("lat", "lon"),
            P("lat", "lon", None),
            P("lat", "lon", None),
        ),
        out_specs=(P(None, None, "lat", "lon"), P()),
        check_vma=False,
    )
```

time: 85.5 us -> 76.8 us (0.90)
  blocking collectives: 41.5 us -> 31.2 us
  starting transfers between devices: 19.2 us -> 27.7 us
  Pallas kernels: 17.3 us -> 10.9 us
  local copies, waits for them, and re-layouts: 1.74 us -> 3.99 us
  waiting for transfers between devices: 3.18 us -> 1.25 us
    all_to_all x2, blocking collectives: 41.5 us -> 31.2 us  [all_parts(): lax.all_to_all(jnp.broadcast_to(part[None], (count,) + part.shape), ('lon...]
    ppermute x6, starting transfers between devices: 19.2 us -> 27.7 us  [the longest x1 10.9 us: on_device(): strip1 = lax.ppermute(strip_msg, 'lon', neighbours('lon', 0, True))]
    pallas_call x3, Pallas kernels: 17.3 us -> 10.9 us  [the longest x1 7.53 us: on_device(): pl.pallas_call(forecast_kernel, out_shape=[jax.ShapeDtypeStruct((6 * DIRS...]
    unnamed x12 -> x10, local copies, waits for them, and re-layouts: 1.67 us -> 3.97 us
    ppermute x6, waiting for transfers between devices: 3.18 us -> 1.25 us  [the longest x1 1.23 us: on_device(): rim1 = lax.ppermute(own_strip, 'lat', neighbours('lat', 0, False))]
where the time goes in v2:
time: 76.8 us; the launch traced here: 76.4 us
  blocking collectives  31.2 us (41%)
  starting transfers between devices  27.7 us (36%)
  Pallas kernels  10.9 us (14%)
  local copies, waits for them, and re-layouts  3.99 us (5%)
  between operations  1.39 us (2%)
  waiting for transfers between devices  1.25 us (2%)
    all_to_all x2, blocking collectives, all_parts(): lax.all_to_all(jnp.broadcast_to(part[None], (count,) + part.shape), ('lon...  31.2 us
    ppermute x1, starting transfers between devices, on_device(): strip1 = lax.ppermute(strip_msg, 'lon', neighbours('lon', 0, True))  10.9 us
    ppermute x1, starting transfers between devices, on_device(): rim1 = lax.ppermute(own_strip, 'lat', neighbours('lat', 0, False))  7.91 us
    pallas_call x1, Pallas kernels, on_device(): pl.pallas_call(forecast_kernel, out_shape=[jax.ShapeDtypeStruct((6 * DIRS...  7.53 us
    ppermute x1, starting transfers between devices, on_device(): strip2 = lax.ppermute(strip_msg, 'lon', neighbours('lon', 1, True))  5.38 us
    unnamed x10, local copies, waits for them, and re-layouts  3.97 us
    pallas_call x1, Pallas kernels, on_device(): pl.pallas_call(analysis_kernel, out_shape=[jax.ShapeDtypeStruct((PAIRS *...  2.81 us
    ppermute x1, starting transfers between devices, on_device(): first = lax.ppermute(first_msg, 'lat', neighbours('lat', 0, False))  2.22 us
  transfers between devices with their start and end apart: 6, of which 1 were waited for; matrix products, arithmetic and copies ran while one was open for 0% of the time, Pallas kernels for 0%

profile of v2, /device:TPU:1, one launch (start us, length us, event | category | flops | bytes accessed | tf_op | source)
XLA Modules:
  0.0 76.4 jit_solution(5624119072515403185)
XLA Ops:
  1.3 0.0 copy-start
  1.3 1.0 %copy-done = f32[17,6,8,128]{3,2,1,0:T(8,128)S(1)} copy-done((f32[17,6,8,128]{3,2,1,0:T(8,128)S(1)}, f32[17,6,8,128]{3,2,1,0:T(8,128)}, u32[]{:S(2)}) %copy-start) | copy-done | bytes 417816
  2.3 0.0 copy-start.2
  2.3 0.7 copy-done.2
  2.9 0.0 copy-start.3
  2.9 0.7 copy-done.3
  3.6 0.0 copy-start.4
  3.6 0.7 copy-done.4
  4.3 0.5 shard_map.68
  4.8 5.4 %collective-permute-start.3 = (f32[7,8,128]{2,1,0:T(8,128)S(1)}, f32[7,8,128]{2,1,0:T(8,128)S(1)}, u32[]{:S(2)}, u32[]{:S(2)}) collective-permute-start(f32[7,8,128]{2,1,0:T(8,128)S(1)} %get-tuple-element.13), channel_id=1, source_target_pairs={{16,32},{48,64},{80,96},{112,128},{144,160},{176,192},{208,224},{2... | collective-permute-start | bytes 86024 | tf_op jit(solution)/shard_map/ppermute | solution.py:369
  10.2 10.9 %collective-permute-start.2 = (f32[7,8,128]{2,1,0:T(8,128)S(1)}, f32[7,8,128]{2,1,0:T(8,128)S(1)}, u32[]{:S(2)}, u32[]{:S(2)}) collective-permute-start(f32[7,8,128]{2,1,0:T(8,128)S(1)} %get-tuple-element.13), channel_id=1, source_target_pairs={{0,16},{32,48},{64,80},{96,112},{128,144},{160,176},{192,208},{224... | collective-permute-start | bytes 86024 | tf_op jit(solution)/shard_map/ppermute | solution.py:368
  21.0 2.2 %collective-permute-start = (f32[408,128]{1,0:T(8,128)S(1)}, f32[408,128]{1,0:T(8,128)S(1)}, u32[]{:S(2)}, u32[]{:S(2)}) collective-permute-start(f32[408,128]{1,0:T(8,128)S(1)} %get-tuple-element.11), channel_id=1, source_target_pairs={{0,1},{2,3},{4,5},{6,7},{8,9},{10,11},{12,13},{14,15},{1,0},{3,2},... | collective-permute-start | bytes 626696 | tf_op jit(solution)/shard_map/ppermute | solution.py:370
  23.3 0.7 collective-permute-start.1
  24.0 0.0 collective-permute-done.3
  24.0 0.0 collective-permute-done.2
  24.0 0.7 collective-permute-start.5
  24.7 7.9 %collective-permute-start.4 = (f32[7,8,128]{2,1,0:T(8,128)S(1)}, f32[7,8,128]{2,1,0:T(8,128)S(1)}, u32[]{:S(2)}, u32[]{:S(2)}) collective-permute-start(f32[7,8,128]{2,1,0:T(8,128)S(1)} %broadcast_select_fusion.own_ref), channel_id=1, source_target_pairs={{0,1},{2,3},{4,5},{6,7},{8,9},{10,11},{12,13},{14,15},{1,0},{3,2},... | collective-permute-start | bytes 86024 | tf_op jit(solution)/shard_map/ppermute | solution.py:374
  32.6 0.0 collective-permute-done.5.rim2_ref
  32.6 1.2 %collective-permute-done.4.rim1_ref = f32[7,8,128]{2,1,0:T(8,128)S(1)} collective-permute-done((f32[7,8,128]{2,1,0:T(8,128)S(1)}, f32[7,8,128]{2,1,0:T(8,128)S(1)}, u32[]{:S(2)}, u32[]{:S(2)}) %collective-permute-start.4) | collective-permute-done | bytes 28704 | tf_op jit(solution)/shard_map/ppermute | solution.py:374
  33.8 0.0 collective-permute-done.first_ref
  33.8 0.0 collective-permute-done.1.second_ref
  33.8 0.0 copy-start.1
  33.9 1.0 %copy-done.1 = f32[17,6,8,128]{3,2,1,0:T(8,128)S(1)} copy-done((f32[17,6,8,128]{3,2,1,0:T(8,128)S(1)}, f32[17,6,8,128]{3,2,1,0:T(8,128)}, u32[]{:S(2)}) %copy-start.1) | copy-done | bytes 417816
  34.9 7.5 %shard_map.69 = (bf16[96,6144]{1,0:T(8,128)(2,1)S(1)}, f32[48,128]{1,0:T(8,128)S(1)}, f32[4,128]{1,0:T(4,128)S(1)}) custom-call(f32[102,8,128]{2,1,0:T(8,128)S(1)} %bitcast.6, f32[408,128]{1,0:T(8,128)S(1)} %collective-permute-done.first_ref, f32[408,128]{1,0:T(8,128)S(1)} %collective-permute-done.1.second_ref, ...), custom_call_target="tpu_custom_call" | custom-call | tf_op jit(solution)/shard_map/pallas_call | solution.py:377
  42.4 11.6 %all_to_all.10 = f32[16,4,128]{2,1,0:T(4,128)S(1)} all-to-all(f32[16,4,128]{2,1,0:T(4,128)S(1)} %broadcast_in_dim.4), channel_id=1, replica_groups={{0,16,32,48,64,80,96,112,128,144,160,176,192,208,224,240},{1,17,33,49,6..., dimensions={0} | all-to-all | bytes 65536 | tf_op jit(solution)/shard_map/all_to_all | solution.py:342
  54.1 19.5 %all_to_all.11.parts_ref = f32[32,4,128]{2,1,0:T(4,128)S(1)} all-to-all(f32[32,4,128]{2,1,0:T(4,128)S(1)} %broadcast_in_dim.5), channel_id=1, replica_groups={{0,1,2,3,4,5,6,7,8,9,10,11,12,13,14,15,256,257,258,259,260,261,262,263,..., dimensions={0} | all-to-all | bytes 131072 | tf_op jit(solution)/shard_map/all_to_all | solution.py:342
  73.6 2.8 %shard_map.70 = (f32[816,128]{1,0:T(8,128)}, f32[17,17]{1,0:T(8,128)}) custom-call(f32[32,4,128]{2,1,0:T(4,128)S(1)} %all_to_all.11.parts_ref, bf16[96,6144]{1,0:T(8,128)(2,1)S(1)} %get-tuple-element.16.modes_ref, f32[48,128]{1,0:T(8,128)S(1)} %get-tuple-element.17.mean_ref), custom_call_target="tpu_custom_call" | custom-call | tf_op jit(solution)/shard_map/pallas_call | solution.py:408
  (5 shorter events, 0.1 us)
Async XLA Ops:
  1.3 1.0 %copy-start = (f32[17,6,8,128]{3,2,1,0:T(8,128)S(1)}, f32[17,6,8,128]{3,2,1,0:T(8,128)}, u32[]{:S(2)}) copy-start(f32[17,6,8,128]{3,2,1,0:T(8,128)} %param.5) | copy-start | bytes 1253380
  2.3 0.7 copy-start.2
  2.9 0.7 copy-start.3
  3.6 0.7 copy-start.4
  4.8 19.2 %collective-permute-start.3 = (f32[7,8,128]{2,1,0:T(8,128)S(1)}, f32[7,8,128]{2,1,0:T(8,128)S(1)}, u32[]{:S(2)}, u32[]{:S(2)}) collective-permute-start(f32[7,8,128]{2,1,0:T(8,128)S(1)} %get-tuple-element.13), channel_id=1, source_target_pairs={{16,32},{48,64},{80,96},{112,128},{144,160},{176,192},{208,224},{2... | collective-permute-start | bytes 86024 | tf_op jit(solution)/shard_map/ppermute | solution.py:369
  10.2 13.8 %collective-permute-start.2 = (f32[7,8,128]{2,1,0:T(8,128)S(1)}, f32[7,8,128]{2,1,0:T(8,128)S(1)}, u32[]{:S(2)}, u32[]{:S(2)}) collective-permute-start(f32[7,8,128]{2,1,0:T(8,128)S(1)} %get-tuple-element.13), channel_id=1, source_target_pairs={{0,16},{32,48},{64,80},{96,112},{128,144},{160,176},{192,208},{224... | collective-permute-start | bytes 86024 | tf_op jit(solution)/shard_map/ppermute | solution.py:368
  21.0 12.8 %collective-permute-start = (f32[408,128]{1,0:T(8,128)S(1)}, f32[408,128]{1,0:T(8,128)S(1)}, u32[]{:S(2)}, u32[]{:S(2)}) collective-permute-start(f32[408,128]{1,0:T(8,128)S(1)} %get-tuple-element.11), channel_id=1, source_target_pairs={{0,1},{2,3},{4,5},{6,7},{8,9},{10,11},{12,13},{14,15},{1,0},{3,2},... | collective-permute-start | bytes 626696 | tf_op jit(solution)/shard_map/ppermute | solution.py:370
  23.3 10.6 %collective-permute-start.1 = (f32[408,128]{1,0:T(8,128)S(1)}, f32[408,128]{1,0:T(8,128)S(1)}, u32[]{:S(2)}, u32[]{:S(2)}) collective-permute-start(f32[408,128]{1,0:T(8,128)S(1)} %get-tuple-element.12), channel_id=1, source_target_pairs={{1,2},{3,4},{5,6},{7,8},{9,10},{11,12},{13,14},{2,1},{4,3},{6,5},{... | collective-permute-start | bytes 626696 | tf_op jit(solution)/shard_map/ppermute | solution.py:371
  24.0 8.6 %collective-permute-start.5 = (f32[7,8,128]{2,1,0:T(8,128)S(1)}, f32[7,8,128]{2,1,0:T(8,128)S(1)}, u32[]{:S(2)}, u32[]{:S(2)}) collective-permute-start(f32[7,8,128]{2,1,0:T(8,128)S(1)} %broadcast_select_fusion.own_ref), channel_id=1, source_target_pairs={{1,2},{3,4},{5,6},{7,8},{9,10},{11,12},{13,14},{2,1},{4,3},{6,5},{... | collective-permute-start | bytes 86024 | tf_op jit(solution)/shard_map/ppermute | solution.py:375
  24.7 9.2 %collective-permute-start.4 = (f32[7,8,128]{2,1,0:T(8,128)S(1)}, f32[7,8,128]{2,1,0:T(8,128)S(1)}, u32[]{:S(2)}, u32[]{:S(2)}) collective-permute-start(f32[7,8,128]{2,1,0:T(8,128)S(1)} %broadcast_select_fusion.own_ref), channel_id=1, source_target_pairs={{0,1},{2,3},{4,5},{6,7},{8,9},{10,11},{12,13},{14,15},{1,0},{3,2},... | collective-permute-start | bytes 86024 | tf_op jit(solution)/shard_map/ppermute | solution.py:374
  33.8 1.0 %copy-start.1 = (f32[17,6,8,128]{3,2,1,0:T(8,128)S(1)}, f32[17,6,8,128]{3,2,1,0:T(8,128)}, u32[]{:S(2)}) copy-start(f32[17,6,8,128]{3,2,1,0:T(8,128)} %param.5) | copy-start | bytes 1253380

commit v3 on v2

--- a/solution.py
+++ b/solution.py
@@ -39,28 +39,11 @@
     return [pl.BlockSpec(memory_space=pltpu.VMEM)] * count
 
 
-def pack_kernel(
-    x_hbm, index_hbm, count_hbm, value_hbm, weight_hbm, first_ref, second_ref, strip_ref, obs_ref,
-    x_ref, index_ref, count_ref, value_ref, weight_ref, sems,
-):
-    moves = [
-        pltpu.make_async_copy(source, target, sems.at[place])
-        for place, (source, target) in enumerate(
-            [
-                (x_hbm, x_ref),
-                (index_hbm, index_ref),
-                (count_hbm, count_ref),
-                (value_hbm, value_ref),
-                (weight_hbm, weight_ref),
-            ]
-        )
-    ]
-    for move in moves:
-        move.start()
-    for move in moves:
-        move.wait()
+def pack_kernel(x_hbm, first_ref, second_ref, strip_ref, x_ref, sem):
+    move = pltpu.make_async_copy(x_hbm, x_ref, sem)
+    move.start()
+    move.wait()
     even = (lax.axis_index("lat") & 1) == 0
-    tiles = lax.axis_size("lat") * lax.axis_size("lon")
 
     def rows_out(north_first):
         first, second = (slice(RIM, ROWS), slice(0, RIM)) if north_first else (slice(0, RIM), slice(RIM, ROWS))
@@ -79,11 +62,6 @@
             mask = ((lane - (8 * place - 4)) & (COLS - 1)) < 8
             total = jnp.where(mask, moved, total)
         strip_ref[strip] = total
-    live = (iota((1, COLS), 1) < count_ref[...]).astype(f32)
-    obs_ref[...] = jnp.zeros((ROWS, COLS), f32)
-    obs_ref[0:1, :] = index_ref[...].astype(f32)
-    obs_ref[1:2, :] = value_ref[...]
-    obs_ref[2:3, :] = weight_ref[...] * live / float(COLS * tiles)
 
 
 def layer(thick, zonal, merid, slope_x, slope_y, depth, turn):
@@ -118,9 +96,18 @@
 
 
 def forecast_kernel(
-    x_ref, first_ref, second_ref, own_ref, rim1_ref, rim2_ref, obs_ref,
-    modes_ref, mean_ref, pay_ref, state, state2, strips, strips2, inner, final, dev, seen, gram,
+    x_ref, first_ref, second_ref, own_ref, rim1_ref, rim2_ref, count_ref, index_hbm, value_hbm, weight_hbm,
+    modes_ref, mean_ref, pay_ref,
+    state, state2, strips, strips2, inner, final, dev, seen, gram, index_ref, value_ref, weight_ref, sems,
 ):
+    moves = [
+        pltpu.make_async_copy(source, target, sems.at[place])
+        for place, (source, target) in enumerate(
+            [(index_hbm, index_ref), (value_hbm, value_ref), (weight_hbm, weight_ref)]
+        )
+    ]
+    for move in moves:
+        move.start()
     lat = lax.axis_index("lat")
     lats = lax.axis_size("lat")
     even = (lat & 1) == 0
@@ -219,7 +206,9 @@
                         fresh_strips[which, field, start : start + ROWS, :] = jnp.where(inside, new[field], 0.0)
 
     sub8 = iota((ROWS, COLS), 0)
-    cell = obs_ref[0:1, :].astype(jnp.int32)
+    for move in moves:
+        move.wait()
+    cell = index_ref[...]
     column = jnp.broadcast_to(cell & (COLS - 1), (ROWS, COLS))
     at_row = jnp.broadcast_to(lax.shift_right_logical(cell, 7), (ROWS, COLS)) == sub8
     for member in range(MEMBERS):
@@ -250,8 +239,9 @@
     observed = seen[...]
     obs_mean = jnp.sum(observed, axis=0, keepdims=True) * (1.0 / MEMBERS)
     anomaly = observed[0:DIRS, :] - obs_mean
-    innovation = obs_ref[1:2, :] - obs_mean
-    weighted = anomaly * obs_ref[2:3, :]
+    innovation = value_ref[...] - obs_mean
+    live = (iota((1, COLS), 1) < count_ref[...]).astype(f32)
+    weighted = anomaly * (weight_ref[...] * live / float(COLS * lats * lax.axis_size("lon")))
     obs_gram = lax.dot_general(
         weighted, anomaly, (((1,), (1,)), ((), ())), precision=highest, preferred_element_type=f32
     )
@@ -350,21 +340,21 @@
     blocks = sample_collection.reshape(PAIRS, ROWS, COLS)
     rows_shape = jax.ShapeDtypeStruct((PAIRS * RIM, COLS), f32)
     strips_shape = jax.ShapeDtypeStruct((STRIPS, ROWS, COLS), f32)
-    first_msg, second_msg, strip_msg, obs = pl.pallas_call(
+    in_hbm = pl.BlockSpec(memory_space=pltpu.HBM)
+    blocks, index, value, weight = [
+        pltpu.with_memory_space_constraint(array, pltpu.HBM)
+        for array in (
+            blocks, obs_index.reshape(1, COLS), obs_value.reshape(1, COLS), obs_weight.reshape(1, COLS)
+        )
+    ]
+    first_msg, second_msg, strip_msg, here = pl.pallas_call(
         pack_kernel,
-        out_shape=[rows_shape, rows_shape, strips_shape, jax.ShapeDtypeStruct((ROWS, COLS), f32)],
-        in_specs=[pl.BlockSpec(memory_space=pltpu.HBM)] * 5,
+        out_shape=[rows_shape, rows_shape, strips_shape, jax.ShapeDtypeStruct((PAIRS, ROWS, COLS), f32)],
+        in_specs=[in_hbm],
         out_specs=vmem(4),
-        scratch_shapes=[
-            pltpu.VMEM((PAIRS, ROWS, COLS), f32),
-            pltpu.VMEM((1, COLS), jnp.int32),
-            pltpu.VMEM((1, 1), jnp.int32),
-            pltpu.VMEM((1, COLS), f32),
-            pltpu.VMEM((1, COLS), f32),
-            pltpu.SemaphoreType.DMA((5,)),
-        ],
+        scratch_shapes=[pltpu.SemaphoreType.DMA],
         compiler_params=small,
-    )(blocks, obs_index.reshape(1, COLS), obs_count, obs_value.reshape(1, COLS), obs_weight.reshape(1, COLS))
+    )(blocks)
     strip1 = lax.ppermute(strip_msg, "lon", neighbours("lon", 0, True))
     strip2 = lax.ppermute(strip_msg, "lon", neighbours("lon", 1, True))
     first = lax.ppermute(first_msg, "lat", neighbours("lat", 0, False))
@@ -381,7 +371,7 @@
             jax.ShapeDtypeStruct((TILES, COLS), f32),
             jax.ShapeDtypeStruct((4, COLS), f32),
         ],
-        in_specs=vmem(7),
+        in_specs=vmem(7) + [in_hbm] * 3,
         out_specs=vmem(3),
         scratch_shapes=[
             pltpu.VMEM((PAIRS, DEEP, COLS), f32),
@@ -393,9 +383,15 @@
             pltpu.VMEM((DIRS * TILES, COLS), f32),
             pltpu.VMEM((MEMBERS, COLS), f32),
             pltpu.VMEM((DIRS, COLS), f32),
+            pltpu.VMEM((1, COLS), jnp.int32),
+            pltpu.VMEM((1, COLS), f32),
+            pltpu.VMEM((1, COLS), f32),
+            pltpu.SemaphoreType.DMA((3,)),
         ],
         compiler_params=small,
-    )(blocks, first, second, own_strip, rim1, rim2, obs)
+    )(
+        here, first, second, own_strip, rim1, rim2, jnp.broadcast_to(obs_count, (1, COLS)), index, value, weight
+    )
 
     fine = min(16, lon_tiles)
     index = [[lon * lat_tiles + lat for lat in range(lat_tiles)] for lon in range(lon_tiles)]

time: 76.8 us -> 73 us (0.951)
  local copies, waits for them, and re-layouts: 3.99 us -> 0.02 us
  Pallas kernels: 10.9 us -> 11.7 us
    unnamed x10 -> x0, local copies, waits for them, and re-layouts: 3.97 us -> none
where the time goes in v3:
time: 73 us; the launch traced here: 72.6 us
  blocking collectives  31.1 us (43%)
  starting transfers between devices  27.7 us (38%)
  Pallas kernels  11.7 us (16%)
  between operations  1.4 us (2%)
    all_to_all x2, blocking collectives, all_parts(): lax.all_to_all(jnp.broadcast_to(part[None], (count,) + part.shape), ('lon...  31.1 us
    ppermute x1, starting transfers between devices, on_device(): strip1 = lax.ppermute(strip_msg, 'lon', neighbours('lon', 0, True))  10.9 us
    ppermute x1, starting transfers between devices, on_device(): rim1 = lax.ppermute(own_strip, 'lat', neighbours('lat', 0, False))  7.91 us
    pallas_call x1, Pallas kernels, on_device(): pl.pallas_call(forecast_kernel, out_shape=[jax.ShapeDtypeStruct((6 * DIRS...  7.68 us
    ppermute x1, starting transfers between devices, on_device(): strip2 = lax.ppermute(strip_msg, 'lon', neighbours('lon', 1, True))  5.38 us
    pallas_call x1, Pallas kernels, on_device(): pl.pallas_call(analysis_kernel, out_shape=[jax.ShapeDtypeStruct((PAIRS *...  2.81 us
    ppermute x1, starting transfers between devices, on_device(): first = lax.ppermute(first_msg, 'lat', neighbours('lat', 0, False))  2.22 us
  transfers between devices with their start and end apart: 6, of which 1 were waited for; matrix products, arithmetic and copies ran while one was open for 0% of the time, Pallas kernels for 0%

profile of v3, /device:TPU:1, one launch (start us, length us, event | category | flops | bytes accessed | tf_op | source)
XLA Modules:
  0.0 72.6 jit_solution(2515218443746654620)
XLA Ops:
  0.6 1.3 %shard_map.68 = (f32[408,128]{1,0:T(8,128)S(1)}, f32[408,128]{1,0:T(8,128)S(1)}, f32[7,8,128]{2,1,0:T(8,128)S(1)}, f32[102,8,128]{2,1,0:T(8,128)S(1)}) custom-call(f32[102,8,128]{2,1,0:T(8,128)} %bitcast.7), custom_call_target="tpu_custom_call" | custom-call | tf_op jit(solution)/shard_map/pallas_call | solution.py:350
  1.9 5.4 %collective-permute-start.3 = (f32[7,8,128]{2,1,0:T(8,128)S(1)}, f32[7,8,128]{2,1,0:T(8,128)S(1)}, u32[]{:S(2)}, u32[]{:S(2)}) collective-permute-start(f32[7,8,128]{2,1,0:T(8,128)S(1)} %get-tuple-element.14), channel_id=1, source_target_pairs={{16,32},{48,64},{80,96},{112,128},{144,160},{176,192},{208,224},{2... | collective-permute-start | bytes 86024 | tf_op jit(solution)/shard_map/ppermute | solution.py:359
  7.3 10.9 %collective-permute-start.2 = (f32[7,8,128]{2,1,0:T(8,128)S(1)}, f32[7,8,128]{2,1,0:T(8,128)S(1)}, u32[]{:S(2)}, u32[]{:S(2)}) collective-permute-start(f32[7,8,128]{2,1,0:T(8,128)S(1)} %get-tuple-element.14), channel_id=1, source_target_pairs={{0,16},{32,48},{64,80},{96,112},{128,144},{160,176},{192,208},{224... | collective-permute-start | bytes 86024 | tf_op jit(solution)/shard_map/ppermute | solution.py:358
  18.2 2.2 %collective-permute-start = (f32[408,128]{1,0:T(8,128)S(1)}, f32[408,128]{1,0:T(8,128)S(1)}, u32[]{:S(2)}, u32[]{:S(2)}) collective-permute-start(f32[408,128]{1,0:T(8,128)S(1)} %get-tuple-element.12), channel_id=1, source_target_pairs={{0,1},{2,3},{4,5},{6,7},{8,9},{10,11},{12,13},{14,15},{1,0},{3,2},... | collective-permute-start | bytes 626696 | tf_op jit(solution)/shard_map/ppermute | solution.py:360
  20.4 0.7 collective-permute-start.1
  21.1 0.0 collective-permute-done.3
  21.1 0.0 collective-permute-done.2
  21.1 0.7 collective-permute-start.5
  21.8 7.9 %collective-permute-start.4 = (f32[7,8,128]{2,1,0:T(8,128)S(1)}, f32[7,8,128]{2,1,0:T(8,128)S(1)}, u32[]{:S(2)}, u32[]{:S(2)}) collective-permute-start(f32[7,8,128]{2,1,0:T(8,128)S(1)} %broadcast_select_fusion.own_ref), channel_id=1, source_target_pairs={{0,1},{2,3},{4,5},{6,7},{8,9},{10,11},{12,13},{14,15},{1,0},{3,2},... | collective-permute-start | bytes 86024 | tf_op jit(solution)/shard_map/ppermute | solution.py:364
  30.4 0.0 collective-permute-done.5.rim2_ref
  30.4 0.6 collective-permute-done.4.rim1_ref
  31.0 0.0 collective-permute-done.first_ref
  31.0 0.0 collective-permute-done.1.second_ref
  31.0 7.7 %shard_map.69 = (bf16[96,6144]{1,0:T(8,128)(2,1)S(1)}, f32[48,128]{1,0:T(8,128)S(1)}, f32[4,128]{1,0:T(4,128)S(1)}) custom-call(f32[102,8,128]{2,1,0:T(8,128)S(1)} %get-tuple-element.11.x_ref, f32[408,128]{1,0:T(8,128)S(1)} %collective-permute-done.first_ref, f32[408,128]{1,0:T(8,128)S(1)} %collective-permute-done.1.second_ref, ...), custom_call_target="tpu_custom_call" | custom-call | tf_op jit(solution)/shard_map/pallas_call | solution.py:367
  38.7 11.6 %all_to_all.10 = f32[16,4,128]{2,1,0:T(4,128)S(1)} all-to-all(f32[16,4,128]{2,1,0:T(4,128)S(1)} %broadcast_in_dim.10), channel_id=1, replica_groups={{0,16,32,48,64,80,96,112,128,144,160,176,192,208,224,240},{1,17,33,49,6..., dimensions={0} | all-to-all | bytes 65536 | tf_op jit(solution)/shard_map/all_to_all | solution.py:332
  50.3 19.5 %all_to_all.11.parts_ref = f32[32,4,128]{2,1,0:T(4,128)S(1)} all-to-all(f32[32,4,128]{2,1,0:T(4,128)S(1)} %broadcast_in_dim.22), channel_id=1, replica_groups={{0,1,2,3,4,5,6,7,8,9,10,11,12,13,14,15,256,257,258,259,260,261,262,263,..., dimensions={0} | all-to-all | bytes 131072 | tf_op jit(solution)/shard_map/all_to_all | solution.py:332
  69.8 2.8 %shard_map.70 = (f32[816,128]{1,0:T(8,128)}, f32[17,17]{1,0:T(8,128)}) custom-call(f32[32,4,128]{2,1,0:T(4,128)S(1)} %all_to_all.11.parts_ref, bf16[96,6144]{1,0:T(8,128)(2,1)S(1)} %get-tuple-element.16.modes_ref, f32[48,128]{1,0:T(8,128)S(1)} %get-tuple-element.17.mean_ref), custom_call_target="tpu_custom_call" | custom-call | tf_op jit(solution)/shard_map/pallas_call | solution.py:404
  (6 shorter events, 0.1 us)
Async XLA Ops:
  1.9 19.2 %collective-permute-start.3 = (f32[7,8,128]{2,1,0:T(8,128)S(1)}, f32[7,8,128]{2,1,0:T(8,128)S(1)}, u32[]{:S(2)}, u32[]{:S(2)}) collective-permute-start(f32[7,8,128]{2,1,0:T(8,128)S(1)} %get-tuple-element.14), channel_id=1, source_target_pairs={{16,32},{48,64},{80,96},{112,128},{144,160},{176,192},{208,224},{2... | collective-permute-start | bytes 86024 | tf_op jit(solution)/shard_map/ppermute | solution.py:359
  7.3 13.8 %collective-permute-start.2 = (f32[7,8,128]{2,1,0:T(8,128)S(1)}, f32[7,8,128]{2,1,0:T(8,128)S(1)}, u32[]{:S(2)}, u32[]{:S(2)}) collective-permute-start(f32[7,8,128]{2,1,0:T(8,128)S(1)} %get-tuple-element.14), channel_id=1, source_target_pairs={{0,16},{32,48},{64,80},{96,112},{128,144},{160,176},{192,208},{224... | collective-permute-start | bytes 86024 | tf_op jit(solution)/shard_map/ppermute | solution.py:358
  18.2 12.8 %collective-permute-start = (f32[408,128]{1,0:T(8,128)S(1)}, f32[408,128]{1,0:T(8,128)S(1)}, u32[]{:S(2)}, u32[]{:S(2)}) collective-permute-start(f32[408,128]{1,0:T(8,128)S(1)} %get-tuple-element.12), channel_id=1, source_target_pairs={{0,1},{2,3},{4,5},{6,7},{8,9},{10,11},{12,13},{14,15},{1,0},{3,2},... | collective-permute-start | bytes 626696 | tf_op jit(solution)/shard_map/ppermute | solution.py:360
  20.4 10.6 %collective-permute-start.1 = (f32[408,128]{1,0:T(8,128)S(1)}, f32[408,128]{1,0:T(8,128)S(1)}, u32[]{:S(2)}, u32[]{:S(2)}) collective-permute-start(f32[408,128]{1,0:T(8,128)S(1)} %get-tuple-element.13), channel_id=1, source_target_pairs={{1,2},{3,4},{5,6},{7,8},{9,10},{11,12},{13,14},{2,1},{4,3},{6,5},{... | collective-permute-start | bytes 626696 | tf_op jit(solution)/shard_map/ppermute | solution.py:361
  21.1 9.2 %collective-permute-start.5 = (f32[7,8,128]{2,1,0:T(8,128)S(1)}, f32[7,8,128]{2,1,0:T(8,128)S(1)}, u32[]{:S(2)}, u32[]{:S(2)}) collective-permute-start(f32[7,8,128]{2,1,0:T(8,128)S(1)} %broadcast_select_fusion.own_ref), channel_id=1, source_target_pairs={{1,2},{3,4},{5,6},{7,8},{9,10},{11,12},{13,14},{2,1},{4,3},{6,5},{... | collective-permute-start | bytes 86024 | tf_op jit(solution)/shard_map/ppermute | solution.py:365
  21.8 9.2 %collective-permute-start.4 = (f32[7,8,128]{2,1,0:T(8,128)S(1)}, f32[7,8,128]{2,1,0:T(8,128)S(1)}, u32[]{:S(2)}, u32[]{:S(2)}) collective-permute-start(f32[7,8,128]{2,1,0:T(8,128)S(1)} %broadcast_select_fusion.own_ref), channel_id=1, source_target_pairs={{0,1},{2,3},{4,5},{6,7},{8,9},{10,11},{12,13},{14,15},{1,0},{3,2},... | collective-permute-start | bytes 86024 | tf_op jit(solution)/shard_map/ppermute | solution.py:364

commit v4 on v3

--- a/solution.py
+++ b/solution.py
@@ -20,8 +20,10 @@
 TILES = FIELDS * ROWS
 HOME = 12
 DEEP = 32
-GROUP = 2
+GUARD = 8
+GROUP = 4
 STRIPS = FIELDS + 1
+MSG_ROWS = (PAIRS + STRIPS) * RIM
 
 time_step = 0.15
 depth_top = 4.0
@@ -39,29 +41,48 @@
     return [pl.BlockSpec(memory_space=pltpu.VMEM)] * count
 
 
-def pack_kernel(x_hbm, first_ref, second_ref, strip_ref, x_ref, sem):
-    move = pltpu.make_async_copy(x_hbm, x_ref, sem)
+def pack_kernel(x_hbm, strip_ref, x_ref, sem):
+    move = pltpu.make_async_copy(x_hbm, x_ref.at[:, GUARD : GUARD + ROWS, :], sem)
     move.start()
     move.wait()
-    even = (lax.axis_index("lat") & 1) == 0
-
-    def rows_out(north_first):
-        first, second = (slice(RIM, ROWS), slice(0, RIM)) if north_first else (slice(0, RIM), slice(RIM, ROWS))
-        for pair in range(PAIRS):
-            first_ref[RIM * pair : RIM * (pair + 1), :] = x_ref[pair, first, :]
-            second_ref[RIM * pair : RIM * (pair + 1), :] = x_ref[pair, second, :]
-
-    pl.when(even)(lambda: rows_out(True))
-    pl.when(jnp.logical_not(even))(lambda: rows_out(False))
     lane = iota((ROWS, COLS), 1)
     for strip in range(STRIPS):
         total = jnp.zeros((ROWS, COLS), f32)
         for place in range(DIRS if strip < FIELDS else FIELDS):
             pair = place * FIELDS + strip if strip < FIELDS else DIRS * FIELDS + place
-            moved = pltpu.roll(x_ref[pair], 8 * place, 1) if place else x_ref[pair]
+            block = x_ref[pair, GUARD : GUARD + ROWS, :]
+            moved = pltpu.roll(block, 8 * place, 1) if place else block
             mask = ((lane - (8 * place - 4)) & (COLS - 1)) < 8
             total = jnp.where(mask, moved, total)
         strip_ref[strip] = total
+
+
+def message_kernel(x_ref, strip1_ref, strip2_ref, own_ref, first_ref, second_ref):
+    even_lon = (lax.axis_index("lon") & 1) == 0
+    even_lat = (lax.axis_index("lat") & 1) == 0
+    eastern = (iota((ROWS, COLS), 1) & 7) < RIM
+
+    def merge(first_is_east):
+        east, west = (strip1_ref, strip2_ref) if first_is_east else (strip2_ref, strip1_ref)
+        for strip in range(STRIPS):
+            own_ref[strip] = jnp.where(eastern, east[strip], west[strip])
+
+    pl.when(even_lon)(lambda: merge(True))
+    pl.when(jnp.logical_not(even_lon))(lambda: merge(False))
+
+    def rows_out(north_first):
+        north, south = (first_ref, second_ref) if north_first else (second_ref, first_ref)
+        for pair in range(PAIRS):
+            at = slice(RIM * pair, RIM * (pair + 1))
+            north[at, :] = x_ref[pair, GUARD + RIM : GUARD + ROWS, :]
+            south[at, :] = x_ref[pair, GUARD : GUARD + RIM, :]
+        for strip in range(STRIPS):
+            at = slice(RIM * (PAIRS + strip), RIM * (PAIRS + strip + 1))
+            north[at, :] = own_ref[strip, RIM:ROWS, :]
+            south[at, :] = own_ref[strip, 0:RIM, :]
+
+    pl.when(even_lat)(lambda: rows_out(True))
+    pl.when(jnp.logical_not(even_lat))(lambda: rows_out(False))
 
 
 def layer(thick, zonal, merid, slope_x, slope_y, depth, turn):
@@ -95,10 +116,104 @@
     return high, middle, (rest - middle.astype(f32)).astype(jnp.bfloat16)
 
 
+def sweep(read, emit, read_strip, emit_strip, inner, turn):
+    lane = iota((ROWS, COLS), 1)
+
+    def members_step(members, which, shifts):
+        stencils = []
+        for member, shift in zip(members, shifts):
+            stencil = []
+            for field in range(FIELDS):
+                c, n, s = read(member * FIELDS + field)
+                beyond = read_strip(which, field)[0]
+                if shift is not None:
+                    beyond = pltpu.roll(beyond, COLS - shift, 1)
+                e = pltpu.roll(jnp.where(lane == 0, beyond, c), COLS - 1, 1)
+                w = pltpu.roll(jnp.where(lane == COLS - 1, beyond, c), 1, 1)
+                stencil.append((c, e, w, n, s))
+            stencils.append(stencil)
+        if emit_strip is not None:
+            for field in range(FIELDS):
+                if shifts[0] is None:
+                    inner[which, field] = stencils[0][field][0]
+                    continue
+                total = inner[which, field]
+                for shift, stencil in zip(shifts, stencils):
+                    edge = ((lane - shift + 1) & (COLS - 1)) < 2
+                    total = jnp.where(edge, pltpu.roll(stencil[field][0], shift, 1), total)
+                inner[which, field] = total
+        for member, stencil in zip(members, stencils):
+            for field, value in enumerate(advance(stencil, turn)):
+                emit(member * FIELDS + field, value)
+
+    def group_step(index, carry):
+        members = [GROUP * index + k for k in range(GROUP)]
+        members_step(members, 0, [8 * member for member in members])
+        return carry
+
+    lax.fori_loop(0, DIRS // GROUP, group_step, 0)
+    members_step([DIRS], 1, [None])
+    if emit_strip is None:
+        return
+    for which in range(2):
+        stencil = []
+        for field in range(FIELDS):
+            c, n, s = read_strip(which, field)
+            beyond = inner[which, field]
+            e = pltpu.roll(jnp.where((lane & 7) == 0, beyond, c), COLS - 1, 1)
+            w = pltpu.roll(jnp.where((lane & 7) == 7, beyond, c), 1, 1)
+            stencil.append((c, e, w, n, s))
+        for field, value in enumerate(advance(stencil, turn)):
+            emit_strip(which, field, value)
+
+
+def row_terms(first, second):
+    lats = lax.axis_size("lat")
+    sub = iota((ROWS, COLS), 0)
+    row = jnp.where(sub < RIM, sub + first, sub - RIM + second) + lax.axis_index("lat") * ROWS
+    inside = (row >= 0) & (row < lats * ROWS)
+    turn = time_step * (0.5 * (2.0 * (row.astype(f32) + 0.5) / float(lats * ROWS) - 1.0))
+    return inside, turn
+
+
+def spread_strips(blocks, strips, first, last, at):
+    for strip in range(STRIPS):
+        for field in range(FIELDS) if strip == FIELDS else [strip]:
+            block = blocks(strip)
+            if strip == FIELDS and field:
+                block = pltpu.roll(block, COLS - 8 * field, 1)
+            strips[strip // FIELDS, field, at : at + last - first, :] = block[first:last, :]
+
+
+def interior_kernel(x_ref, own_ref, *refs):
+    levels, strip_levels, inner = [x_ref, *refs[0:3]], [refs[6], *refs[3:6]], refs[7]
+    _, turn = row_terms(0, RIM)
+    spread_strips(lambda strip: own_ref[strip], strip_levels[0], 0, ROWS, HOME)
+    for step in range(SUBSTEPS - 1):
+        old, fresh = levels[step], levels[step + 1]
+        old_strips, fresh_strips = strip_levels[step], strip_levels[step + 1]
+
+        def read(pair, old=old):
+            return [old[pair, GUARD + d : GUARD + d + ROWS, :] for d in (0, 1, -1)]
+
+        def emit(pair, value, fresh=fresh):
+            fresh[pair, GUARD : GUARD + ROWS, :] = value
+
+        def read_strip(which, field, old_strips=old_strips):
+            return [old_strips[which, field, HOME + d : HOME + d + ROWS, :] for d in (0, 1, -1)]
+
+        def emit_strip(which, field, value, fresh_strips=fresh_strips):
+            fresh_strips[which, field, HOME : HOME + ROWS, :] = value
+
+        sweep(read, emit, read_strip, emit_strip, inner, turn)
+
+
 def forecast_kernel(
-    x_ref, first_ref, second_ref, own_ref, rim1_ref, rim2_ref, count_ref, index_hbm, value_hbm, weight_hbm,
+    x_ref, own_ref, inner1, inner2, inner3, strip1, strip2, strip3, first_ref, second_ref,
+    count_ref, index_hbm, value_hbm, weight_hbm,
     modes_ref, mean_ref, pay_ref,
-    state, state2, strips, strips2, inner, final, dev, seen, gram, index_ref, value_ref, weight_ref, sems,
+    state0, state1, state2, state3, strips0, strips1, strips2, strips3, inner, final, dev, seen, gram,
+    index_ref, value_ref, weight_ref, sems,
 ):
     moves = [
         pltpu.make_async_copy(source, target, sems.at[place])
@@ -108,102 +223,79 @@
     ]
     for move in moves:
         move.start()
-    lat = lax.axis_index("lat")
     lats = lax.axis_size("lat")
-    even = (lat & 1) == 0
+    even = (lax.axis_index("lat") & 1) == 0
+    states = [state0, state1, state2, state3]
+    strips = [strips0, strips1, strips2, strips3]
 
     def rows_in(north_first):
         north, south = (first_ref, second_ref) if north_first else (second_ref, first_ref)
         for pair in range(PAIRS):
-            state[pair, HOME - RIM : HOME, :] = south[RIM * pair : RIM * (pair + 1), :]
-            state[pair, HOME : HOME + ROWS, :] = x_ref[pair]
-            state[pair, HOME + ROWS : HOME + ROWS + RIM, :] = north[RIM * pair : RIM * (pair + 1), :]
-        north, south = (rim1_ref, rim2_ref) if north_first else (rim2_ref, rim1_ref)
-        for strip in range(STRIPS):
-            blocks = [south[strip], own_ref[strip], north[strip]]
-            for field in range(FIELDS) if strip == FIELDS else [strip]:
-                which = 1 if strip == FIELDS else 0
-                if which and field:
-                    low, mid, high = [pltpu.roll(block, COLS - 8 * field, 1) for block in blocks]
-                else:
-                    low, mid, high = blocks
-                strips[which, field, HOME - RIM : HOME, :] = low[RIM:, :]
-                strips[which, field, HOME : HOME + ROWS, :] = mid
-                strips[which, field, HOME + ROWS : HOME + ROWS + RIM, :] = high[:RIM, :]
+            at = slice(RIM * pair, RIM * (pair + 1))
+            state0[pair, HOME - RIM : HOME, :] = south[at, :]
+            state0[pair, HOME + ROWS : HOME + ROWS + RIM, :] = north[at, :]
+
+        def corner(rows):
+            return lambda strip: rows[RIM * (PAIRS + strip) : RIM * (PAIRS + strip + 1), :]
+
+        spread_strips(corner(south), strips0, 0, RIM, HOME - RIM)
+        spread_strips(corner(north), strips0, 0, RIM, HOME + ROWS)
 
     pl.when(even)(lambda: rows_in(True))
     pl.when(jnp.logical_not(even))(lambda: rows_in(False))
-
-    def row_terms(first):
-        row = iota((ROWS, COLS), 0) + (first + lat * ROWS)
-        inside = (row >= 0) & (row < lats * ROWS)
-        turn = time_step * (0.5 * (2.0 * (row.astype(f32) + 0.5) / float(lats * ROWS) - 1.0))
-        return inside, turn
-
-    lane = iota((ROWS, COLS), 1)
-    for step in range(SUBSTEPS):
-        done = step == SUBSTEPS - 1
-        old, fresh = (state, state2) if step % 2 == 0 else (state2, state)
-        old_strips, fresh_strips = (strips, strips2) if step % 2 == 0 else (strips2, strips)
-        starts = [HOME] if done else [HOME - RIM, HOME + RIM]
-
-        def triple(ref, start, *at):
-            return [ref[(*at, slice(start + d, start + d + ROWS), slice(None))] for d in (0, 1, -1)]
-
-        def members_step(members, which, shifts):
-            for half, start in enumerate(starts):
-                inside, turn = row_terms(start - HOME)
-                stencils = []
-                for member, shift in zip(members, shifts):
-                    stencil = []
-                    for field in range(FIELDS):
-                        c, n, s = triple(old, start, member * FIELDS + field)
-                        beyond = old_strips[which, field, start : start + ROWS, :]
-                        if shift is not None:
-                            beyond = pltpu.roll(beyond, COLS - shift, 1)
-                        e = pltpu.roll(jnp.where(lane == 0, beyond, c), COLS - 1, 1)
-                        w = pltpu.roll(jnp.where(lane == COLS - 1, beyond, c), 1, 1)
-                        stencil.append((c, e, w, n, s))
-                    stencils.append(stencil)
-                if not done:
-                    for field in range(FIELDS):
-                        if shifts[0] is None:
-                            inner[which, field, ROWS * half : ROWS * (half + 1), :] = stencils[0][field][0]
-                            continue
-                        total = inner[which, field, ROWS * half : ROWS * (half + 1), :]
-                        for shift, stencil in zip(shifts, stencils):
-                            edge = ((lane - shift + 1) & (COLS - 1)) < 2
-                            total = jnp.where(edge, pltpu.roll(stencil[field][0], shift, 1), total)
-                        inner[which, field, ROWS * half : ROWS * (half + 1), :] = total
-                for member, stencil in zip(members, stencils):
-                    new = advance(stencil, turn)
-                    for field in range(FIELDS):
-                        if done:
-                            final[member * FIELDS + field] = new[field]
-                        else:
-                            fresh[member * FIELDS + field, start : start + ROWS, :] = jnp.where(inside, new[field], 0.0)
-
-        def group_step(index, carry):
-            members = [GROUP * index + k for k in range(GROUP)]
-            members_step(members, 0, [8 * member for member in members])
-            return carry
-
-        lax.fori_loop(0, DIRS // GROUP, group_step, 0)
-        members_step([DIRS], 1, [None])
-        if not done:
-            for which in range(2):
-                for half, start in enumerate(starts):
-                    inside, turn = row_terms(start - HOME)
-                    stencil = []
-                    for field in range(FIELDS):
-                        c, n, s = triple(old_strips, start, which, field)
-                        beyond = inner[which, field, ROWS * half : ROWS * (half + 1), :]
-                        e = pltpu.roll(jnp.where((lane & 7) == 0, beyond, c), COLS - 1, 1)
-                        w = pltpu.roll(jnp.where((lane & 7) == 7, beyond, c), 1, 1)
-                        stencil.append((c, e, w, n, s))
-                    new = advance(stencil, turn)
-                    for field in range(FIELDS):
-                        fresh_strips[which, field, start : start + ROWS, :] = jnp.where(inside, new[field], 0.0)
+    home = slice(HOME, HOME + ROWS)
+    for source, target in zip((x_ref, inner1, inner2, inner3), states):
+        for pair in range(PAIRS):
+            target[pair, home, :] = source[pair, GUARD : GUARD + ROWS, :]
+    spread_strips(lambda strip: own_ref[strip], strips0, 0, ROWS, HOME)
+    for source, target in zip((strip1, strip2, strip3), strips[1:]):
+        for which in range(2):
+            for field in range(FIELDS):
+                target[which, field, home, :] = source[which, field, home, :]
+
+    upper = iota((ROWS, COLS), 0) < RIM
+    for step in range(SUBSTEPS - 1):
+        low, high = step - 3, 7 - step
+        inside, turn = row_terms(low, high)
+
+        def both(ref, *at, low=low, high=high):
+            return [
+                jnp.where(
+                    upper,
+                    ref[(*at, slice(HOME + low + d, HOME + low + d + ROWS), slice(None))],
+                    ref[(*at, slice(HOME + high - RIM + d, HOME + high + RIM + d), slice(None))],
+                )
+                for d in (0, 1, -1)
+            ]
+
+        def put(ref, value, *at, low=low, high=high, inside=inside):
+            value = jnp.where(inside, value, 0.0)
+            ref[(*at, slice(HOME + low, HOME + low + RIM), slice(None))] = value[0:RIM, :]
+            ref[(*at, slice(HOME + high, HOME + high + RIM), slice(None))] = value[RIM:ROWS, :]
+
+        sweep(
+            lambda pair, step=step, both=both: both(states[step], pair),
+            lambda pair, value, step=step, put=put: put(states[step + 1], value, pair),
+            lambda which, field, step=step, both=both: both(strips[step], which, field),
+            lambda which, field, value, step=step, put=put: put(strips[step + 1], value, which, field),
+            inner,
+            turn,
+        )
+
+    def own_rows(ref, *at):
+        return [ref[(*at, slice(HOME + d, HOME + d + ROWS), slice(None))] for d in (0, 1, -1)]
+
+    def finish(pair, value):
+        final[pair] = value
+
+    sweep(
+        lambda pair: own_rows(state3, pair),
+        finish,
+        lambda which, field: own_rows(strips3, which, field),
+        None,
+        inner,
+        row_terms(0, RIM)[1],
+    )
 
     sub8 = iota((ROWS, COLS), 0)
     for move in moves:
@@ -228,10 +320,10 @@
     for tile in range(TILES):
         span = slice(COLS * tile, COLS * (tile + 1))
         parts = split(dev[pl.ds(tile, DIRS, stride=TILES), :])
-        for place, part in enumerate((0, 1, 2, 0, 1, 0)):
-            modes_ref[DIRS * place : DIRS * (place + 1), span] = parts[part]
-
-    stack = modes_ref[0 : 3 * DIRS, :]
+        for place, part in enumerate(parts):
+            modes_ref[DIRS * place : DIRS * (place + 1), span] = part
+
+    stack = modes_ref[...]
     blocks = lax.dot_general(stack, stack, (((1,), (1,)), ((), ())), preferred_element_type=f32)
     rows3 = blocks[0:DIRS, :] + (blocks[DIRS : 2 * DIRS, :] + blocks[2 * DIRS :, :])
     mode_gram = rows3[:, 0:DIRS] + (rows3[:, DIRS : 2 * DIRS] + rows3[:, 2 * DIRS :])
@@ -305,7 +397,10 @@
     stack = stack.astype(jnp.bfloat16)
     for field in range(FIELDS):
         span = slice(field * ROWS * COLS, (field + 1) * ROWS * COLS)
-        update = jnp.dot(stack, modes_ref[:, span], preferred_element_type=f32)
+        parts = jnp.concatenate(
+            [modes_ref[:, span], modes_ref[0 : 2 * DIRS, span], modes_ref[0:DIRS, span]], axis=0
+        )
+        update = jnp.dot(stack, parts, preferred_element_type=f32)
         for row_here in range(ROWS):
             tile = field * ROWS + row_here
             out_ref[pl.ds(tile, MEMBERS, stride=TILES), :] = (
@@ -336,49 +431,62 @@
 
 def on_device(sample_collection, obs_index, obs_count, obs_value, obs_weight):
     lat_tiles, lon_tiles = lax.axis_size("lat"), lax.axis_size("lon")
-    small = pltpu.CompilerParams(vmem_limit_bytes=16 * 2**20)
-    blocks = sample_collection.reshape(PAIRS, ROWS, COLS)
-    rows_shape = jax.ShapeDtypeStruct((PAIRS * RIM, COLS), f32)
-    strips_shape = jax.ShapeDtypeStruct((STRIPS, ROWS, COLS), f32)
+    small = pltpu.CompilerParams(vmem_limit_bytes=20 * 2**20)
     in_hbm = pl.BlockSpec(memory_space=pltpu.HBM)
     blocks, index, value, weight = [
         pltpu.with_memory_space_constraint(array, pltpu.HBM)
         for array in (
-            blocks, obs_index.reshape(1, COLS), obs_value.reshape(1, COLS), obs_weight.reshape(1, COLS)
+            sample_collection.reshape(PAIRS, ROWS, COLS),
+            obs_index.reshape(1, COLS),
+            obs_value.reshape(1, COLS),
+            obs_weight.reshape(1, COLS),
         )
     ]
-    first_msg, second_msg, strip_msg, here = pl.pallas_call(
+    strips_shape = jax.ShapeDtypeStruct((STRIPS, ROWS, COLS), f32)
+    level_shape = jax.ShapeDtypeStruct((PAIRS, ROWS + 2 * GUARD, COLS), f32)
+    strip_level = (2, FIELDS, DEEP, COLS)
+    strip_msg, here = pl.pallas_call(
         pack_kernel,
-        out_shape=[rows_shape, rows_shape, strips_shape, jax.ShapeDtypeStruct((PAIRS, ROWS, COLS), f32)],
+        out_shape=[strips_shape, level_shape],
         in_specs=[in_hbm],
-        out_specs=vmem(4),
+        out_specs=vmem(2),
         scratch_shapes=[pltpu.SemaphoreType.DMA],
         compiler_params=small,
     )(blocks)
     strip1 = lax.ppermute(strip_msg, "lon", neighbours("lon", 0, True))
     strip2 = lax.ppermute(strip_msg, "lon", neighbours("lon", 1, True))
+    own_strip, first_msg, second_msg = pl.pallas_call(
+        message_kernel,
+        out_shape=[strips_shape] + [jax.ShapeDtypeStruct((MSG_ROWS, COLS), f32)] * 2,
+        in_specs=vmem(3),
+        out_specs=vmem(3),
+        compiler_params=small,
+    )(here, strip1, strip2)
     first = lax.ppermute(first_msg, "lat", neighbours("lat", 0, False))
     second = lax.ppermute(second_msg, "lat", neighbours("lat", 1, False))
-    eastern = (iota(strip_msg.shape, 2) & 7) < RIM
-    own_strip = jnp.where(eastern == ((lax.axis_index("lon") & 1) == 0), strip1, strip2)
-    rim1 = lax.ppermute(own_strip, "lat", neighbours("lat", 0, False))
-    rim2 = lax.ppermute(own_strip, "lat", neighbours("lat", 1, False))
+    interior = pl.pallas_call(
+        interior_kernel,
+        out_shape=[level_shape] * 3 + [jax.ShapeDtypeStruct(strip_level, f32)] * 3,
+        in_specs=vmem(2),
+        out_specs=vmem(6),
+        scratch_shapes=[pltpu.VMEM(strip_level, f32), pltpu.VMEM((2, FIELDS, ROWS, COLS), f32)],
+        compiler_params=small,
+        cost_estimate=pl.CostEstimate(flops=40_000_000, bytes_accessed=2_000_000, transcendentals=0),
+    )(here, own_strip)
 
     modes, mean, part = pl.pallas_call(
         forecast_kernel,
         out_shape=[
-            jax.ShapeDtypeStruct((6 * DIRS, CELLS), jnp.bfloat16),
+            jax.ShapeDtypeStruct((3 * DIRS, CELLS), jnp.bfloat16),
             jax.ShapeDtypeStruct((TILES, COLS), f32),
             jax.ShapeDtypeStruct((4, COLS), f32),
         ],
-        in_specs=vmem(7) + [in_hbm] * 3,
+        in_specs=vmem(11) + [in_hbm] * 3,
         out_specs=vmem(3),
-        scratch_shapes=[
-            pltpu.VMEM((PAIRS, DEEP, COLS), f32),
-            pltpu.VMEM((PAIRS, DEEP, COLS), f32),
-            pltpu.VMEM((2, FIELDS, DEEP, COLS), f32),
-            pltpu.VMEM((2, FIELDS, DEEP, COLS), f32),
-            pltpu.VMEM((2, FIELDS, ROWS + 2 * RIM, COLS), f32),
+        scratch_shapes=[pltpu.VMEM((PAIRS, DEEP, COLS), f32)] * 4
+        + [pltpu.VMEM(strip_level, f32)] * 4
+        + [
+            pltpu.VMEM((2, FIELDS, ROWS, COLS), f32),
             pltpu.VMEM((PAIRS, ROWS, COLS), f32),
             pltpu.VMEM((DIRS * TILES, COLS), f32),
             pltpu.VMEM((MEMBERS, COLS), f32),
@@ -390,7 +498,8 @@
         ],
         compiler_params=small,
     )(
-        here, first, second, own_strip, rim1, rim2, jnp.broadcast_to(obs_count, (1, COLS)), index, value, weight
+        here, own_strip, *interior, first, second,
+        jnp.broadcast_to(obs_count, (1, COLS)), index, value, weight,
     )
 
     fine = min(16, lon_tiles)

time: 73 us -> 68.8 us (0.942)
  starting transfers between devices: 27.7 us -> 19.1 us
  waiting for transfers between devices: 0.6 us -> 2.97 us
  blocking collectives: 31.1 us -> 33.1 us
    ppermute x2 -> x0, starting transfers between devices: 8.57 us -> none  [the longest x1 7.91 us: on_device(): rim1 = lax.ppermute(own_strip, 'lat', neighbours('lat', 0, False))]
    ppermute x1, waiting for transfers between devices: 0.01 us -> 2.14 us  [on_device(): first = lax.ppermute(first_msg, 'lat', neighbours('lat', 0, False))]
    all_to_all x2, blocking collectives: 31.1 us -> 33.1 us  [all_parts(): lax.all_to_all(jnp.broadcast_to(part[None], (count,) + part.shape), ('lon...]
    ppermute x1, waiting for transfers between devices: 0.01 us -> 0.82 us  [on_device(): strip1 = lax.ppermute(strip_msg, 'lon', neighbours('lon', 0, True))]
    pallas_call x2 -> x4, Pallas kernels: 8.93 us -> 9 us  [the longest x1 4.81 us: on_device(): pl.pallas_call(forecast_kernel, out_shape=[jax.ShapeDtypeStruct((3 * DIRS...]
  transfers between devices with their start and end apart: 6 -> 4, of which waited for: 1 -> 2; matrix products, arithmetic and copies ran while one was open for 0% -> 0% of each run, Pallas kernels for 0% -> 4%
where the time goes in v4:
time: 68.8 us; the launch traced here: 68.5 us
  blocking collectives  33.1 us (48%)
  starting transfers between devices  19.1 us (28%)
  Pallas kernels  11.8 us (17%)
  waiting for transfers between devices  2.97 us (4%)
  between operations  1.36 us (2%)
    all_to_all x2, blocking collectives, all_parts(): lax.all_to_all(jnp.broadcast_to(part[None], (count,) + part.shape), ('lon...  33.1 us
    ppermute x1, starting transfers between devices, on_device(): strip1 = lax.ppermute(strip_msg, 'lon', neighbours('lon', 0, True))  10.9 us
    ppermute x1, starting transfers between devices, on_device(): strip2 = lax.ppermute(strip_msg, 'lon', neighbours('lon', 1, True))  5.38 us
    pallas_call x1, Pallas kernels, on_device(): pl.pallas_call(forecast_kernel, out_shape=[jax.ShapeDtypeStruct((3 * DIRS...  4.81 us
    pallas_call x1, Pallas kernels, on_device(): pl.pallas_call(interior_kernel, out_shape=[level_shape] * 3 + [jax.ShapeD...  2.92 us
    pallas_call x1, Pallas kernels, on_device(): pl.pallas_call(analysis_kernel, out_shape=[jax.ShapeDtypeStruct((PAIRS *...  2.82 us
    ppermute x1, starting transfers between devices, on_device(): first = lax.ppermute(first_msg, 'lat', neighbours('lat', 0, False))  2.22 us
    ppermute x1, waiting for transfers between devices, on_device(): first = lax.ppermute(first_msg, 'lat', neighbours('lat', 0, False))  2.14 us
  transfers between devices with their start and end apart: 4, of which 2 were waited for; matrix products, arithmetic and copies ran while one was open for 0% of the time, Pallas kernels for 4%

profile of v4, /device:TPU:1, one launch (start us, length us, event | category | flops | bytes accessed | tf_op | source)
XLA Modules:
  0.0 68.5 jit_solution(1971363651828147223)
XLA Ops:
  0.6 1.2 %shard_map.68 = (f32[7,8,128]{2,1,0:T(8,128)S(1)}, f32[102,24,128]{2,1,0:T(8,128)S(1)}) custom-call(f32[102,8,128]{2,1,0:T(8,128)} %bitcast.7), custom_call_target="tpu_custom_call" | custom-call | tf_op jit(solution)/shard_map/pallas_call | solution.py:448
  1.8 5.4 %collective-permute-start.1 = (f32[7,8,128]{2,1,0:T(8,128)S(1)}, f32[7,8,128]{2,1,0:T(8,128)S(1)}, u32[]{:S(2)}, u32[]{:S(2)}) collective-permute-start(f32[7,8,128]{2,1,0:T(8,128)S(1)} %get-tuple-element.19), channel_id=1, source_target_pairs={{16,32},{48,64},{80,96},{112,128},{144,160},{176,192},{208,224},{2... | collective-permute-start | bytes 86024 | tf_op jit(solution)/shard_map/ppermute | solution.py:457
  7.2 10.9 %collective-permute-start = (f32[7,8,128]{2,1,0:T(8,128)S(1)}, f32[7,8,128]{2,1,0:T(8,128)S(1)}, u32[]{:S(2)}, u32[]{:S(2)}) collective-permute-start(f32[7,8,128]{2,1,0:T(8,128)S(1)} %get-tuple-element.19), channel_id=1, source_target_pairs={{0,16},{32,48},{64,80},{96,112},{128,144},{160,176},{192,208},{224... | collective-permute-start | bytes 86024 | tf_op jit(solution)/shard_map/ppermute | solution.py:456
  18.1 0.0 collective-permute-done.1.strip2_ref
  18.1 0.8 %collective-permute-done.strip1_ref = f32[7,8,128]{2,1,0:T(8,128)S(1)} collective-permute-done((f32[7,8,128]{2,1,0:T(8,128)S(1)}, f32[7,8,128]{2,1,0:T(8,128)S(1)}, u32[]{:S(2)}, u32[]{:S(2)}) %collective-permute-start) | collective-permute-done | bytes 28704 | tf_op jit(solution)/shard_map/ppermute | solution.py:456
  18.9 0.1 shard_map.69
  19.0 2.2 %collective-permute-start.2 = (f32[436,128]{1,0:T(8,128)S(1)}, f32[436,128]{1,0:T(8,128)S(1)}, u32[]{:S(2)}, u32[]{:S(2)}) collective-permute-start(f32[436,128]{1,0:T(8,128)S(1)} %get-tuple-element.27), channel_id=1, source_target_pairs={{0,1},{2,3},{4,5},{6,7},{8,9},{10,11},{12,13},{14,15},{1,0},{3,2},... | collective-permute-start | bytes 669704 | tf_op jit(solution)/shard_map/ppermute | solution.py:465
  21.2 0.7 collective-permute-start.3
  22.6 2.9 %shard_map.70 = (f32[102,24,128]{2,1,0:T(8,128)S(1)}, f32[102,24,128]{2,1,0:T(8,128)S(1)}, f32[102,24,128]{2,1,0:T(8,128)S(1)}, f32[2,6,32,128]{3,2,1,0:T(8,128)...) custom-call(f32[102,24,128]{2,1,0:T(8,128)S(1)} %get-tuple-element.18.x_ref, ...), custom_call_target="tpu_custom_call" | custom-call | flops 40000000 | bytes 2000000 | tf_op jit(solution)/shard_map/pallas_call | solution.py:467
  25.5 2.1 %collective-permute-done.2.first_ref = f32[436,128]{1,0:T(8,128)S(1)} collective-permute-done((f32[436,128]{1,0:T(8,128)S(1)}, f32[436,128]{1,0:T(8,128)S(1)}, u32[]{:S(2)}, u32[]{:S(2)}) %collective-permute-start.2) | collective-permute-done | bytes 223264 | tf_op jit(solution)/shard_map/ppermute | solution.py:465
  27.6 0.0 collective-permute-done.3.second_ref
  27.6 4.8 %shard_map.71 = (bf16[48,6144]{1,0:T(8,128)(2,1)S(1)}, f32[48,128]{1,0:T(8,128)S(1)}, f32[4,128]{1,0:T(4,128)S(1)}) custom-call(f32[102,24,128]{2,1,0:T(8,128)S(1)} %get-tuple-element.18.x_ref, f32[7,8,128]{2,1,0:T(8,128)S(1)} %get-tuple-element.20.own_ref, f32[102,24,128]{2,1,0:T(8,128)S(1)} %get-tuple-element.21.inner1, ...), custom_call_target="tpu_custom_call" | custom-call | tf_op jit(solution)/shard_map/pallas_call | solution.py:477
  32.5 14.0 %all_to_all.10 = f32[16,4,128]{2,1,0:T(4,128)S(1)} all-to-all(f32[16,4,128]{2,1,0:T(4,128)S(1)} %broadcast_in_dim.10), channel_id=1, replica_groups={{0,16,32,48,64,80,96,112,128,144,160,176,192,208,224,240},{1,17,33,49,6..., dimensions={0} | all-to-all | bytes 65536 | tf_op jit(solution)/shard_map/all_to_all | solution.py:427
  46.5 19.1 %all_to_all.11.parts_ref = f32[32,4,128]{2,1,0:T(4,128)S(1)} all-to-all(f32[32,4,128]{2,1,0:T(4,128)S(1)} %broadcast_in_dim.22), channel_id=1, replica_groups={{0,1,2,3,4,5,6,7,8,9,10,11,12,13,14,15,256,257,258,259,260,261,262,263,..., dimensions={0} | all-to-all | bytes 131072 | tf_op jit(solution)/shard_map/all_to_all | solution.py:427
  65.7 2.8 %shard_map.72 = (f32[816,128]{1,0:T(8,128)}, f32[17,17]{1,0:T(8,128)}) custom-call(f32[32,4,128]{2,1,0:T(4,128)S(1)} %all_to_all.11.parts_ref, bf16[48,6144]{1,0:T(8,128)(2,1)S(1)} %get-tuple-element.30.modes_ref, f32[48,128]{1,0:T(8,128)S(1)} %get-tuple-element.31.mean_ref), custom_call_target="tpu_custom_call" | custom-call | tf_op jit(solution)/shard_map/pallas_call | solution.py:513
  (4 shorter events, 0.0 us)
Async XLA Ops:
  1.8 16.3 %collective-permute-start.1 = (f32[7,8,128]{2,1,0:T(8,128)S(1)}, f32[7,8,128]{2,1,0:T(8,128)S(1)}, u32[]{:S(2)}, u32[]{:S(2)}) collective-permute-start(f32[7,8,128]{2,1,0:T(8,128)S(1)} %get-tuple-element.19), channel_id=1, source_target_pairs={{16,32},{48,64},{80,96},{112,128},{144,160},{176,192},{208,224},{2... | collective-permute-start | bytes 86024 | tf_op jit(solution)/shard_map/ppermute | solution.py:457
  7.2 11.7 %collective-permute-start = (f32[7,8,128]{2,1,0:T(8,128)S(1)}, f32[7,8,128]{2,1,0:T(8,128)S(1)}, u32[]{:S(2)}, u32[]{:S(2)}) collective-permute-start(f32[7,8,128]{2,1,0:T(8,128)S(1)} %get-tuple-element.19), channel_id=1, source_target_pairs={{0,16},{32,48},{64,80},{96,112},{128,144},{160,176},{192,208},{224... | collective-permute-start | bytes 86024 | tf_op jit(solution)/shard_map/ppermute | solution.py:456
  19.0 8.6 %collective-permute-start.2 = (f32[436,128]{1,0:T(8,128)S(1)}, f32[436,128]{1,0:T(8,128)S(1)}, u32[]{:S(2)}, u32[]{:S(2)}) collective-permute-start(f32[436,128]{1,0:T(8,128)S(1)} %get-tuple-element.27), channel_id=1, source_target_pairs={{0,1},{2,3},{4,5},{6,7},{8,9},{10,11},{12,13},{14,15},{1,0},{3,2},... | collective-permute-start | bytes 669704 | tf_op jit(solution)/shard_map/ppermute | solution.py:465
  21.2 6.4 %collective-permute-start.3 = (f32[436,128]{1,0:T(8,128)S(1)}, f32[436,128]{1,0:T(8,128)S(1)}, u32[]{:S(2)}, u32[]{:S(2)}) collective-permute-start(f32[436,128]{1,0:T(8,128)S(1)} %get-tuple-element.28), channel_id=1, source_target_pairs={{1,2},{3,4},{5,6},{7,8},{9,10},{11,12},{13,14},{2,1},{4,3},{6,5},{... | collective-permute-start | bytes 669704 | tf_op jit(solution)/shard_map/ppermute | solution.py:466

commit v5 on v4

--- a/solution.py
+++ b/solution.py
@@ -20,7 +20,6 @@
 TILES = FIELDS * ROWS
 HOME = 12
 DEEP = 32
-GUARD = 8
 GROUP = 4
 STRIPS = FIELDS + 1
 MSG_ROWS = (PAIRS + STRIPS) * RIM
@@ -42,7 +41,7 @@
 
 
 def pack_kernel(x_hbm, strip_ref, x_ref, sem):
-    move = pltpu.make_async_copy(x_hbm, x_ref.at[:, GUARD : GUARD + ROWS, :], sem)
+    move = pltpu.make_async_copy(x_hbm, x_ref.at[:, HOME : HOME + ROWS, :], sem)
     move.start()
     move.wait()
     lane = iota((ROWS, COLS), 1)
@@ -50,7 +49,7 @@
         total = jnp.zeros((ROWS, COLS), f32)
         for place in range(DIRS if strip < FIELDS else FIELDS):
             pair = place * FIELDS + strip if strip < FIELDS else DIRS * FIELDS + place
-            block = x_ref[pair, GUARD : GUARD + ROWS, :]
+            block = x_ref[pair, HOME : HOME + ROWS, :]
             moved = pltpu.roll(block, 8 * place, 1) if place else block
             mask = ((lane - (8 * place - 4)) & (COLS - 1)) < 8
             total = jnp.where(mask, moved, total)
@@ -74,8 +73,8 @@
         north, south = (first_ref, second_ref) if north_first else (second_ref, first_ref)
         for pair in range(PAIRS):
             at = slice(RIM * pair, RIM * (pair + 1))
-            north[at, :] = x_ref[pair, GUARD + RIM : GUARD + ROWS, :]
-            south[at, :] = x_ref[pair, GUARD : GUARD + RIM, :]
+            north[at, :] = x_ref[pair, HOME + RIM : HOME + ROWS, :]
+            south[at, :] = x_ref[pair, HOME : HOME + RIM, :]
         for strip in range(STRIPS):
             at = slice(RIM * (PAIRS + strip), RIM * (PAIRS + strip + 1))
             north[at, :] = own_ref[strip, RIM:ROWS, :]
@@ -186,7 +185,7 @@
 
 
 def interior_kernel(x_ref, own_ref, *refs):
-    levels, strip_levels, inner = [x_ref, *refs[0:3]], [refs[6], *refs[3:6]], refs[7]
+    levels, strip_levels, inner = [x_ref, *refs[0:3]], refs[3:7], refs[7]
     _, turn = row_terms(0, RIM)
     spread_strips(lambda strip: own_ref[strip], strip_levels[0], 0, ROWS, HOME)
     for step in range(SUBSTEPS - 1):
@@ -194,10 +193,10 @@
         old_strips, fresh_strips = strip_levels[step], strip_levels[step + 1]
 
         def read(pair, old=old):
-            return [old[pair, GUARD + d : GUARD + d + ROWS, :] for d in (0, 1, -1)]
+            return [old[pair, HOME + d : HOME + d + ROWS, :] for d in (0, 1, -1)]
 
         def emit(pair, value, fresh=fresh):
-            fresh[pair, GUARD : GUARD + ROWS, :] = value
+            fresh[pair, HOME : HOME + ROWS, :] = value
 
         def read_strip(which, field, old_strips=old_strips):
             return [old_strips[which, field, HOME + d : HOME + d + ROWS, :] for d in (0, 1, -1)]
@@ -208,13 +207,10 @@
         sweep(read, emit, read_strip, emit_strip, inner, turn)
 
 
-def forecast_kernel(
-    x_ref, own_ref, inner1, inner2, inner3, strip1, strip2, strip3, first_ref, second_ref,
-    count_ref, index_hbm, value_hbm, weight_hbm,
-    modes_ref, mean_ref, pay_ref,
-    state0, state1, state2, state3, strips0, strips1, strips2, strips3, inner, final, dev, seen, gram,
-    index_ref, value_ref, weight_ref, sems,
-):
+def forecast_kernel(*refs):
+    first_ref, second_ref, count_ref, index_hbm, value_hbm, weight_hbm = refs[8:14]
+    states, strips = refs[14:18], refs[18:22]
+    modes_ref, mean_ref, pay_ref, inner, final, seen, gram, index_ref, value_ref, weight_ref, sems = refs[22:]
     moves = [
         pltpu.make_async_copy(source, target, sems.at[place])
         for place, (source, target) in enumerate(
@@ -225,34 +221,22 @@
         move.start()
     lats = lax.axis_size("lat")
     even = (lax.axis_index("lat") & 1) == 0
-    states = [state0, state1, state2, state3]
-    strips = [strips0, strips1, strips2, strips3]
 
     def rows_in(north_first):
         north, south = (first_ref, second_ref) if north_first else (second_ref, first_ref)
         for pair in range(PAIRS):
             at = slice(RIM * pair, RIM * (pair + 1))
-            state0[pair, HOME - RIM : HOME, :] = south[at, :]
-            state0[pair, HOME + ROWS : HOME + ROWS + RIM, :] = north[at, :]
+            states[0][pair, HOME - RIM : HOME, :] = south[at, :]
+            states[0][pair, HOME + ROWS : HOME + ROWS + RIM, :] = north[at, :]
 
         def corner(rows):
             return lambda strip: rows[RIM * (PAIRS + strip) : RIM * (PAIRS + strip + 1), :]
 
-        spread_strips(corner(south), strips0, 0, RIM, HOME - RIM)
-        spread_strips(corner(north), strips0, 0, RIM, HOME + ROWS)
+        spread_strips(corner(south), strips[0], 0, RIM, HOME - RIM)
+        spread_strips(corner(north), strips[0], 0, RIM, HOME + ROWS)
 
     pl.when(even)(lambda: rows_in(True))
     pl.when(jnp.logical_not(even))(lambda: rows_in(False))
-    home = slice(HOME, HOME + ROWS)
-    for source, target in zip((x_ref, inner1, inner2, inner3), states):
-        for pair in range(PAIRS):
-            target[pair, home, :] = source[pair, GUARD : GUARD + ROWS, :]
-    spread_strips(lambda strip: own_ref[strip], strips0, 0, ROWS, HOME)
-    for source, target in zip((strip1, strip2, strip3), strips[1:]):
-        for which in range(2):
-            for field in range(FIELDS):
-                target[which, field, home, :] = source[which, field, home, :]
-
     upper = iota((ROWS, COLS), 0) < RIM
     for step in range(SUBSTEPS - 1):
         low, high = step - 3, 7 - step
@@ -286,12 +270,12 @@
         return [ref[(*at, slice(HOME + d, HOME + d + ROWS), slice(None))] for d in (0, 1, -1)]
 
     def finish(pair, value):
-        final[pair] = value
+        final[pl.ds(pl.multiple_of(pair * ROWS, ROWS), ROWS), :] = value
 
     sweep(
-        lambda pair: own_rows(state3, pair),
+        lambda pair: own_rows(states[3], pair),
         finish,
-        lambda which, field: own_rows(strips3, which, field),
+        lambda which, field: own_rows(strips[3], which, field),
         None,
         inner,
         row_terms(0, RIM)[1],
@@ -303,23 +287,23 @@
     cell = index_ref[...]
     column = jnp.broadcast_to(cell & (COLS - 1), (ROWS, COLS))
     at_row = jnp.broadcast_to(lax.shift_right_logical(cell, 7), (ROWS, COLS)) == sub8
+    def block(member, field):
+        at = (member * FIELDS + field) * ROWS
+        return final[at : at + ROWS, :]
+
     for member in range(MEMBERS):
-        surface = final[member * FIELDS] + final[member * FIELDS + 3]
+        surface = block(member, 0) + block(member, 3)
         picked = jnp.take_along_axis(surface, column, axis=1)
         seen[member : member + 1, :] = jnp.sum(jnp.where(at_row, picked, 0.0), axis=0, keepdims=True)
 
     for field in range(FIELDS):
-        total = final[field]
+        total = block(0, field)
         for member in range(1, MEMBERS):
-            total = total + final[member * FIELDS + field]
-        mean = total * (1.0 / MEMBERS)
-        mean_ref[ROWS * field : ROWS * (field + 1), :] = mean
-        for member in range(DIRS):
-            at = member * TILES + field * ROWS
-            dev[at : at + ROWS, :] = final[member * FIELDS + field] - mean
+            total = total + block(member, field)
+        mean_ref[ROWS * field : ROWS * (field + 1), :] = total * (1.0 / MEMBERS)
     for tile in range(TILES):
         span = slice(COLS * tile, COLS * (tile + 1))
-        parts = split(dev[pl.ds(tile, DIRS, stride=TILES), :])
+        parts = split(final[pl.ds(tile, DIRS, stride=TILES), :] - mean_ref[tile : tile + 1, :])
         for place, part in enumerate(parts):
             modes_ref[DIRS * place : DIRS * (place + 1), span] = part
 
@@ -370,13 +354,27 @@
     unit = jnp.where((lane & (DIRS - 1)) == sub, 1.0, 0.0)
     work = jnp.where(lane < copies, unit, gram[...])
     work = jnp.where(lane <= copies + DIRS, work, 0.0)
-    for pivot in range(DIRS):
-        column = jnp.broadcast_to(work[:, copies + pivot : copies + pivot + 1], (DIRS, COLS))
-        value = column[pivot : pivot + 1, :]
-        inverse = lax.rsqrt(value)
-        inverse = inverse * (1.5 - 0.5 * value * inverse * inverse)
-        pivot_row = work[pivot : pivot + 1, :] * inverse
-        work = jnp.where(sub == pivot, pivot_row, work - jnp.where(sub > pivot, column * inverse, 0.0) * pivot_row)
+    for first in range(0, DIRS, 16):
+        pivots = range(first, first + 16)
+        columns = [jnp.broadcast_to(work[:, copies + p : copies + p + 1], (DIRS, COLS)) for p in pivots]
+        rows = []
+        for k, pivot in enumerate(pivots):
+            column, pivot_row = columns[k], work[pivot : pivot + 1, :]
+            for q in range(k):
+                factor = columns[q][pivot : pivot + 1, :]
+                column = column - columns[q] * factor
+                pivot_row = pivot_row - factor * rows[q]
+            value = column[pivot : pivot + 1, :]
+            inverse = lax.rsqrt(value)
+            inverse = inverse * (1.5 - 0.5 * value * inverse * inverse)
+            columns[k] = column * inverse
+            rows.append(pivot_row * inverse)
+        below = work
+        for k in range(16):
+            below = below - columns[k] * rows[k]
+        work = jnp.where(sub >= first + 16, below, work)
+        for k, pivot in enumerate(pivots):
+            work = jnp.where(sub == pivot, rows[k], work)
     inverse_factor = work[:, :copies]
     solved = work[:, copies + DIRS : copies + DIRS + 1]
     weights = jnp.sum(solved * inverse_factor, axis=0, keepdims=True)
@@ -443,8 +441,8 @@
         )
     ]
     strips_shape = jax.ShapeDtypeStruct((STRIPS, ROWS, COLS), f32)
-    level_shape = jax.ShapeDtypeStruct((PAIRS, ROWS + 2 * GUARD, COLS), f32)
-    strip_level = (2, FIELDS, DEEP, COLS)
+    level_shape = jax.ShapeDtypeStruct((PAIRS, DEEP, COLS), f32)
+    strip_level = jax.ShapeDtypeStruct((2, FIELDS, DEEP, COLS), f32)
     strip_msg, here = pl.pallas_call(
         pack_kernel,
         out_shape=[strips_shape, level_shape],
@@ -466,29 +464,28 @@
     second = lax.ppermute(second_msg, "lat", neighbours("lat", 1, False))
     interior = pl.pallas_call(
         interior_kernel,
-        out_shape=[level_shape] * 3 + [jax.ShapeDtypeStruct(strip_level, f32)] * 3,
+        out_shape=[level_shape] * 3 + [strip_level] * 4,
         in_specs=vmem(2),
-        out_specs=vmem(6),
-        scratch_shapes=[pltpu.VMEM(strip_level, f32), pltpu.VMEM((2, FIELDS, ROWS, COLS), f32)],
+        out_specs=vmem(7),
+        scratch_shapes=[pltpu.VMEM((2, FIELDS, ROWS, COLS), f32)],
         compiler_params=small,
         cost_estimate=pl.CostEstimate(flops=40_000_000, bytes_accessed=2_000_000, transcendentals=0),
     )(here, own_strip)
 
-    modes, mean, part = pl.pallas_call(
+    *_, modes, mean, part = pl.pallas_call(
         forecast_kernel,
-        out_shape=[
+        out_shape=[level_shape] * 4
+        + [strip_level] * 4
+        + [
             jax.ShapeDtypeStruct((3 * DIRS, CELLS), jnp.bfloat16),
             jax.ShapeDtypeStruct((TILES, COLS), f32),
             jax.ShapeDtypeStruct((4, COLS), f32),
         ],
         in_specs=vmem(11) + [in_hbm] * 3,
-        out_specs=vmem(3),
-        scratch_shapes=[pltpu.VMEM((PAIRS, DEEP, COLS), f32)] * 4
-        + [pltpu.VMEM(strip_level, f32)] * 4
-        + [
+        out_specs=vmem(11),
+        scratch_shapes=[
             pltpu.VMEM((2, FIELDS, ROWS, COLS), f32),
-            pltpu.VMEM((PAIRS, ROWS, COLS), f32),
-            pltpu.VMEM((DIRS * TILES, COLS), f32),
+            pltpu.VMEM((PAIRS * ROWS, COLS), f32),
             pltpu.VMEM((MEMBERS, COLS), f32),
             pltpu.VMEM((DIRS, COLS), f32),
             pltpu.VMEM((1, COLS), jnp.int32),
@@ -496,11 +493,9 @@
             pltpu.VMEM((1, COLS), f32),
             pltpu.SemaphoreType.DMA((3,)),
         ],
+        input_output_aliases={level: level for level in range(8)},
         compiler_params=small,
-    )(
-        here, own_strip, *interior, first, second,
-        jnp.broadcast_to(obs_count, (1, COLS)), index, value, weight,
-    )
+    )(here, *interior, first, second, jnp.broadcast_to(obs_count, (1, COLS)), index, value, weight)
 
     fine = min(16, lon_tiles)
     index = [[lon * lat_tiles + lat for lat in range(lat_tiles)] for lon in range(lon_tiles)]

time: 68.8 us -> 67.5 us (0.981)
  Pallas kernels: 11.8 us -> 10.6 us
    pallas_call x1, Pallas kernels: 2.82 us -> 1.82 us  [on_device(): pl.pallas_call(analysis_kernel, out_shape=[jax.ShapeDtypeStruct((PAIRS *...]
where the time goes in v5:
time: 67.5 us; the launch traced here: 67.2 us
  blocking collectives  33.1 us (49%)
  starting transfers between devices  19.1 us (28%)
  Pallas kernels  10.6 us (16%)
  waiting for transfers between devices  2.97 us (4%)
  between operations  1.36 us (2%)
    all_to_all x2, blocking collectives, all_parts(): lax.all_to_all(jnp.broadcast_to(part[None], (count,) + part.shape), ('lon...  33.1 us
    ppermute x1, starting transfers between devices, on_device(): strip1 = lax.ppermute(strip_msg, 'lon', neighbours('lon', 0, True))  10.9 us
    ppermute x1, starting transfers between devices, on_device(): strip2 = lax.ppermute(strip_msg, 'lon', neighbours('lon', 1, True))  5.38 us
    pallas_call x1, Pallas kernels, on_device(): pl.pallas_call(forecast_kernel, out_shape=[level_shape] * 4 + [strip_leve...  4.55 us
    pallas_call x1, Pallas kernels, on_device(): pl.pallas_call(interior_kernel, out_shape=[level_shape] * 3 + [strip_leve...  2.92 us
    ppermute x1, starting transfers between devices, on_device(): first = lax.ppermute(first_msg, 'lat', neighbours('lat', 0, False))  2.22 us
    ppermute x1, waiting for transfers between devices, on_device(): first = lax.ppermute(first_msg, 'lat', neighbours('lat', 0, False))  2.15 us
    pallas_call x1, Pallas kernels, on_device(): pl.pallas_call(analysis_kernel, out_shape=[jax.ShapeDtypeStruct((PAIRS *...  1.82 us
  transfers between devices with their start and end apart: 4, of which 2 were waited for; matrix products, arithmetic and copies ran while one was open for 0% of the time, Pallas kernels for 4%

profile of v5, /device:TPU:1, one launch (start us, length us, event | category | flops | bytes accessed | tf_op | source)
XLA Modules:
  0.0 67.2 jit_solution(10831613260333481731)
XLA Ops:
  0.6 1.2 %shard_map.68 = (f32[7,8,128]{2,1,0:T(8,128)S(1)}, f32[102,32,128]{2,1,0:T(8,128)S(1)}) custom-call(f32[102,8,128]{2,1,0:T(8,128)} %bitcast.7), custom_call_target="tpu_custom_call" | custom-call | tf_op jit(solution)/shard_map/pallas_call | solution.py:446
  1.8 5.4 %collective-permute-start.1 = (f32[7,8,128]{2,1,0:T(8,128)S(1)}, f32[7,8,128]{2,1,0:T(8,128)S(1)}, u32[]{:S(2)}, u32[]{:S(2)}) collective-permute-start(f32[7,8,128]{2,1,0:T(8,128)S(1)} %get-tuple-element.20), channel_id=1, source_target_pairs={{16,32},{48,64},{80,96},{112,128},{144,160},{176,192},{208,224},{2... | collective-permute-start | bytes 86024 | tf_op jit(solution)/shard_map/ppermute | solution.py:455
  7.2 10.9 %collective-permute-start = (f32[7,8,128]{2,1,0:T(8,128)S(1)}, f32[7,8,128]{2,1,0:T(8,128)S(1)}, u32[]{:S(2)}, u32[]{:S(2)}) collective-permute-start(f32[7,8,128]{2,1,0:T(8,128)S(1)} %get-tuple-element.20), channel_id=1, source_target_pairs={{0,16},{32,48},{64,80},{96,112},{128,144},{160,176},{192,208},{224... | collective-permute-start | bytes 86024 | tf_op jit(solution)/shard_map/ppermute | solution.py:454
  18.1 0.0 collective-permute-done.1.strip2_ref
  18.1 0.8 %collective-permute-done.strip1_ref = f32[7,8,128]{2,1,0:T(8,128)S(1)} collective-permute-done((f32[7,8,128]{2,1,0:T(8,128)S(1)}, f32[7,8,128]{2,1,0:T(8,128)S(1)}, u32[]{:S(2)}, u32[]{:S(2)}) %collective-permute-start) | collective-permute-done | bytes 28704 | tf_op jit(solution)/shard_map/ppermute | solution.py:454
  18.9 0.1 shard_map.69
  19.0 2.2 %collective-permute-start.2 = (f32[436,128]{1,0:T(8,128)S(1)}, f32[436,128]{1,0:T(8,128)S(1)}, u32[]{:S(2)}, u32[]{:S(2)}) collective-permute-start(f32[436,128]{1,0:T(8,128)S(1)} %get-tuple-element.29), channel_id=1, source_target_pairs={{0,1},{2,3},{4,5},{6,7},{8,9},{10,11},{12,13},{14,15},{1,0},{3,2},... | collective-permute-start | bytes 669704 | tf_op jit(solution)/shard_map/ppermute | solution.py:463
  21.2 0.7 %collective-permute-start.3 = (f32[436,128]{1,0:T(8,128)S(1)}, f32[436,128]{1,0:T(8,128)S(1)}, u32[]{:S(2)}, u32[]{:S(2)}) collective-permute-start(f32[436,128]{1,0:T(8,128)S(1)} %get-tuple-element.30), channel_id=1, source_target_pairs={{1,2},{3,4},{5,6},{7,8},{9,10},{11,12},{13,14},{2,1},{4,3},{6,5},{... | collective-permute-start | bytes 669704 | tf_op jit(solution)/shard_map/ppermute | solution.py:464
  22.6 2.9 %shard_map.70 = (f32[102,32,128]{2,1,0:T(8,128)S(1)}, f32[102,32,128]{2,1,0:T(8,128)S(1)}, f32[102,32,128]{2,1,0:T(8,128)S(1)}, f32[2,6,32,128]{3,2,1,0:T(8,128)...) custom-call(f32[102,32,128]{2,1,0:T(8,128)S(1)} %get-tuple-element.19.x_ref.refs_0, ...), custom_call_target="tpu_custom_call" | custom-call | flops 40000000 | bytes 2000000 | tf_op jit(solution)/shard_map/pallas_call | solution.py:465
  25.5 2.1 %collective-permute-done.2.refs_8_ = f32[436,128]{1,0:T(8,128)S(1)} collective-permute-done((f32[436,128]{1,0:T(8,128)S(1)}, f32[436,128]{1,0:T(8,128)S(1)}, u32[]{:S(2)}, u32[]{:S(2)}) %collective-permute-start.2) | collective-permute-done | bytes 223264 | tf_op jit(solution)/shard_map/ppermute | solution.py:463
  27.6 0.0 collective-permute-done.3.refs_9_
  27.6 4.6 %shard_map.71 = (f32[102,32,128]{2,1,0:T(8,128)S(1)}, f32[102,32,128]{2,1,0:T(8,128)S(1)}, f32[102,32,128]{2,1,0:T(8,128)S(1)}, f32[102,32,128]{2,1,0:T(8,128)S(...) custom-call(f32[102,32,128]{2,1,0:T(8,128)S(1)} %get-tuple-element.1, ...), custom_call_target="tpu_custom_call", output_to_operand_aliasing={{0}: (0, {}), {1}: (1, {}), {2}: (2, {}), {3}: (3, {}), {4}... | custom-call | tf_op jit(solution)/shard_map/pallas_call | solution.py:475
  32.2 14.0 %all_to_all.10 = f32[16,4,128]{2,1,0:T(4,128)S(1)} all-to-all(f32[16,4,128]{2,1,0:T(4,128)S(1)} %broadcast_in_dim.10), channel_id=1, replica_groups={{0,16,32,48,64,80,96,112,128,144,160,176,192,208,224,240},{1,17,33,49,6..., dimensions={0} | all-to-all | bytes 65536 | tf_op jit(solution)/shard_map/all_to_all | solution.py:425
  46.3 19.1 %all_to_all.11.parts_ref = f32[32,4,128]{2,1,0:T(4,128)S(1)} all-to-all(f32[32,4,128]{2,1,0:T(4,128)S(1)} %broadcast_in_dim.22), channel_id=1, replica_groups={{0,1,2,3,4,5,6,7,8,9,10,11,12,13,14,15,256,257,258,259,260,261,262,263,..., dimensions={0} | all-to-all | bytes 131072 | tf_op jit(solution)/shard_map/all_to_all | solution.py:425
  65.4 1.8 %shard_map.72 = (f32[816,128]{1,0:T(8,128)}, f32[17,17]{1,0:T(8,128)}) custom-call(f32[32,4,128]{2,1,0:T(4,128)S(1)} %all_to_all.11.parts_ref, bf16[48,6144]{1,0:T(8,128)(2,1)S(1)} %get-tuple-element.32.modes_ref, f32[48,128]{1,0:T(8,128)S(1)} %get-tuple-element.33.mean_ref), custom_call_target="tpu_custom_call" | custom-call | tf_op jit(solution)/shard_map/pallas_call | solution.py:508
  (4 shorter events, 0.0 us)
Async XLA Ops:
  1.8 16.3 %collective-permute-start.1 = (f32[7,8,128]{2,1,0:T(8,128)S(1)}, f32[7,8,128]{2,1,0:T(8,128)S(1)}, u32[]{:S(2)}, u32[]{:S(2)}) collective-permute-start(f32[7,8,128]{2,1,0:T(8,128)S(1)} %get-tuple-element.20), channel_id=1, source_target_pairs={{16,32},{48,64},{80,96},{112,128},{144,160},{176,192},{208,224},{2... | collective-permute-start | bytes 86024 | tf_op jit(solution)/shard_map/ppermute | solution.py:455
  7.2 11.7 %collective-permute-start = (f32[7,8,128]{2,1,0:T(8,128)S(1)}, f32[7,8,128]{2,1,0:T(8,128)S(1)}, u32[]{:S(2)}, u32[]{:S(2)}) collective-permute-start(f32[7,8,128]{2,1,0:T(8,128)S(1)} %get-tuple-element.20), channel_id=1, source_target_pairs={{0,16},{32,48},{64,80},{96,112},{128,144},{160,176},{192,208},{224... | collective-permute-start | bytes 86024 | tf_op jit(solution)/shard_map/ppermute | solution.py:454
  19.0 8.6 %collective-permute-start.2 = (f32[436,128]{1,0:T(8,128)S(1)}, f32[436,128]{1,0:T(8,128)S(1)}, u32[]{:S(2)}, u32[]{:S(2)}) collective-permute-start(f32[436,128]{1,0:T(8,128)S(1)} %get-tuple-element.29), channel_id=1, source_target_pairs={{0,1},{2,3},{4,5},{6,7},{8,9},{10,11},{12,13},{14,15},{1,0},{3,2},... | collective-permute-start | bytes 669704 | tf_op jit(solution)/shard_map/ppermute | solution.py:463
  21.2 6.4 %collective-permute-start.3 = (f32[436,128]{1,0:T(8,128)S(1)}, f32[436,128]{1,0:T(8,128)S(1)}, u32[]{:S(2)}, u32[]{:S(2)}) collective-permute-start(f32[436,128]{1,0:T(8,128)S(1)} %get-tuple-element.30), channel_id=1, source_target_pairs={{1,2},{3,4},{5,6},{7,8},{9,10},{11,12},{13,14},{2,1},{4,3},{6,5},{... | collective-permute-start | bytes 669704 | tf_op jit(solution)/shard_map/ppermute | solution.py:464

commit v6 on v5

--- a/solution.py
+++ b/solution.py
@@ -20,7 +20,7 @@
 TILES = FIELDS * ROWS
 HOME = 12
 DEEP = 32
-GROUP = 4
+GROUP = 2
 STRIPS = FIELDS + 1
 MSG_ROWS = (PAIRS + STRIPS) * RIM
 
@@ -146,11 +146,12 @@
                 emit(member * FIELDS + field, value)
 
     def group_step(index, carry):
-        members = [GROUP * index + k for k in range(GROUP)]
-        members_step(members, 0, [8 * member for member in members])
+        for part in range(2):
+            members = [GROUP * (2 * index + part) + k for k in range(GROUP)]
+            members_step(members, 0, [8 * member for member in members])
         return carry
 
-    lax.fori_loop(0, DIRS // GROUP, group_step, 0)
+    lax.fori_loop(0, DIRS // GROUP // 2, group_step, 0)
     members_step([DIRS], 1, [None])
     if emit_strip is None:
         return
@@ -208,9 +209,10 @@
 
 
 def forecast_kernel(*refs):
+    levels, strip_levels = refs[0:4], refs[4:8]
     first_ref, second_ref, count_ref, index_hbm, value_hbm, weight_hbm = refs[8:14]
-    states, strips = refs[14:18], refs[18:22]
-    modes_ref, mean_ref, pay_ref, inner, final, seen, gram, index_ref, value_ref, weight_ref, sems = refs[22:]
+    modes_ref, mean_ref, pay_ref, inner, final, seen, gram, index_ref, value_ref, weight_ref, sems = refs[14:25]
+    states, strips = refs[25:29], refs[29:33]
     moves = [
         pltpu.make_async_copy(source, target, sems.at[place])
         for place, (source, target) in enumerate(
@@ -237,6 +239,15 @@
 
     pl.when(even)(lambda: rows_in(True))
     pl.when(jnp.logical_not(even))(lambda: rows_in(False))
+    home = slice(HOME, HOME + ROWS)
+    for source, target in zip(levels, states):
+        for pair in range(PAIRS):
+            target[pair, home, :] = source[pair, home, :]
+    for source, target in zip(strip_levels, strips):
+        for which in range(2):
+            for field in range(FIELDS):
+                target[which, field, home, :] = source[which, field, home, :]
+
     upper = iota((ROWS, COLS), 0) < RIM
     for step in range(SUBSTEPS - 1):
         low, high = step - 3, 7 - step
@@ -472,17 +483,15 @@
         cost_estimate=pl.CostEstimate(flops=40_000_000, bytes_accessed=2_000_000, transcendentals=0),
     )(here, own_strip)
 
-    *_, modes, mean, part = pl.pallas_call(
+    modes, mean, part = pl.pallas_call(
         forecast_kernel,
-        out_shape=[level_shape] * 4
-        + [strip_level] * 4
-        + [
+        out_shape=[
             jax.ShapeDtypeStruct((3 * DIRS, CELLS), jnp.bfloat16),
             jax.ShapeDtypeStruct((TILES, COLS), f32),
             jax.ShapeDtypeStruct((4, COLS), f32),
         ],
         in_specs=vmem(11) + [in_hbm] * 3,
-        out_specs=vmem(11),
+        out_specs=vmem(3),
         scratch_shapes=[
             pltpu.VMEM((2, FIELDS, ROWS, COLS), f32),
             pltpu.VMEM((PAIRS * ROWS, COLS), f32),
@@ -492,8 +501,9 @@
             pltpu.VMEM((1, COLS), f32),
             pltpu.VMEM((1, COLS), f32),
             pltpu.SemaphoreType.DMA((3,)),
-        ],
-        input_output_aliases={level: level for level in range(8)},
+        ]
+        + [pltpu.VMEM(level_shape.shape, f32)] * 4
+        + [pltpu.VMEM(strip_level.shape, f32)] * 4,
         compiler_params=small,
     )(here, *interior, first, second, jnp.broadcast_to(obs_count, (1, COLS)), index, value, weight)
 

time: 67.5 us -> 67.6 us (level)
  no operation moved by 1% of the time
where the time goes in v6:
time: 67.6 us; the launch traced here: 67.3 us
  blocking collectives  33.1 us (49%)
  starting transfers between devices  19.1 us (28%)
  Pallas kernels  10.6 us (16%)
  waiting for transfers between devices  3.07 us (5%)
  between operations  1.36 us (2%)
    all_to_all x2, blocking collectives, all_parts(): lax.all_to_all(jnp.broadcast_to(part[None], (count,) + part.shape), ('lon...  33.1 us
    ppermute x1, starting transfers between devices, on_device(): strip1 = lax.ppermute(strip_msg, 'lon', neighbours('lon', 0, True))  10.9 us
    ppermute x1, starting transfers between devices, on_device(): strip2 = lax.ppermute(strip_msg, 'lon', neighbours('lon', 1, True))  5.38 us
    pallas_call x1, Pallas kernels, on_device(): pl.pallas_call(forecast_kernel, out_shape=[jax.ShapeDtypeStruct((3 * DIRS...  4.68 us
    pallas_call x1, Pallas kernels, on_device(): pl.pallas_call(interior_kernel, out_shape=[level_shape] * 3 + [strip_leve...  2.82 us
    ppermute x1, waiting for transfers between devices, on_device(): first = lax.ppermute(first_msg, 'lat', neighbours('lat', 0, False))  2.24 us
    ppermute x1, starting transfers between devices, on_device(): first = lax.ppermute(first_msg, 'lat', neighbours('lat', 0, False))  2.22 us
    pallas_call x1, Pallas kernels, on_device(): pl.pallas_call(analysis_kernel, out_shape=[jax.ShapeDtypeStruct((PAIRS *...  1.82 us
  transfers between devices with their start and end apart: 4, of which 2 were waited for; matrix products, arithmetic and copies ran while one was open for 0% of the time, Pallas kernels for 4%

profile of v6, /device:TPU:1, one launch (start us, length us, event | category | flops | bytes accessed | tf_op | source)
XLA Modules:
  0.0 67.3 jit_solution(15385705525907058116)
XLA Ops:
  0.6 1.2 %shard_map.68 = (f32[7,8,128]{2,1,0:T(8,128)S(1)}, f32[102,32,128]{2,1,0:T(8,128)S(1)}) custom-call(f32[102,8,128]{2,1,0:T(8,128)} %bitcast.7), custom_call_target="tpu_custom_call" | custom-call | tf_op jit(solution)/shard_map/pallas_call | solution.py:457
  1.8 5.4 %collective-permute-start.1 = (f32[7,8,128]{2,1,0:T(8,128)S(1)}, f32[7,8,128]{2,1,0:T(8,128)S(1)}, u32[]{:S(2)}, u32[]{:S(2)}) collective-permute-start(f32[7,8,128]{2,1,0:T(8,128)S(1)} %get-tuple-element.20), channel_id=1, source_target_pairs={{16,32},{48,64},{80,96},{112,128},{144,160},{176,192},{208,224},{2... | collective-permute-start | bytes 86024 | tf_op jit(solution)/shard_map/ppermute | solution.py:466
  7.2 10.9 %collective-permute-start = (f32[7,8,128]{2,1,0:T(8,128)S(1)}, f32[7,8,128]{2,1,0:T(8,128)S(1)}, u32[]{:S(2)}, u32[]{:S(2)}) collective-permute-start(f32[7,8,128]{2,1,0:T(8,128)S(1)} %get-tuple-element.20), channel_id=1, source_target_pairs={{0,16},{32,48},{64,80},{96,112},{128,144},{160,176},{192,208},{224... | collective-permute-start | bytes 86024 | tf_op jit(solution)/shard_map/ppermute | solution.py:465
  18.1 0.0 collective-permute-done.1.strip2_ref
  18.1 0.8 %collective-permute-done.strip1_ref = f32[7,8,128]{2,1,0:T(8,128)S(1)} collective-permute-done((f32[7,8,128]{2,1,0:T(8,128)S(1)}, f32[7,8,128]{2,1,0:T(8,128)S(1)}, u32[]{:S(2)}, u32[]{:S(2)}) %collective-permute-start) | collective-permute-done | bytes 28704 | tf_op jit(solution)/shard_map/ppermute | solution.py:465
  18.9 0.1 shard_map.69
  19.0 2.2 %collective-permute-start.2 = (f32[436,128]{1,0:T(8,128)S(1)}, f32[436,128]{1,0:T(8,128)S(1)}, u32[]{:S(2)}, u32[]{:S(2)}) collective-permute-start(f32[436,128]{1,0:T(8,128)S(1)} %get-tuple-element.29), channel_id=1, source_target_pairs={{0,1},{2,3},{4,5},{6,7},{8,9},{10,11},{12,13},{14,15},{1,0},{3,2},... | collective-permute-start | bytes 669704 | tf_op jit(solution)/shard_map/ppermute | solution.py:474
  21.2 0.7 %collective-permute-start.3 = (f32[436,128]{1,0:T(8,128)S(1)}, f32[436,128]{1,0:T(8,128)S(1)}, u32[]{:S(2)}, u32[]{:S(2)}) collective-permute-start(f32[436,128]{1,0:T(8,128)S(1)} %get-tuple-element.30), channel_id=1, source_target_pairs={{1,2},{3,4},{5,6},{7,8},{9,10},{11,12},{13,14},{2,1},{4,3},{6,5},{... | collective-permute-start | bytes 669704 | tf_op jit(solution)/shard_map/ppermute | solution.py:475
  22.6 2.8 %shard_map.70 = (f32[102,32,128]{2,1,0:T(8,128)S(1)}, f32[102,32,128]{2,1,0:T(8,128)S(1)}, f32[102,32,128]{2,1,0:T(8,128)S(1)}, f32[2,6,32,128]{3,2,1,0:T(8,128)...) custom-call(f32[102,32,128]{2,1,0:T(8,128)S(1)} %get-tuple-element.19.x_ref.refs_0, ...), custom_call_target="tpu_custom_call" | custom-call | flops 40000000 | bytes 2000000 | tf_op jit(solution)/shard_map/pallas_call | solution.py:476
  25.4 2.2 %collective-permute-done.2.refs_8_ = f32[436,128]{1,0:T(8,128)S(1)} collective-permute-done((f32[436,128]{1,0:T(8,128)S(1)}, f32[436,128]{1,0:T(8,128)S(1)}, u32[]{:S(2)}, u32[]{:S(2)}) %collective-permute-start.2) | collective-permute-done | bytes 223264 | tf_op jit(solution)/shard_map/ppermute | solution.py:474
  27.6 0.0 collective-permute-done.3.refs_9_
  27.6 4.7 %shard_map.71 = (bf16[48,6144]{1,0:T(8,128)(2,1)S(1)}, f32[48,128]{1,0:T(8,128)S(1)}, f32[4,128]{1,0:T(4,128)S(1)}) custom-call(f32[102,32,128]{2,1,0:T(8,128)S(1)} %get-tuple-element.19.x_ref.refs_0_, f32[102,32,128]{2,1,0:T(8,128)S(1)} %get-tuple-element.22.refs_1_, f32[102,32,128]{2,1,0:T(8,128)S(1)} %get-tuple-element.23.refs_2_, ...), custom_call_target="tpu_custom_call" | custom-call | tf_op jit(solution)/shard_map/pallas_call | solution.py:486
  32.3 14.0 %all_to_all.10 = f32[16,4,128]{2,1,0:T(4,128)S(1)} all-to-all(f32[16,4,128]{2,1,0:T(4,128)S(1)} %broadcast_in_dim.10), channel_id=1, replica_groups={{0,16,32,48,64,80,96,112,128,144,160,176,192,208,224,240},{1,17,33,49,6..., dimensions={0} | all-to-all | bytes 65536 | tf_op jit(solution)/shard_map/all_to_all | solution.py:436
  46.4 19.1 %all_to_all.11.parts_ref = f32[32,4,128]{2,1,0:T(4,128)S(1)} all-to-all(f32[32,4,128]{2,1,0:T(4,128)S(1)} %broadcast_in_dim.22), channel_id=1, replica_groups={{0,1,2,3,4,5,6,7,8,9,10,11,12,13,14,15,256,257,258,259,260,261,262,263,..., dimensions={0} | all-to-all | bytes 131072 | tf_op jit(solution)/shard_map/all_to_all | solution.py:436
  65.5 1.8 %shard_map.72 = (f32[816,128]{1,0:T(8,128)}, f32[17,17]{1,0:T(8,128)}) custom-call(f32[32,4,128]{2,1,0:T(4,128)S(1)} %all_to_all.11.parts_ref, bf16[48,6144]{1,0:T(8,128)(2,1)S(1)} %get-tuple-element.32.modes_ref, f32[48,128]{1,0:T(8,128)S(1)} %get-tuple-element.33.mean_ref), custom_call_target="tpu_custom_call" | custom-call | tf_op jit(solution)/shard_map/pallas_call | solution.py:518
  (4 shorter events, 0.0 us)
Async XLA Ops:
  1.8 16.3 %collective-permute-start.1 = (f32[7,8,128]{2,1,0:T(8,128)S(1)}, f32[7,8,128]{2,1,0:T(8,128)S(1)}, u32[]{:S(2)}, u32[]{:S(2)}) collective-permute-start(f32[7,8,128]{2,1,0:T(8,128)S(1)} %get-tuple-element.20), channel_id=1, source_target_pairs={{16,32},{48,64},{80,96},{112,128},{144,160},{176,192},{208,224},{2... | collective-permute-start | bytes 86024 | tf_op jit(solution)/shard_map/ppermute | solution.py:466
  7.2 11.7 %collective-permute-start = (f32[7,8,128]{2,1,0:T(8,128)S(1)}, f32[7,8,128]{2,1,0:T(8,128)S(1)}, u32[]{:S(2)}, u32[]{:S(2)}) collective-permute-start(f32[7,8,128]{2,1,0:T(8,128)S(1)} %get-tuple-element.20), channel_id=1, source_target_pairs={{0,16},{32,48},{64,80},{96,112},{128,144},{160,176},{192,208},{224... | collective-permute-start | bytes 86024 | tf_op jit(solution)/shard_map/ppermute | solution.py:465
  19.0 8.6 %collective-permute-start.2 = (f32[436,128]{1,0:T(8,128)S(1)}, f32[436,128]{1,0:T(8,128)S(1)}, u32[]{:S(2)}, u32[]{:S(2)}) collective-permute-start(f32[436,128]{1,0:T(8,128)S(1)} %get-tuple-element.29), channel_id=1, source_target_pairs={{0,1},{2,3},{4,5},{6,7},{8,9},{10,11},{12,13},{14,15},{1,0},{3,2},... | collective-permute-start | bytes 669704 | tf_op jit(solution)/shard_map/ppermute | solution.py:474
  21.2 6.4 %collective-permute-start.3 = (f32[436,128]{1,0:T(8,128)S(1)}, f32[436,128]{1,0:T(8,128)S(1)}, u32[]{:S(2)}, u32[]{:S(2)}) collective-permute-start(f32[436,128]{1,0:T(8,128)S(1)} %get-tuple-element.30), channel_id=1, source_target_pairs={{1,2},{3,4},{5,6},{7,8},{9,10},{11,12},{13,14},{2,1},{4,3},{6,5},{... | collective-permute-start | bytes 669704 | tf_op jit(solution)/shard_map/ppermute | solution.py:475

commit v7 on v6

--- a/solution.py
+++ b/solution.py
@@ -412,9 +412,9 @@
         update = jnp.dot(stack, parts, preferred_element_type=f32)
         for row_here in range(ROWS):
             tile = field * ROWS + row_here
-            out_ref[pl.ds(tile, MEMBERS, stride=TILES), :] = (
-                update[:, COLS * row_here : COLS * (row_here + 1)] + mean_ref[tile : tile + 1, :]
-            )
+            values = update[:, COLS * row_here : COLS * (row_here + 1)] + mean_ref[tile : tile + 1, :]
+            out_ref[pl.ds(tile, DIRS, stride=TILES), :] = values[0:DIRS, :]
+            out_ref[DIRS * TILES + tile : DIRS * TILES + tile + 1, :] = values[DIRS:MEMBERS, :]
     rotation_t = rotation_t[:, 0:DIRS]
     half_way = jnp.dot(rotation_t, mode_gram, precision=highest, preferred_element_type=f32)
     spread = lax.dot_general(
@@ -513,8 +513,8 @@
         [index[base + k][lat] for k in range(fine)] for base in range(0, lon_tiles, fine) for lat in range(lat_tiles)
     ]
     far = [[index[lon][lat] for lon in range(k, lon_tiles, fine) for lat in range(lat_tiles)] for k in range(fine)]
-    part = jnp.sum(all_parts(part, near), axis=0)
-    parts = all_parts(part, far)
+    part = jnp.sum(all_parts(part, far), axis=0)
+    parts = all_parts(part, near)
     analysis, spread = pl.pallas_call(
         analysis_kernel,
         out_shape=[jax.ShapeDtypeStruct((PAIRS * ROWS, COLS), f32), jax.ShapeDtypeStruct((MEMBERS, MEMBERS), f32)],

time: 67.6 us -> 69.1 us (1.022)
  blocking collectives: 33.1 us -> 34.6 us
    all_to_all x2, blocking collectives: 33.1 us -> 34.6 us  [all_parts(): lax.all_to_all(jnp.broadcast_to(part[None], (count,) + part.shape), ('lon...]
where the time goes in v7:
time: 69.1 us; the launch traced here: 68.8 us
  blocking collectives  34.6 us (50%)
  starting transfers between devices  19.1 us (28%)
  Pallas kernels  10.6 us (15%)
  waiting for transfers between devices  3.07 us (4%)
  between operations  1.36 us (2%)
    all_to_all x2, blocking collectives, all_parts(): lax.all_to_all(jnp.broadcast_to(part[None], (count,) + part.shape), ('lon...  34.6 us
    ppermute x1, starting transfers between devices, on_device(): strip1 = lax.ppermute(strip_msg, 'lon', neighbours('lon', 0, True))  10.9 us
    ppermute x1, starting transfers between devices, on_device(): strip2 = lax.ppermute(strip_msg, 'lon', neighbours('lon', 1, True))  5.38 us
    pallas_call x1, Pallas kernels, on_device(): pl.pallas_call(forecast_kernel, out_shape=[jax.ShapeDtypeStruct((3 * DIRS...  4.68 us
    pallas_call x1, Pallas kernels, on_device(): pl.pallas_call(interior_kernel, out_shape=[level_shape] * 3 + [strip_leve...  2.82 us
    ppermute x1, waiting for transfers between devices, on_device(): first = lax.ppermute(first_msg, 'lat', neighbours('lat', 0, False))  2.24 us
    ppermute x1, starting transfers between devices, on_device(): first = lax.ppermute(first_msg, 'lat', neighbours('lat', 0, False))  2.22 us
    pallas_call x1, Pallas kernels, on_device(): pl.pallas_call(analysis_kernel, out_shape=[jax.ShapeDtypeStruct((PAIRS *...  1.8 us
  transfers between devices with their start and end apart: 4, of which 2 were waited for; matrix products, arithmetic and copies ran while one was open for 0% of the time, Pallas kernels for 4%

profile of v7, /device:TPU:1, one launch (start us, length us, event | category | flops | bytes accessed | tf_op | source)
XLA Modules:
  0.0 68.8 jit_solution(7402196112180614794)
XLA Ops:
  0.6 1.2 %shard_map.68 = (f32[7,8,128]{2,1,0:T(8,128)S(1)}, f32[102,32,128]{2,1,0:T(8,128)S(1)}) custom-call(f32[102,8,128]{2,1,0:T(8,128)} %bitcast.7), custom_call_target="tpu_custom_call" | custom-call | tf_op jit(solution)/shard_map/pallas_call | solution.py:457
  1.8 5.4 %collective-permute-start.1 = (f32[7,8,128]{2,1,0:T(8,128)S(1)}, f32[7,8,128]{2,1,0:T(8,128)S(1)}, u32[]{:S(2)}, u32[]{:S(2)}) collective-permute-start(f32[7,8,128]{2,1,0:T(8,128)S(1)} %get-tuple-element.20), channel_id=1, source_target_pairs={{16,32},{48,64},{80,96},{112,128},{144,160},{176,192},{208,224},{2... | collective-permute-start | bytes 86024 | tf_op jit(solution)/shard_map/ppermute | solution.py:466
  7.2 10.9 %collective-permute-start = (f32[7,8,128]{2,1,0:T(8,128)S(1)}, f32[7,8,128]{2,1,0:T(8,128)S(1)}, u32[]{:S(2)}, u32[]{:S(2)}) collective-permute-start(f32[7,8,128]{2,1,0:T(8,128)S(1)} %get-tuple-element.20), channel_id=1, source_target_pairs={{0,16},{32,48},{64,80},{96,112},{128,144},{160,176},{192,208},{224... | collective-permute-start | bytes 86024 | tf_op jit(solution)/shard_map/ppermute | solution.py:465
  18.1 0.0 collective-permute-done.1.strip2_ref
  18.1 0.8 %collective-permute-done.strip1_ref = f32[7,8,128]{2,1,0:T(8,128)S(1)} collective-permute-done((f32[7,8,128]{2,1,0:T(8,128)S(1)}, f32[7,8,128]{2,1,0:T(8,128)S(1)}, u32[]{:S(2)}, u32[]{:S(2)}) %collective-permute-start) | collective-permute-done | bytes 28704 | tf_op jit(solution)/shard_map/ppermute | solution.py:465
  18.9 0.1 shard_map.69
  19.0 2.2 %collective-permute-start.2 = (f32[436,128]{1,0:T(8,128)S(1)}, f32[436,128]{1,0:T(8,128)S(1)}, u32[]{:S(2)}, u32[]{:S(2)}) collective-permute-start(f32[436,128]{1,0:T(8,128)S(1)} %get-tuple-element.29), channel_id=1, source_target_pairs={{0,1},{2,3},{4,5},{6,7},{8,9},{10,11},{12,13},{14,15},{1,0},{3,2},... | collective-permute-start | bytes 669704 | tf_op jit(solution)/shard_map/ppermute | solution.py:474
  21.2 0.7 collective-permute-start.3
  22.6 2.8 %shard_map.70 = (f32[102,32,128]{2,1,0:T(8,128)S(1)}, f32[102,32,128]{2,1,0:T(8,128)S(1)}, f32[102,32,128]{2,1,0:T(8,128)S(1)}, f32[2,6,32,128]{3,2,1,0:T(8,128)...) custom-call(f32[102,32,128]{2,1,0:T(8,128)S(1)} %get-tuple-element.19.x_ref.refs_0, ...), custom_call_target="tpu_custom_call" | custom-call | flops 40000000 | bytes 2000000 | tf_op jit(solution)/shard_map/pallas_call | solution.py:476
  25.4 2.2 %collective-permute-done.2.refs_8_ = f32[436,128]{1,0:T(8,128)S(1)} collective-permute-done((f32[436,128]{1,0:T(8,128)S(1)}, f32[436,128]{1,0:T(8,128)S(1)}, u32[]{:S(2)}, u32[]{:S(2)}) %collective-permute-start.2) | collective-permute-done | bytes 223264 | tf_op jit(solution)/shard_map/ppermute | solution.py:474
  27.6 0.0 collective-permute-done.3.refs_9_
  27.6 4.7 %shard_map.71 = (bf16[48,6144]{1,0:T(8,128)(2,1)S(1)}, f32[48,128]{1,0:T(8,128)S(1)}, f32[4,128]{1,0:T(4,128)S(1)}) custom-call(f32[102,32,128]{2,1,0:T(8,128)S(1)} %get-tuple-element.19.x_ref.refs_0_, f32[102,32,128]{2,1,0:T(8,128)S(1)} %get-tuple-element.22.refs_1_, f32[102,32,128]{2,1,0:T(8,128)S(1)} %get-tuple-element.23.refs_2_, ...), custom_call_target="tpu_custom_call" | custom-call | tf_op jit(solution)/shard_map/pallas_call | solution.py:486
  32.3 21.8 %all_to_all.10 = f32[32,4,128]{2,1,0:T(4,128)S(1)} all-to-all(f32[32,4,128]{2,1,0:T(4,128)S(1)} %broadcast_in_dim.10), channel_id=1, replica_groups={{0,1,2,3,4,5,6,7,8,9,10,11,12,13,14,15,256,257,258,259,260,261,262,263,..., dimensions={0} | all-to-all | bytes 131072 | tf_op jit(solution)/shard_map/all_to_all | solution.py:436
  54.2 12.8 %all_to_all.11.parts_ref = f32[16,4,128]{2,1,0:T(4,128)S(1)} all-to-all(f32[16,4,128]{2,1,0:T(4,128)S(1)} %broadcast_in_dim.22), channel_id=1, replica_groups={{0,16,32,48,64,80,96,112,128,144,160,176,192,208,224,240},{1,17,33,49,6..., dimensions={0} | all-to-all | bytes 65536 | tf_op jit(solution)/shard_map/all_to_all | solution.py:436
  67.0 1.8 %shard_map.72 = (f32[816,128]{1,0:T(8,128)}, f32[17,17]{1,0:T(8,128)}) custom-call(f32[16,4,128]{2,1,0:T(4,128)S(1)} %all_to_all.11.parts_ref, bf16[48,6144]{1,0:T(8,128)(2,1)S(1)} %get-tuple-element.32.modes_ref, f32[48,128]{1,0:T(8,128)S(1)} %get-tuple-element.33.mean_ref), custom_call_target="tpu_custom_call" | custom-call | tf_op jit(solution)/shard_map/pallas_call | solution.py:518
  (4 shorter events, 0.1 us)
Async XLA Ops:
  1.8 16.3 %collective-permute-start.1 = (f32[7,8,128]{2,1,0:T(8,128)S(1)}, f32[7,8,128]{2,1,0:T(8,128)S(1)}, u32[]{:S(2)}, u32[]{:S(2)}) collective-permute-start(f32[7,8,128]{2,1,0:T(8,128)S(1)} %get-tuple-element.20), channel_id=1, source_target_pairs={{16,32},{48,64},{80,96},{112,128},{144,160},{176,192},{208,224},{2... | collective-permute-start | bytes 86024 | tf_op jit(solution)/shard_map/ppermute | solution.py:466
  7.2 11.7 %collective-permute-start = (f32[7,8,128]{2,1,0:T(8,128)S(1)}, f32[7,8,128]{2,1,0:T(8,128)S(1)}, u32[]{:S(2)}, u32[]{:S(2)}) collective-permute-start(f32[7,8,128]{2,1,0:T(8,128)S(1)} %get-tuple-element.20), channel_id=1, source_target_pairs={{0,16},{32,48},{64,80},{96,112},{128,144},{160,176},{192,208},{224... | collective-permute-start | bytes 86024 | tf_op jit(solution)/shard_map/ppermute | solution.py:465
  19.0 8.6 %collective-permute-start.2 = (f32[436,128]{1,0:T(8,128)S(1)}, f32[436,128]{1,0:T(8,128)S(1)}, u32[]{:S(2)}, u32[]{:S(2)}) collective-permute-start(f32[436,128]{1,0:T(8,128)S(1)} %get-tuple-element.29), channel_id=1, source_target_pairs={{0,1},{2,3},{4,5},{6,7},{8,9},{10,11},{12,13},{14,15},{1,0},{3,2},... | collective-permute-start | bytes 669704 | tf_op jit(solution)/shard_map/ppermute | solution.py:474
  21.2 6.4 %collective-permute-start.3 = (f32[436,128]{1,0:T(8,128)S(1)}, f32[436,128]{1,0:T(8,128)S(1)}, u32[]{:S(2)}, u32[]{:S(2)}) collective-permute-start(f32[436,128]{1,0:T(8,128)S(1)} %get-tuple-element.30), channel_id=1, source_target_pairs={{1,2},{3,4},{5,6},{7,8},{9,10},{11,12},{13,14},{2,1},{4,3},{6,5},{... | collective-permute-start | bytes 669704 | tf_op jit(solution)/shard_map/ppermute | solution.py:475

commit v8 on v6

--- a/solution.py
+++ b/solution.py
@@ -507,12 +507,17 @@
         compiler_params=small,
     )(here, *interior, first, second, jnp.broadcast_to(obs_count, (1, COLS)), index, value, weight)
 
-    fine = min(16, lon_tiles)
     index = [[lon * lat_tiles + lat for lat in range(lat_tiles)] for lon in range(lon_tiles)]
     near = [
-        [index[base + k][lat] for k in range(fine)] for base in range(0, lon_tiles, fine) for lat in range(lat_tiles)
+        [index[base + k][lat] for k in range(2) for lat in range(start, lat_tiles, 2)]
+        for base in range(0, lon_tiles, 2)
+        for start in range(2)
     ]
-    far = [[index[lon][lat] for lon in range(k, lon_tiles, fine) for lat in range(lat_tiles)] for k in range(fine)]
+    far = [
+        [index[lon][base + k] for lon in range(start, lon_tiles, 2) for k in range(2)]
+        for base in range(0, lat_tiles, 2)
+        for start in range(2)
+    ]
     part = jnp.sum(all_parts(part, near), axis=0)
     parts = all_parts(part, far)
     analysis, spread = pl.pallas_call(

time: 67.6 us -> 67.1 us (level)
  no operation moved by 1% of the time
where the time goes in v8:
time: 67.1 us; the launch traced here: 66.8 us
  blocking collectives  32.6 us (49%)
  starting transfers between devices  19.1 us (28%)
  Pallas kernels  10.6 us (16%)
  waiting for transfers between devices  3.07 us (5%)
  between operations  1.36 us (2%)
    all_to_all x2, blocking collectives, all_parts(): lax.all_to_all(jnp.broadcast_to(part[None], (count,) + part.shape), ('lon...  32.6 us
    ppermute x1, starting transfers between devices, on_device(): strip1 = lax.ppermute(strip_msg, 'lon', neighbours('lon', 0, True))  10.9 us
    ppermute x1, starting transfers between devices, on_device(): strip2 = lax.ppermute(strip_msg, 'lon', neighbours('lon', 1, True))  5.38 us
    pallas_call x1, Pallas kernels, on_device(): pl.pallas_call(forecast_kernel, out_shape=[jax.ShapeDtypeStruct((3 * DIRS...  4.68 us
    pallas_call x1, Pallas kernels, on_device(): pl.pallas_call(interior_kernel, out_shape=[level_shape] * 3 + [strip_leve...  2.82 us
    ppermute x1, waiting for transfers between devices, on_device(): first = lax.ppermute(first_msg, 'lat', neighbours('lat', 0, False))  2.24 us
    ppermute x1, starting transfers between devices, on_device(): first = lax.ppermute(first_msg, 'lat', neighbours('lat', 0, False))  2.22 us
    pallas_call x1, Pallas kernels, on_device(): pl.pallas_call(analysis_kernel, out_shape=[jax.ShapeDtypeStruct((PAIRS *...  1.82 us
  transfers between devices with their start and end apart: 4, of which 2 were waited for; matrix products, arithmetic and copies ran while one was open for 0% of the time, Pallas kernels for 4%

profile of v8, /device:TPU:1, one launch (start us, length us, event | category | flops | bytes accessed | tf_op | source)
XLA Modules:
  0.0 66.8 jit_solution(11858853653902546735)
XLA Ops:
  0.6 1.2 %shard_map.68 = (f32[7,8,128]{2,1,0:T(8,128)S(1)}, f32[102,32,128]{2,1,0:T(8,128)S(1)}) custom-call(f32[102,8,128]{2,1,0:T(8,128)} %bitcast.7), custom_call_target="tpu_custom_call" | custom-call | tf_op jit(solution)/shard_map/pallas_call | solution.py:457
  1.8 5.4 %collective-permute-start.1 = (f32[7,8,128]{2,1,0:T(8,128)S(1)}, f32[7,8,128]{2,1,0:T(8,128)S(1)}, u32[]{:S(2)}, u32[]{:S(2)}) collective-permute-start(f32[7,8,128]{2,1,0:T(8,128)S(1)} %get-tuple-element.20), channel_id=1, source_target_pairs={{16,32},{48,64},{80,96},{112,128},{144,160},{176,192},{208,224},{2... | collective-permute-start | bytes 86024 | tf_op jit(solution)/shard_map/ppermute | solution.py:466
  7.2 10.9 %collective-permute-start = (f32[7,8,128]{2,1,0:T(8,128)S(1)}, f32[7,8,128]{2,1,0:T(8,128)S(1)}, u32[]{:S(2)}, u32[]{:S(2)}) collective-permute-start(f32[7,8,128]{2,1,0:T(8,128)S(1)} %get-tuple-element.20), channel_id=1, source_target_pairs={{0,16},{32,48},{64,80},{96,112},{128,144},{160,176},{192,208},{224... | collective-permute-start | bytes 86024 | tf_op jit(solution)/shard_map/ppermute | solution.py:465
  18.1 0.0 collective-permute-done.1.strip2_ref
  18.1 0.8 %collective-permute-done.strip1_ref = f32[7,8,128]{2,1,0:T(8,128)S(1)} collective-permute-done((f32[7,8,128]{2,1,0:T(8,128)S(1)}, f32[7,8,128]{2,1,0:T(8,128)S(1)}, u32[]{:S(2)}, u32[]{:S(2)}) %collective-permute-start) | collective-permute-done | bytes 28704 | tf_op jit(solution)/shard_map/ppermute | solution.py:465
  18.9 0.1 shard_map.69
  19.0 2.2 %collective-permute-start.2 = (f32[436,128]{1,0:T(8,128)S(1)}, f32[436,128]{1,0:T(8,128)S(1)}, u32[]{:S(2)}, u32[]{:S(2)}) collective-permute-start(f32[436,128]{1,0:T(8,128)S(1)} %get-tuple-element.29), channel_id=1, source_target_pairs={{0,1},{2,3},{4,5},{6,7},{8,9},{10,11},{12,13},{14,15},{1,0},{3,2},... | collective-permute-start | bytes 669704 | tf_op jit(solution)/shard_map/ppermute | solution.py:474
  21.2 0.7 %collective-permute-start.3 = (f32[436,128]{1,0:T(8,128)S(1)}, f32[436,128]{1,0:T(8,128)S(1)}, u32[]{:S(2)}, u32[]{:S(2)}) collective-permute-start(f32[436,128]{1,0:T(8,128)S(1)} %get-tuple-element.30), channel_id=1, source_target_pairs={{1,2},{3,4},{5,6},{7,8},{9,10},{11,12},{13,14},{2,1},{4,3},{6,5},{... | collective-permute-start | bytes 669704 | tf_op jit(solution)/shard_map/ppermute | solution.py:475
  22.6 2.8 %shard_map.70 = (f32[102,32,128]{2,1,0:T(8,128)S(1)}, f32[102,32,128]{2,1,0:T(8,128)S(1)}, f32[102,32,128]{2,1,0:T(8,128)S(1)}, f32[2,6,32,128]{3,2,1,0:T(8,128)...) custom-call(f32[102,32,128]{2,1,0:T(8,128)S(1)} %get-tuple-element.19.x_ref.refs_0, ...), custom_call_target="tpu_custom_call" | custom-call | flops 40000000 | bytes 2000000 | tf_op jit(solution)/shard_map/pallas_call | solution.py:476
  25.4 2.2 %collective-permute-done.2.refs_8_ = f32[436,128]{1,0:T(8,128)S(1)} collective-permute-done((f32[436,128]{1,0:T(8,128)S(1)}, f32[436,128]{1,0:T(8,128)S(1)}, u32[]{:S(2)}, u32[]{:S(2)}) %collective-permute-start.2) | collective-permute-done | bytes 223264 | tf_op jit(solution)/shard_map/ppermute | solution.py:474
  27.6 0.0 collective-permute-done.3.refs_9_
  27.6 4.7 %shard_map.71 = (bf16[48,6144]{1,0:T(8,128)(2,1)S(1)}, f32[48,128]{1,0:T(8,128)S(1)}, f32[4,128]{1,0:T(4,128)S(1)}) custom-call(f32[102,32,128]{2,1,0:T(8,128)S(1)} %get-tuple-element.19.x_ref.refs_0_, f32[102,32,128]{2,1,0:T(8,128)S(1)} %get-tuple-element.22.refs_1_, f32[102,32,128]{2,1,0:T(8,128)S(1)} %get-tuple-element.23.refs_2_, ...), custom_call_target="tpu_custom_call" | custom-call | tf_op jit(solution)/shard_map/pallas_call | solution.py:486
  32.3 20.0 %all_to_all.10 = f32[16,4,128]{2,1,0:T(4,128)S(1)} all-to-all(f32[16,4,128]{2,1,0:T(4,128)S(1)} %broadcast_in_dim.10), channel_id=1, replica_groups={{0,2,4,6,8,10,12,14,16,18,20,22,24,26,28,30},{1,3,5,7,9,11,13,15,17,19,..., dimensions={0} | all-to-all | bytes 65536 | tf_op jit(solution)/shard_map/all_to_all | solution.py:436
  52.4 12.6 %all_to_all.11.parts_ref = f32[32,4,128]{2,1,0:T(4,128)S(1)} all-to-all(f32[32,4,128]{2,1,0:T(4,128)S(1)} %broadcast_in_dim.22), channel_id=1, replica_groups={{0,1,32,33,64,65,96,97,128,129,160,161,192,193,224,225,256,257,288,289,..., dimensions={0} | all-to-all | bytes 131072 | tf_op jit(solution)/shard_map/all_to_all | solution.py:436
  65.0 1.8 %shard_map.72 = (f32[816,128]{1,0:T(8,128)}, f32[17,17]{1,0:T(8,128)}) custom-call(f32[32,4,128]{2,1,0:T(4,128)S(1)} %all_to_all.11.parts_ref, bf16[48,6144]{1,0:T(8,128)(2,1)S(1)} %get-tuple-element.32.modes_ref, f32[48,128]{1,0:T(8,128)S(1)} %get-tuple-element.33.mean_ref), custom_call_target="tpu_custom_call" | custom-call | tf_op jit(solution)/shard_map/pallas_call | solution.py:523
  (4 shorter events, 0.0 us)
Async XLA Ops:
  1.8 16.3 %collective-permute-start.1 = (f32[7,8,128]{2,1,0:T(8,128)S(1)}, f32[7,8,128]{2,1,0:T(8,128)S(1)}, u32[]{:S(2)}, u32[]{:S(2)}) collective-permute-start(f32[7,8,128]{2,1,0:T(8,128)S(1)} %get-tuple-element.20), channel_id=1, source_target_pairs={{16,32},{48,64},{80,96},{112,128},{144,160},{176,192},{208,224},{2... | collective-permute-start | bytes 86024 | tf_op jit(solution)/shard_map/ppermute | solution.py:466
  7.2 11.7 %collective-permute-start = (f32[7,8,128]{2,1,0:T(8,128)S(1)}, f32[7,8,128]{2,1,0:T(8,128)S(1)}, u32[]{:S(2)}, u32[]{:S(2)}) collective-permute-start(f32[7,8,128]{2,1,0:T(8,128)S(1)} %get-tuple-element.20), channel_id=1, source_target_pairs={{0,16},{32,48},{64,80},{96,112},{128,144},{160,176},{192,208},{224... | collective-permute-start | bytes 86024 | tf_op jit(solution)/shard_map/ppermute | solution.py:465
  19.0 8.6 %collective-permute-start.2 = (f32[436,128]{1,0:T(8,128)S(1)}, f32[436,128]{1,0:T(8,128)S(1)}, u32[]{:S(2)}, u32[]{:S(2)}) collective-permute-start(f32[436,128]{1,0:T(8,128)S(1)} %get-tuple-element.29), channel_id=1, source_target_pairs={{0,1},{2,3},{4,5},{6,7},{8,9},{10,11},{12,13},{14,15},{1,0},{3,2},... | collective-permute-start | bytes 669704 | tf_op jit(solution)/shard_map/ppermute | solution.py:474
  21.2 6.4 %collective-permute-start.3 = (f32[436,128]{1,0:T(8,128)S(1)}, f32[436,128]{1,0:T(8,128)S(1)}, u32[]{:S(2)}, u32[]{:S(2)}) collective-permute-start(f32[436,128]{1,0:T(8,128)S(1)} %get-tuple-element.30), channel_id=1, source_target_pairs={{1,2},{3,4},{5,6},{7,8},{9,10},{11,12},{13,14},{2,1},{4,3},{6,5},{... | collective-permute-start | bytes 669704 | tf_op jit(solution)/shard_map/ppermute | solution.py:475
